TPU v7x, 32 devices: a whole 2x2x4 slice. The times are simulated.
32 devices in a mesh: clip: 2 (over y), patch: 4 (over z), head: 2 (over x), rep: 2 (over core).
Axes of the slice: x: 2, y: 2, z: 4, core: 2. Of those that a mesh axis runs over, the one named last changes fastest.
Arguments:
- tokens: bfloat16 [1024, 3072], P(('clip', 'patch', 'head', 'rep')), parts along dimension 0, may hold values from -24 to 24
- modulation: float32 [3, 3072], replicated, may hold values from -3 to 3
- in_weight: bfloat16 [3072, 16, 384], P(None, ('head', 'rep')), may hold values from -0.109375 to 0.109375
- query_gain: float32 [128], replicated, may hold values from 1 to 2.5
- key_gain: float32 [128], replicated, may hold values from 0.25 to 1.75
- out_weight: bfloat16 [16, 128, 3072], P(('head', 'rep')), may hold values from -1.5 to 1.5
- stale_cache: bfloat16 [1024, 16, 256], P(('clip', 'patch', 'head', 'rep')), parts along dimension 0, may hold values from -440 to 440, as said below
- lengths: int32 [8], P('clip'), parts along dimension 0, may hold values from 1 to 128, 384 in all
Outputs:
- update: bfloat16 [1024, 3072], P(('clip', 'patch', 'head', 'rep')), parts along dimension 0
- new_cache: bfloat16 [1024, 16, 256], P(('clip', 'patch', 'head', 'rep')), parts along dimension 0
There are 2 independent parts, one for each index of `clip`. A program takes and returns all parts, laid end to end along the dimension named above; an argument that names none is the same for every part. Nothing has to cross between parts.
Inputs may be any that keep to these rules, and one draw needn't show every extreme that they name: stale_cache[s, h] holds the stale key of token s and head h in its first 128 entries and the stale value in its last 128. Only the first lengths[p] tokens of patch p are live keys.
All inputs are finite; a program needn't handle non-finite values.
Results may differ from a plain program's by a relative error of at most 0.02.
The roundings to bfloat16 on the way count: a program that leaves them out, or rounds other values in their place, can miss the bound.
Values may be sent and summed in bfloat16 or wider, within the bound.
No kernel may reach another device: no remote copies, remote signals or barrier semaphores. Data moves between devices by JAX's collectives and lax.ppermute only.
A program may use at most 128 MiB of HBM per device.

v0:
```python
import math

import jax
import jax.numpy as jnp
from jax import lax
from jax.sharding import PartitionSpec as P

EPSILON = 1e-06
NEGATIVE = -1e30
key_block = 512


def normalize_rows(values):
    average = jnp.mean(values, axis=-1, keepdims=True)
    centred = values - average
    variance = jnp.mean(centred * centred, axis=-1, keepdims=True)
    return centred * lax.rsqrt(variance + EPSILON)


def rms_gain(values, gain):
    return values * lax.rsqrt(jnp.mean(values * values, axis=-1, keepdims=True) + EPSILON) * gain


def project(normed, in_weight, query_gain, key_gain):
    row_count = normed.shape[0]
    head_count = in_weight.shape[1]
    triple = in_weight.shape[2]
    head_dim = triple // 3
    flat_weight = in_weight.reshape(in_weight.shape[0], head_count * triple)
    projected = jnp.dot(normed, flat_weight, preferred_element_type=jnp.float32).reshape(
        row_count, head_count, triple
    )
    queries = rms_gain(projected[..., :head_dim], query_gain)
    fresh_keys = rms_gain(projected[..., head_dim : 2 * head_dim], key_gain)
    return jnp.concatenate([queries, fresh_keys, projected[..., 2 * head_dim :]], axis=-1).astype(
        jnp.bfloat16
    )


def lookup(lengths, patch_of):
    patch_ids = jnp.arange(lengths.shape[0], dtype=jnp.int32)
    return jnp.sum(jnp.where(patch_of[:, None] == patch_ids[None, :], lengths[None, :], 0), axis=1)


def attend(running, queries, key_rows, usable):
    head_dim = queries.shape[-1]
    row_max, denominator, weighted = running
    scores = jnp.einsum(
        "qhd,khd->qhk", queries, key_rows[..., :head_dim], preferred_element_type=jnp.float32
    )
    scores = scores * (1.0 / math.sqrt(head_dim))
    key_mask = usable[None, None, :]
    scores = jnp.where(key_mask, scores, NEGATIVE)
    new_max = jnp.maximum(row_max, jnp.max(scores, axis=-1))
    weights = jnp.where(key_mask, jnp.exp(scores - new_max[..., None]), 0.0)
    factor = jnp.exp(row_max - new_max)
    denominator = denominator * factor + jnp.sum(weights, axis=-1)
    weighted = weighted * factor[..., None] + jnp.einsum(
        "qhk,khd->qhd",
        weights.astype(jnp.bfloat16),
        key_rows[..., head_dim:],
        preferred_element_type=jnp.float32,
    )
    return (new_max, denominator, weighted)


def attend_blocks(running, queries, key_rows, usable):
    key_count = key_rows.shape[0]
    if key_count > key_block and key_count % key_block == 0:
        shaped = key_rows.reshape((key_count // key_block, key_block) + key_rows.shape[1:])
        usable_rows = usable.reshape(key_count // key_block, key_block)

        def step_block(current, operands):
            return (attend(current, queries, operands[0], operands[1]), None)

        running, _ = lax.scan(step_block, running, (shaped, usable_rows))
        return running
    return attend(running, queries, key_rows, usable)


def per_device(
    tokens, modulation, in_weight, query_gain, key_gain, out_weight, stale_cache, lengths
):
    heads_dev = in_weight.shape[1]
    head_dim = query_gain.shape[0]
    normed = (
        normalize_rows(tokens.astype(jnp.float32)) * (1.0 + modulation[1]) + modulation[0]
    ).astype(jnp.bfloat16)
    fresh = project(
        lax.all_gather(normed, ("head", "rep"), axis=0, tiled=True), in_weight, query_gain, key_gain
    )
    queries = fresh[..., :head_dim]
    own_rows = fresh[..., head_dim:]
    new_cache = lax.all_to_all(own_rows, ("head", "rep"), split_axis=0, concat_axis=1, tiled=True)
    patch_tok = fresh.shape[0]
    own_patch = lax.axis_index("patch")
    own_length = lookup(lengths, jnp.full((1,), own_patch, jnp.int32))[0]
    running = (
        jnp.full((patch_tok, heads_dev), NEGATIVE, jnp.float32),
        jnp.zeros((patch_tok, heads_dev), jnp.float32),
        jnp.zeros((patch_tok, heads_dev, head_dim), jnp.float32),
    )
    running = attend_blocks(
        running, queries, own_rows, jnp.arange(patch_tok, dtype=jnp.int32) < own_length
    )
    stale_heads = lax.all_to_all(
        stale_cache, ("head", "rep"), split_axis=1, concat_axis=0, tiled=True
    )
    shard_part = lax.all_gather(stale_heads, "patch", axis=0, tiled=True)
    key_index = jnp.arange(shard_part.shape[0], dtype=jnp.int32)
    patch_of = key_index // patch_tok
    position = key_index % patch_tok
    usable = (position < lookup(lengths, patch_of)) & (patch_of != own_patch)
    running = attend_blocks(running, queries, shard_part, usable)
    attended = (running[2] / running[1][..., None]).astype(jnp.bfloat16)
    flat_rows = attended.reshape(patch_tok, heads_dev * head_dim)
    flat_weight = out_weight.reshape(heads_dev * head_dim, out_weight.shape[2])
    attention = lax.psum_scatter(
        jnp.dot(flat_rows, flat_weight, preferred_element_type=jnp.float32).astype(jnp.bfloat16),
        ("head", "rep"),
        scatter_dimension=0,
        tiled=True,
    ).astype(jnp.float32)
    update = (modulation[2] * attention).astype(jnp.bfloat16)
    return (update, new_cache)


def solution(mesh):
    return jax.shard_map(
        per_device,
        mesh=mesh,
        in_specs=(
            P(("clip", "patch", "head", "rep"), None),
            P(),
            P(None, ("head", "rep"), None),
            P(),
            P(),
            P(("head", "rep"), None, None),
            P(("clip", "patch", "head", "rep"), None, None),
            P("clip"),
        ),
        out_specs=(
            P(("clip", "patch", "head", "rep"), None),
            P(("clip", "patch", "head", "rep"), None, None),
        ),
        check_vma=False,
    )
```

profile of v0, /device:TPU:0, one launch (start us, length us, event | category | flops | bytes accessed | tf_op | source)
XLA Modules:
  0.0 127.5 jit_solution(7977245236789460566)
XLA Ops:
  7.2 0.0 copy-start
  7.2 1.9 %copy.21 = bf16[32,16,256]{2,0,1:T(8,128)(2,1)} copy(bf16[32,16,256]{2,1,0:T(8,128)(2,1)} %param.14) | data formatting | bytes 524288 | tf_op args[6]
  9.1 4.2 %all-to-all-start = ((bf16[32,16,256]{2,0,1:T(8,128)(2,1)}), bf16[32,16,256]{2,0,1:T(8,128)(2,1)}, u32[]{:S(2)}, u32[]{:S(2)}) async-start(bf16[32,16,256]{2,0,1:T(8,128)(2,1)} %copy.21), calls=%async_computation | async-start | bytes 524288 | tf_op jit(solution)/shard_map/all_to_all | solution.py:106
  13.3 0.0 all-gather.2.cloned.1.call-start
  13.3 9.0 %copy.31 = bf16[384,8,4,384]{3,1,2,0:T(8,128)(2,1)} copy(bf16[384,8,4,384]{3,2,1,0:T(4,128)(2,1)} %bitcast.47) | data formatting | bytes 18874368
  22.3 0.0 copy-start.3
  22.3 0.0 copy-start.2
  22.3 12.7 %copy.18 = bf16[1536,3072]{1,0:T(8,128)(2,1)} copy(bf16[1536,3072]{0,1:T(8,128)(2,1)} %bitcast.46) | data formatting | bytes 18874368 | tf_op jit(solution)/shard_map/dot_general | solution.py:30
  35.0 0.0 copy-done.3
  35.0 0.0 copy-start.6
  35.1 0.0 copy-done.2
  35.1 0.0 copy-start.5
  35.1 0.1 convert_reduce_fusion
  35.2 0.2 fusion.27
  35.5 0.1 fusion.30
  35.6 9.9 %all_gather.6 = bf16[128,3072]{1,0:T(8,128)(2,1)S(1)} all-gather(bf16[32,3072]{1,0:T(8,128)(2,1)S(1)} %fusion.30), channel_id=1, replica_groups=mesh['clip'=2,'patch'=4,'head'=2,'rep'=2] {'head','rep'}, dimensions={0}, use_global_device_ids=true | all-gather | bytes 983040 | tf_op jit(solution)/shard_map/all_gather | solution.py:90
  45.6 7.8 %fusion.12 = f32[128,4,384]{2,0,1:T(8,128)} fusion(bf16[4,384,3072]{2,1,0:T(8,128)(2,1)} %bitcast.45, bf16[128,3072]{1,0:T(8,128)(2,1)S(1)} %all_gather.6), kind=kOutput, calls=%fused_computation.18 | convolution fusion | flops 1207959552 | bytes 11010048 | tf_op jit(solution)/shard_map/dot_general | solution.py:30
  53.4 0.0 copy-done.6
  53.4 0.6 fusion.44
  54.0 0.0 all-to-all-done
  54.0 1.7 %copy.22 = bf16[32,4,4,256]{3,0,1,2:T(8,128)(2,1)} copy(bf16[32,4,4,256]{3,0,2,1:T(8,128)(2,1)} %bitcast.8) | data formatting | bytes 524288 | tf_op jit(solution)/shard_map/all_to_all | solution.py:106
  55.7 0.0 all-gather.2.cloned.1.call-update
  55.7 0.0 reduce-scatter.2.cloned.1.call-start
  55.7 0.7 iota_compare_fusion.1
  56.4 0.0 copy-start.4
  56.4 0.1 select_reduce_fusion
  56.5 1.2 multiply_reduce_fusion
  57.8 0.6 compare_and_fusion
  58.4 0.0 copy-done.5
  58.4 1.1 multiply_convert_fusion.2
  59.5 0.0 copy-done.4
  59.5 1.8 %fusion.50 = (f32[128,4]{0,1:T(4,128)}, f32[128,4,128]{0,2,1:T(8,128)S(1)}) fusion(bf16[128,4,128]{2,0,1:T(8,128)(2,1)S(1)} %multiply_convert_fusion.2, f32[128,4,384]{2,0,1:T(8,128)} %fusion.12, f32[128]{0:T(128)} %param.11, f32[128,4]{0,1:T(4,128)S(1)} %add_rsqrt_fusion, pred[128]{0:T(512)(128)(4,1)S(1)} %iota_compare_fusion.1), kind=kOutput, calls=%fused_computation.77 | convolution fusion | flops 17169920 | bytes 660096 | tf_op jit(solution)/shard_map/qhd,khd->qhk/dot_general | solution.py:48
  61.3 24.1 %all-gather.2.cloned.1.call-done = bf16[512,4,256]{2,0,1:T(8,128)(2,1)} async-done(((bf16[128,4,256]{2,0,1:T(8,128)(2,1)}), bf16[512,4,256]{2,0,1:T(8,128)(2,1)}) %all-gather.2.cloned.1.call-update) | async-done | bytes 1048592 | tf_op jit(solution)/shard_map/all_gather | solution.py:109
  85.4 1.6 %fusion.51 = (f32[128,4]{0,1:T(4,128)S(1)}, f32[128,4,512]{2,0,1:T(8,128)S(1)}) fusion(bf16[512,4,256]{2,0,1:T(8,128)(2,1)} %all-gather.2.cloned.1.call-done, f32[128,4,384]{2,0,1:T(8,128)} %fusion.12, f32[128]{0:T(128)} %param.11, f32[128,4]{0,1:T(4,128)S(1)} %add_rsqrt_fusion, pred[512]{0:T(512)(128)(4,1)} %compare_and_fusion), kind=kOutput, calls=%fused_computation.78 | convolution fusion | flops 68091392 | bytes 1840128 | tf_op jit(solution)/shard_map/qhd,khd->qhk/dot_general | solution.py:48
  87.0 0.0 copy-start.1
  87.0 0.7 exponential_multiply_fusion
  87.7 0.3 copy-done.1
  88.0 1.0 fusion.10
  89.0 0.7 fusion.31
  89.7 1.3 %multiply_add_fusion = (f32[128,4]{0,1:T(4,128)}, f32[128,4]{0,1:T(4,128)S(1)}) fusion(f32[128,4]{0,1:T(4,128)S(1)} %fusion.10, f32[128,4]{0,1:T(4,128)S(1)} %fusion.31, f32[128,4]{0,1:T(4,128)} %get-tuple-element.12, f32[128,4]{0,1:T(4,128)S(1)} %get-tuple-element.14), kind=kLoop, calls=%fused_computation.56 | loop fusion | flops 4096 | bytes 12288 | tf_op jit(solution)/shard_map/add | solution.py:57
  91.0 1.9 %fusion.7 = f32[128,4,128]{0,2,1:T(8,128)} fusion(f32[128,4,128]{0,2,1:T(8,128)S(1)} %get-tuple-element.13, f32[128,4]{0,1:T(4,128)S(1)} %get-tuple-element.5, f32[128,4]{0,1:T(4,128)S(1)} %get-tuple-element.11, f32[128,4]{0,1:T(4,128)S(1)} %get-tuple-element.9, pred[128]{0:T(512)(128)(4,1)} %copy-done.4, f32[128,4,384]{2,0,1:T(8,128)} %fusion.12), kind=kOutput, calls=%fused_computation.12 | convolution fusion | flops 17104896 | bytes 662016 | tf_op jit(solution)/shard_map/qhk,khd->qhd/dot_general | solution.py:58
  92.9 0.0 copy-done
  92.9 3.3 %fusion = bf16[128,3072]{1,0:T(8,128)(2,1)} fusion(bf16[4,128,3072]{2,1,0:T(8,128)(2,1)S(1)} %copy-done, f32[128,4,128]{0,2,1:T(8,128)} %fusion.7, f32[128,4,512]{2,0,1:T(8,128)} %copy-done.1, bf16[512,4,256]{2,0,1:T(8,128)(2,1)} %all-gather.2.cloned.1.call-done, f32[128,4]{0,1:T(4,128)S(1)} %get-tuple-element.10, pred[512]{0:T(512)(128)(4,1)} %compare_and_fusion, ...), kind=kOutput, calls=%fused_computation.1 | convolution fusion | flops 471138304 | bytes 5771776 | tf_op jit(solution)/shard_map/dot_general | solution.py:119
  96.2 0.0 reduce-scatter.2.cloned.1.call-update
  96.2 1.0 slice.68
  97.2 0.2 copy.25
  97.5 8.5 %all_to_all.36 = bf16[128,4,256]{2,1,0:T(4,128)(2,1)S(1)} all-to-all(bf16[128,4,256]{2,1,0:T(4,128)(2,1)S(1)} %copy.25), channel_id=1, replica_groups=mesh['clip'=2,'patch'=4,'head'=2,'rep'=2] {'head','rep'}, dimensions={0} | all-to-all | bytes 524288 | tf_op jit(solution)/shard_map/all_to_all | solution.py:94
  106.0 0.1 copy.26
  106.1 0.8 all_to_all.33
  106.9 12.1 %reduce-scatter.2.cloned.1.call-done = bf16[32,3072]{1,0:T(8,128)(2,1)} async-done(((bf16[128,3072]{1,0:T(8,128)(2,1)}), bf16[32,3072]{1,0:T(8,128)(2,1)}) %reduce-scatter.2.cloned.1.call-update) | async-done | bytes 196624 | tf_op jit(solution)/shard_map/reduce_scatter | solution.py:118
  119.0 1.6 %multiply_convert_fusion = bf16[32,3072]{1,0:T(8,128)(2,1)} fusion(bf16[32,3072]{1,0:T(8,128)(2,1)} %reduce-scatter.2.cloned.1.call-done, f32[3072]{0:T(1024)S(1)} %bitcast.50), kind=kLoop, calls=%fused_computation.33 | loop fusion | flops 294912 | bytes 405504 | tf_op jit(solution)/shard_map/convert_element_type | solution.py:124
  (7 shorter events, 0.1 us)
Async XLA Ops:
  7.2 85.8 %copy-start = (bf16[4,128,3072]{2,1,0:T(8,128)(2,1)S(1)}, bf16[4,128,3072]{2,1,0:T(8,128)(2,1)}, u32[]{:S(2)}) copy-start(bf16[4,128,3072]{2,1,0:T(8,128)(2,1)} %param.13) | copy-start | bytes 9437188
  9.1 44.9 %all-to-all-start = ((bf16[32,16,256]{2,0,1:T(8,128)(2,1)}), bf16[32,16,256]{2,0,1:T(8,128)(2,1)}, u32[]{:S(2)}, u32[]{:S(2)}) async-start(bf16[32,16,256]{2,0,1:T(8,128)(2,1)} %copy.21), calls=%async_computation | async-start | bytes 524288 | tf_op jit(solution)/shard_map/all_to_all | solution.py:106
  13.3 72.1 %all-gather.2.cloned.1.call-start = ((), (), s32[]{:S(2)}) async-start(), calls=%async_computation.3 | async-start | bytes 1310720 | tf_op jit(solution)/shard_map/all_gather | solution.py:109
  22.3 12.7 %copy-start.3 = (f32[3,3072]{1,0:T(4,128)S(1)}, f32[3,3072]{1,0:T(4,128)}, u32[]{:S(2)}) copy-start(f32[3,3072]{1,0:T(4,128)} %param.9) | copy-start | bytes 110596
  22.3 12.8 %copy-start.2 = (bf16[32,3072]{1,0:T(8,128)(2,1)S(1)}, bf16[32,3072]{1,0:T(8,128)(2,1)}, u32[]{:S(2)}) copy-start(bf16[32,3072]{1,0:T(8,128)(2,1)} %param.8) | copy-start | bytes 589828
  35.0 18.3 %copy-start.6 = (s32[4]{0:T(128)S(1)}, s32[4]{0:T(128)}, u32[]{:S(2)}) copy-start(s32[4]{0:T(128)} %param.15) | copy-start | bytes 52
  35.1 23.3 %copy-start.5 = (f32[128]{0:T(128)S(1)}, f32[128]{0:T(128)}, u32[]{:S(2)}) copy-start(f32[128]{0:T(128)} %param.12) | copy-start | bytes 1540
  55.7 63.3 %reduce-scatter.2.cloned.1.call-start = ((), (), s32[]{:S(2)}) async-start(), calls=%async_computation.4 | async-start | bytes 983040 | tf_op jit(solution)/shard_map/reduce_scatter | solution.py:118
  56.4 3.1 %copy-start.4 = (pred[128]{0:T(512)(128)(4,1)}, pred[128]{0:T(512)(128)(4,1)S(1)}, u32[]{:S(2)}) copy-start(pred[128]{0:T(512)(128)(4,1)S(1)} %iota_compare_fusion.1) | copy-start | bytes 388
  87.0 1.0 copy-start.1
Sparse Core Ops, SparseCore 0:
  55.8 29.5 all-gather.1
  96.4 22.5 reduce-scatter.1
where the time goes:
time: 128 us; the launch traced here: 127 us
  waiting for transfers between devices  36.3 us (28%)
  local copies, waits for them, and re-layouts  27.7 us (22%)
  blocking collectives  18.5 us (14%)
  matrix products  16.4 us (13%)
  between operations  14.2 us (11%)
  other arithmetic  10.2 us (8%)
  starting transfers between devices  4.28 us (3%)
    all_gather x1, waiting for transfers between devices, per_device(): shard_part = lax.all_gather(stale_heads, 'patch', axis=0, tiled=True)  24.1 us
    dot_general x1, local copies, waits for them, and re-layouts, project(): jnp.dot(normed, flat_weight, preferred_element_type=jnp.float32)  12.7 us
    reduce_scatter x1, waiting for transfers between devices, per_device(): lax.psum_scatter(jnp.dot(flat_rows, flat_weight, preferred_element_type=j...  12.1 us
    unnamed x16, local copies, waits for them, and re-layouts  11.2 us
    all_gather x1, blocking collectives, per_device(): lax.all_gather(normed, ('head', 'rep'), axis=0, tiled=True)  9.92 us
    all_to_all x1, blocking collectives, per_device(): lax.all_to_all(own_rows, ('head', 'rep'), split_axis=0, concat_axis=1, ti...  8.54 us
    dot_general x1, matrix products, project(): jnp.dot(normed, flat_weight, preferred_element_type=jnp.float32)  7.79 us
    all_to_all x1, starting transfers between devices, per_device(): lax.all_to_all(stale_cache, ('head', 'rep'), split_axis=1, concat_axis=0,...  4.24 us
  transfers between devices with their start and end apart: 3, of which 2 were waited for; matrix products, arithmetic and copies ran while one was open for 29% of the time, Pallas kernels for 0%

commit v1 on v0

--- a/solution.py
+++ b/solution.py
@@ -1,8 +1,11 @@
+import functools
 import math
 
 import jax
 import jax.numpy as jnp
 from jax import lax
+from jax.experimental import pallas as pl
+from jax.experimental.pallas import tpu as pltpu
 from jax.sharding import PartitionSpec as P
 
 EPSILON = 1e-06
@@ -124,10 +127,172 @@
     update = (modulation[2] * attention).astype(jnp.bfloat16)
     return (update, new_cache)
 
+def swap(values, axis):
+    return lax.ppermute(values, axis, [(0, 1), (1, 0)])
+
+
+def project_kernel(normed_ref, weight_ref, query_gain_ref, key_gain_ref, query_ref, cache_ref):
+    head_dim = query_gain_ref.shape[1]
+    projected = jnp.dot(normed_ref[...], weight_ref[0], preferred_element_type=jnp.float32)
+    query_ref[0] = rms_gain(projected[:, :head_dim], query_gain_ref[...]).astype(jnp.bfloat16)
+    keys = rms_gain(projected[:, head_dim : 2 * head_dim], key_gain_ref[...])
+    cache_ref[0, :, :head_dim] = keys.astype(jnp.bfloat16)
+    cache_ref[0, :, head_dim:] = projected[:, 2 * head_dim :].astype(jnp.bfloat16)
+
+
+def project_heads(normed, weight, query_gain, key_gain):
+    rows, width = normed.shape
+    heads, _, triple = weight.shape
+    head_dim = triple // 3
+    whole = lambda i: (0, 0)
+    one = lambda i: (i, 0, 0)
+    return pl.pallas_call(
+        project_kernel,
+        grid=(heads,),
+        in_specs=[
+            pl.BlockSpec((rows, width), whole),
+            pl.BlockSpec((1, width, triple), one),
+            pl.BlockSpec((1, head_dim), whole),
+            pl.BlockSpec((1, head_dim), whole),
+        ],
+        out_specs=[
+            pl.BlockSpec((1, rows, head_dim), one),
+            pl.BlockSpec((1, rows, 2 * head_dim), one),
+        ],
+        out_shape=[
+            jax.ShapeDtypeStruct((heads, rows, head_dim), jnp.bfloat16),
+            jax.ShapeDtypeStruct((heads, rows, 2 * head_dim), jnp.bfloat16),
+        ],
+        cost_estimate=pl.CostEstimate(
+            flops=2 * rows * width * heads * triple,
+            bytes_accessed=2 * (rows * width + heads * width * triple + heads * rows * triple),
+            transcendentals=0,
+        ),
+        name="project_heads",
+    )(normed, weight, query_gain[None], key_gain[None])
+
+
+def attend_kernel(
+    place_ref, query_ref, cache_ref, source_ref, usable_ref, weight_ref, out_ref, keys_ref, attended_ref
+):
+    heads, rows, head_dim = query_ref.shape
+    sources, _, chunk, both = source_ref.shape
+    chunks = rows // chunk
+    scale = 1.0 / math.sqrt(head_dim)
+    mask = usable_ref[...] > 0
+    for head in range(heads):
+        for source in range(sources):
+            keys_ref[source * chunk : (source + 1) * chunk] = source_ref[source, head]
+        for part in range(chunks):
+            start = pl.multiple_of(place_ref[part] * chunk, chunk)
+            keys_ref[pl.ds(start, chunk)] = cache_ref[head, part * chunk : (part + 1) * chunk]
+        scores = lax.dot_general(
+            query_ref[head],
+            keys_ref[:, :head_dim],
+            (((1,), (1,)), ((), ())),
+            preferred_element_type=jnp.float32,
+        )
+        scores = jnp.where(mask, scores * scale, NEGATIVE)
+        row_max = jnp.max(scores, axis=1, keepdims=True)
+        weights = jnp.where(mask, jnp.exp(scores - row_max), 0.0)
+        denominator = jnp.sum(weights, axis=1, keepdims=True)
+        summed = jnp.dot(
+            weights.astype(jnp.bfloat16), keys_ref[:, head_dim:], preferred_element_type=jnp.float32
+        )
+        attended_ref[:, head * head_dim : (head + 1) * head_dim] = (summed / denominator).astype(
+            jnp.bfloat16
+        )
+    out_ref[...] = jnp.dot(
+        attended_ref[...], weight_ref[...], preferred_element_type=jnp.float32
+    ).astype(jnp.bfloat16)
+
+
+def attend_heads(place, queries, own_cache, sources, usable, out_weight):
+    heads, rows, head_dim = queries.shape
+    count, _, chunk, both = sources.shape
+    depth, width = out_weight.shape
+    vmem = pl.BlockSpec(memory_space=pltpu.VMEM)
+    return pl.pallas_call(
+        attend_kernel,
+        in_specs=[pl.BlockSpec(memory_space=pltpu.SMEM)] + [vmem] * 5,
+        out_specs=vmem,
+        out_shape=jax.ShapeDtypeStruct((rows, width), jnp.bfloat16),
+        scratch_shapes=[
+            pltpu.VMEM((count * chunk, both), jnp.bfloat16),
+            pltpu.VMEM((rows, depth), jnp.bfloat16),
+        ],
+        cost_estimate=pl.CostEstimate(
+            flops=2 * rows * depth * width + 4 * rows * count * chunk * depth,
+            bytes_accessed=2 * (depth * width + count * chunk * heads * both + rows * width),
+            transcendentals=rows * count * chunk * heads,
+        ),
+        name="attend_heads",
+    )(place, queries, own_cache, sources, usable, out_weight)
+
+
+def per_device_pair(
+    tokens, modulation, in_weight, query_gain, key_gain, out_weight, stale_cache, lengths
+):
+    rows, width = tokens.shape
+    _, heads_dev, triple = in_weight.shape
+    head_dim = query_gain.shape[0]
+    patches = lax.axis_size("patch")
+    chunks = 4
+    heads = heads_dev * chunks
+    own_patch = lax.axis_index("patch")
+    own_chunk = lax.axis_index("head") * 2 + lax.axis_index("rep")
+
+    groups = stale_cache.reshape(rows, chunks, heads_dev, 2 * head_dim).transpose(1, 2, 0, 3)
+    outgoing = jnp.broadcast_to(groups[None], (patches,) + groups.shape)
+    outgoing = outgoing.reshape((patches * chunks,) + groups.shape[1:])
+    sources = lax.all_to_all(
+        outgoing, ("patch", "head", "rep"), split_axis=0, concat_axis=0, tiled=True
+    )
+
+    weight_rows = jnp.transpose(in_weight, (1, 0, 2))
+    normed = (
+        normalize_rows(tokens.astype(jnp.float32)) * (1.0 + modulation[1]) + modulation[0]
+    ).astype(jnp.bfloat16)
+    across = swap(normed, "head")
+    beside = swap(normed, "rep")
+    diagonal = swap(across, "rep")
+    all_normed = jnp.concatenate([normed, beside, across, diagonal], axis=0)
+    queries, own_cache = project_heads(all_normed, weight_rows, query_gain, key_gain)
+
+    parts = own_chunk ^ jnp.arange(chunks, dtype=jnp.int32)
+    pieces = own_cache.reshape(heads_dev, chunks, rows, 2 * head_dim)
+    from_beside = swap(pieces[:, 1::2], "rep")
+    own_heads = jnp.stack([pieces[:, 0::2], from_beside], axis=0)
+    from_across = swap(own_heads[:, :, 1], "head")
+    by_part = jnp.stack(
+        [own_heads[0, :, 0], own_heads[1, :, 0], from_across[0], from_across[1]], axis=0
+    )
+    by_group = jnp.take(by_part, parts, axis=0)
+    new_cache = by_group.reshape(heads, rows, 2 * head_dim).transpose(1, 0, 2)
+
+    key_index = jnp.arange(patches * chunks * rows, dtype=jnp.int32)
+    patch_of = key_index // (chunks * rows)
+    usable = (key_index % (chunks * rows) < lookup(lengths, patch_of)).astype(jnp.int32)[None]
+    partial = attend_heads(
+        own_patch * chunks + parts,
+        queries,
+        own_cache,
+        sources,
+        usable,
+        out_weight.reshape(heads_dev * head_dim, width),
+    ).reshape(chunks, rows, width)
+    from_beside = swap(partial[1::2], "rep")
+    pair_sum = partial[0::2].astype(jnp.float32) + from_beside.astype(jnp.float32)
+    from_across = swap(pair_sum[1].astype(jnp.bfloat16), "head")
+    attention = pair_sum[0] + from_across.astype(jnp.float32)
+    return ((modulation[2] * attention).astype(jnp.bfloat16), new_cache)
+
 
 def solution(mesh):
+    paired = mesh.shape["head"] == 2 and mesh.shape["rep"] == 2
+
     return jax.shard_map(
-        per_device,
+        per_device_pair if paired else per_device,
         mesh=mesh,
         in_specs=(
             P(("clip", "patch", "head", "rep"), None),

time: 128 us -> 57.2 us (0.45)
  waiting for transfers between devices: 36.3 us -> 15 us
  blocking collectives: 18.5 us -> 0 us
  matrix products: 16.4 us -> 0 us
  between operations: 14.2 us -> 0.82 us
  local copies, waits for them, and re-layouts: 27.7 us -> 14.6 us
  Pallas kernels: 0 us -> 11.6 us
  starting transfers between devices: 4.28 us -> 10.4 us
  other arithmetic: 10.2 us -> 4.5 us
    all_gather x1 -> x0, waiting for transfers between devices: 24.1 us -> none  [per_device(): shard_part = lax.all_gather(stale_heads, 'patch', axis=0, tiled=True)]
    dot_general x5 -> x0, matrix products: 16.4 us -> none  [the longest x1 7.79 us: project(): jnp.dot(normed, flat_weight, preferred_element_type=jnp.float32)]
    ppermute x0 -> x7, waiting for transfers between devices: none -> 15 us  [swap(): return lax.ppermute(values, axis, [(0, 1), (1, 0)])]
    dot_general x1 -> x0, local copies, waits for them, and re-layouts: 12.7 us -> none  [project(): jnp.dot(normed, flat_weight, preferred_element_type=jnp.float32)]
    reduce_scatter x1 -> x0, waiting for transfers between devices: 12.1 us -> none  [per_device(): lax.psum_scatter(jnp.dot(flat_rows, flat_weight, preferred_element_type=j...]
    pallas_call x0 -> x2, Pallas kernels: none -> 11.6 us  [the longest x1 6.51 us: project_heads(): pl.pallas_call(project_kernel, grid=(heads,), in_specs=[pl.BlockSpec((row...]
    all_gather x1 -> x0, blocking collectives: 9.92 us -> none  [per_device(): lax.all_gather(normed, ('head', 'rep'), axis=0, tiled=True)]
    all_to_all x1 -> x0, blocking collectives: 8.54 us -> none  [per_device(): lax.all_to_all(own_rows, ('head', 'rep'), split_axis=0, concat_axis=1, ti...]
  transfers between devices with their start and end apart: 3 -> 8, of which waited for: 2 -> 4; matrix products, arithmetic and copies ran while one was open for 29% -> 26% of each run, Pallas kernels for 0% -> 20%
where the time goes in v1:
time: 57.2 us; the launch traced here: 56.9 us
  waiting for transfers between devices  15 us (26%)
  local copies, waits for them, and re-layouts  14.6 us (26%)
  Pallas kernels  11.6 us (20%)
  starting transfers between devices  10.4 us (18%)
  other arithmetic  4.5 us (8%)
  between operations  0.82 us (1%)
    ppermute x7, waiting for transfers between devices, swap(): return lax.ppermute(values, axis, [(0, 1), (1, 0)])  15 us
    unnamed x12, local copies, waits for them, and re-layouts  9.53 us
    all_to_all x1, starting transfers between devices, per_device_pair(): lax.all_to_all(outgoing, ('patch', 'head', 'rep'), split_axis=0, concat_a...  7.39 us
    pallas_call x1, Pallas kernels, project_heads(): pl.pallas_call(project_kernel, grid=(heads,), in_specs=[pl.BlockSpec((row...  6.51 us
    pallas_call x1, Pallas kernels, attend_heads(): pl.pallas_call(attend_kernel, in_specs=[pl.BlockSpec(memory_space=pltpu.S...  5.04 us
    ppermute x7, starting transfers between devices, swap(): return lax.ppermute(values, axis, [(0, 1), (1, 0)])  3.06 us
  transfers between devices with their start and end apart: 8, of which 4 were waited for; matrix products, arithmetic and copies ran while one was open for 26% of the time, Pallas kernels for 20%

profile of v1, /device:TPU:0, one launch (start us, length us, event | category | flops | bytes accessed | tf_op | source)
XLA Modules:
  0.0 56.9 jit_solution(7595977845847004037)
XLA Ops:
  0.6 1.0 %reshape.103 = bf16[32,4,4,256]{3,2,1,0:T(4,128)(2,1)S(1)} reshape(bf16[32,16,256]{2,1,0:T(8,128)(2,1)} %param.14) | data formatting | bytes 524288 | tf_op jit(solution)/shard_map/reshape | solution.py:245
  1.6 0.1 copy.17
  1.7 0.0 copy-start.3
  1.7 0.0 copy-start.2
  1.8 1.1 %broadcast_in_dim.47 = bf16[4,4,4,32,256]{4,3,2,1,0:T(8,128)(2,1)} broadcast(bf16[4,4,32,256]{3,2,1,0:T(8,128)(2,1)S(1)} %copy.17), dimensions={1,2,3,4} | broadcast | bytes 1310720 | tf_op jit(solution)/shard_map/broadcast_in_dim | solution.py:246
  2.8 7.4 %all-to-all-start = ((bf16[16,4,32,256]{3,2,1,0:T(8,128)(2,1)}), bf16[16,4,32,256]{3,2,1,0:T(8,128)(2,1)S(1)}, u32[]{:S(2)}, u32[]{:S(2)}) async-start(bf16[16,4,32,256]{3,2,1,0:T(8,128)(2,1)} %bitcast.7), calls=%async_computation | async-start | bytes 2097152 | tf_op jit(solution)/shard_map/all_to_all | solution.py:248
  10.2 0.0 copy-done.3
  10.3 0.0 copy-done.2
  10.3 0.1 convert_reduce_fusion
  10.4 0.2 fusion.2
  10.7 0.1 fusion.5
  10.8 2.0 %collective-permute-start.1 = (bf16[32,3072]{1,0:T(8,128)(2,1)S(1)}, bf16[32,3072]{1,0:T(8,128)(2,1)S(1)}, u32[]{:S(2)}, u32[]{:S(2)}) collective-permute-start(bf16[32,3072]{1,0:T(8,128)(2,1)S(1)} %fusion.5), channel_id=1, source_target_pairs={{0,2},{2,0},{1,3},{3,1},{4,6},{6,4},{5,7},{7,5},{8,10},{10,8},{9,1... | collective-permute-start | bytes 589832 | tf_op jit(solution)/shard_map/ppermute | solution.py:131
  12.8 0.0 collective-permute-start
  12.8 0.0 copy-start.4
  12.8 8.5 %copy.34 = bf16[3072,4,384]{2,0,1:T(8,128)(2,1)} copy(bf16[3072,4,384]{2,1,0:T(4,128)(2,1)} %param.10) | data formatting | bytes 18874368 | tf_op args[2]
  21.4 0.1 broadcast_in_dim.50
  21.5 0.1 broadcast_in_dim.51
  21.6 0.6 %fusion.16.place_ref = s32[4]{0:T(128)} fusion(s32[]{:T(128)S(6)} %add.77, s32[]{:T(128)S(6)} %mul.39), kind=kLoop, calls=%fused_computation.45 | loop fusion | flops 8 | bytes 24 | tf_op jit(solution)/shard_map/add | solution.py:277
  22.2 0.0 copy-done.4
  22.2 0.1 select_reduce_fusion
  22.2 3.7 %collective-permute-done.1 = bf16[32,3072]{1,0:T(8,128)(2,1)S(1)} collective-permute-done((bf16[32,3072]{1,0:T(8,128)(2,1)S(1)}, bf16[32,3072]{1,0:T(8,128)(2,1)S(1)}, u32[]{:S(2)}, u32[]{:S(2)}) %collective-permute-start.1) | collective-permute-done | bytes 196640 | tf_op jit(solution)/shard_map/ppermute | solution.py:131
  26.0 0.0 collective-permute-start.2
  26.0 0.6 %compare_convert_fusion.usable_ref = s32[1,512]{1,0:T(1,128)} fusion(s32[1,512]{1,0:T(1,128)S(1)} %bitcast.56), kind=kLoop, calls=%fused_computation.29 | loop fusion | flops 4096 | bytes 4096 | tf_op jit(solution)/shard_map/convert_element_type | solution.py:275
  26.6 0.0 collective-permute-done
  26.6 0.8 %collective-permute-done.2 = bf16[32,3072]{1,0:T(8,128)(2,1)S(1)} collective-permute-done((bf16[32,3072]{1,0:T(8,128)(2,1)S(1)}, bf16[32,3072]{1,0:T(8,128)(2,1)S(1)}, u32[]{:S(2)}, u32[]{:S(2)}) %collective-permute-start.2) | collective-permute-done | bytes 196640 | tf_op jit(solution)/shard_map/ppermute | solution.py:131
  27.4 0.9 %pad_maximum_fusion.normed_ref = bf16[128,3072]{1,0:T(8,128)(2,1)} fusion(bf16[32,3072]{1,0:T(8,128)(2,1)S(1)} %collective-permute-done.2, bf16[32,3072]{1,0:T(8,128)(2,1)S(1)} %collective-permute-done.1, bf16[32,3072]{1,0:T(8,128)(2,1)S(1)} %collective-permute-done, bf16[32,3072]{1,0:T(8,128)(2,1)S(1)} %fusion.5), kind=kLoop, calls=%fused_computation.2 | loop fusion | flops 3145728 | bytes 1572864 | tf_op jit(solution)/shard_map/concatenate | solution.py:259
  28.4 6.5 %project_heads.1 = (bf16[4,128,128]{2,1,0:T(8,128)(2,1)}, bf16[4,128,256]{2,1,0:T(8,128)(2,1)}) custom-call(bf16[128,3072]{1,0:T(8,128)(2,1)} %pad_maximum_fusion.normed_ref, bf16[4,3072,384]{2,1,0:T(8,128)(2,1)} %bitcast.43, f32[1,128]{1,0:T(1,128)} %bitcast.57, f32[1,128]{1,0:T(1,128)} %bitcast.58), custom_call_target="tpu_custom_call" | custom-call | flops 1207959552 | bytes 10616832 | tf_op jit(solution)/shard_map/project_heads/pallas_call | solution.py:149
  34.9 1.0 %fusion.17 = (bf16[4,2,32,256]{3,2,1,0:T(8,128)(2,1)S(1)}, bf16[4,2,32,256]{3,2,1,0:T(8,128)(2,1)S(1)}) fusion(bf16[4,4,32,256]{3,2,1,0:T(8,128)(2,1)} %bitcast.47), kind=kLoop, calls=%fused_computation.47 | loop fusion | bytes 524288 | tf_op jit(solution)/shard_map/slice | solution.py:265
  35.9 0.2 collective-permute-start.5
  36.1 0.0 all-to-all-done.source_ref
  36.1 0.0 copy-start
  36.1 1.0 %copy-done = bf16[16,4,32,256]{3,2,1,0:T(8,128)(2,1)} copy-done((bf16[16,4,32,256]{3,2,1,0:T(8,128)(2,1)}, bf16[16,4,32,256]{3,2,1,0:T(8,128)(2,1)S(1)}, u32[]{:S(2)}) %copy-start) | copy-done | bytes 1048600
  37.1 5.0 %attend_heads.1 = bf16[128,3072]{1,0:T(8,128)(2,1)} custom-call(s32[4]{0:T(128)} %fusion.16.place_ref, bf16[4,128,128]{2,1,0:T(8,128)(2,1)} %get-tuple-element.4.query_ref, bf16[4,128,256]{2,1,0:T(8,128)(2,1)} %get-tuple-element.5.cache_ref, bf16[16,4,32,256]{3,2,1,0:T(8,128)(2,1)} %copy-done, s32[1,512]{1,0:T(1,128)} %compare_convert_fusion.usable_ref, ...), custom_call_target="tpu_custom_call" | custom-call | flops 536870912 | bytes 4980736 | tf_op jit(solution)/shard_map/attend_heads/pallas_call | solution.py:215
  42.1 0.0 copy-start.1
  42.1 1.1 %slice.44 = bf16[2,32,3072]{2,1,0:T(8,128)(2,1)S(1)} slice(bf16[4,32,3072]{2,1,0:T(8,128)(2,1)} %bitcast.45), slice={[1:4:2], [0:32:1], [0:3072:1]} | slice | bytes 786432 | tf_op jit(solution)/shard_map/slice | solution.py:284
  43.2 0.4 collective-permute-start.3
  43.7 0.0 collective-permute-done.5
  43.7 0.1 collective-permute-start.6
  43.8 5.5 %collective-permute-done.6 = bf16[2,4,32,256]{3,2,1,0:T(8,128)(2,1)S(1)} collective-permute-done((bf16[2,4,32,256]{3,2,1,0:T(8,128)(2,1)S(1)}, bf16[2,4,32,256]{3,2,1,0:T(8,128)(2,1)S(1)}, u32[]{:S(2)}, u32[]{:S(2)}) %collective-permute-start.6) | collective-permute-done | bytes 131104 | tf_op jit(solution)/shard_map/ppermute | solution.py:131
  49.3 0.6 gather_fusion
  49.9 0.0 collective-permute-done.3
  49.9 0.0 copy-done.1
  49.9 0.1 convert_add_fusion
  50.0 0.4 collective-permute-start.4
  50.4 0.9 %fusion.9 = bf16[32,16,256]{2,1,0:T(8,128)(2,1)} fusion(bf16[16,32,256]{2,1,0:T(8,128)(2,1)S(1)} %bitcast.48, pred[16]{0:T(512)(128)(4,1)S(1)} %broadcast_in_dim.51), kind=kLoop, calls=%fused_computation.19 | loop fusion | flops 131072 | bytes 524304 | tf_op jit(solution)/shard_map/transpose | solution.py:271
  51.2 4.9 %collective-permute-done.4 = bf16[32,3072]{1,0:T(8,128)(2,1)S(1)} collective-permute-done((bf16[32,3072]{1,0:T(8,128)(2,1)S(1)}, bf16[32,3072]{1,0:T(8,128)(2,1)S(1)}, u32[]{:S(2)}, u32[]{:S(2)}) %collective-permute-start.4) | collective-permute-done | bytes 196640 | tf_op jit(solution)/shard_map/ppermute | solution.py:131
  56.2 0.7 %fusion.8 = bf16[32,3072]{1,0:T(8,128)(2,1)} fusion(f32[2,32,3072]{2,1,0:T(8,128)S(1)} %convert_add_fusion, bf16[32,3072]{1,0:T(8,128)(2,1)S(1)} %collective-permute-done.4, f32[3072]{0:T(1024)S(1)} %bitcast.55), kind=kLoop, calls=%fused_computation.16 | loop fusion | flops 393216 | bytes 798720 | tf_op jit(solution)/shard_map/convert_element_type | solution.py:288
  (13 shorter events, 0.1 us)
Async XLA Ops:
  1.7 8.5 %copy-start.3 = (f32[3,3072]{1,0:T(4,128)S(1)}, f32[3,3072]{1,0:T(4,128)}, u32[]{:S(2)}) copy-start(f32[3,3072]{1,0:T(4,128)} %param.9) | copy-start | bytes 110596
  1.7 8.5 %copy-start.2 = (bf16[32,3072]{1,0:T(8,128)(2,1)S(1)}, bf16[32,3072]{1,0:T(8,128)(2,1)}, u32[]{:S(2)}) copy-start(bf16[32,3072]{1,0:T(8,128)(2,1)} %param.8) | copy-start | bytes 589828
  2.8 33.2 %all-to-all-start = ((bf16[16,4,32,256]{3,2,1,0:T(8,128)(2,1)}), bf16[16,4,32,256]{3,2,1,0:T(8,128)(2,1)S(1)}, u32[]{:S(2)}, u32[]{:S(2)}) async-start(bf16[16,4,32,256]{3,2,1,0:T(8,128)(2,1)} %bitcast.7), calls=%async_computation | async-start | bytes 2097152 | tf_op jit(solution)/shard_map/all_to_all | solution.py:248
  10.8 15.1 %collective-permute-start.1 = (bf16[32,3072]{1,0:T(8,128)(2,1)S(1)}, bf16[32,3072]{1,0:T(8,128)(2,1)S(1)}, u32[]{:S(2)}, u32[]{:S(2)}) collective-permute-start(bf16[32,3072]{1,0:T(8,128)(2,1)S(1)} %fusion.5), channel_id=1, source_target_pairs={{0,2},{2,0},{1,3},{3,1},{4,6},{6,4},{5,7},{7,5},{8,10},{10,8},{9,1... | collective-permute-start | bytes 589832 | tf_op jit(solution)/shard_map/ppermute | solution.py:131
  12.8 13.7 %collective-permute-start = (bf16[32,3072]{1,0:T(8,128)(2,1)S(1)}, bf16[32,3072]{1,0:T(8,128)(2,1)S(1)}, u32[]{:S(2)}, u32[]{:S(2)}) collective-permute-start(bf16[32,3072]{1,0:T(8,128)(2,1)S(1)} %fusion.5), channel_id=1, source_target_pairs={{0,1},{1,0},{2,3},{3,2},{4,5},{5,4},{6,7},{7,6},{8,9},{9,8},{10,11... | collective-permute-start | bytes 589832 | tf_op jit(solution)/shard_map/ppermute | solution.py:131
  12.8 9.3 %copy-start.4 = (s32[4]{0:T(128)S(1)}, s32[4]{0:T(128)}, u32[]{:S(2)}) copy-start(s32[4]{0:T(128)} %param.15) | copy-start | bytes 52
  26.0 1.4 %collective-permute-start.2 = (bf16[32,3072]{1,0:T(8,128)(2,1)S(1)}, bf16[32,3072]{1,0:T(8,128)(2,1)S(1)}, u32[]{:S(2)}, u32[]{:S(2)}) collective-permute-start(bf16[32,3072]{1,0:T(8,128)(2,1)S(1)} %collective-permute-done.1), channel_id=1, source_target_pairs={{0,1},{1,0},{2,3},{3,2},{4,5},{5,4},{6,7},{7,6},{8,9},{9,8},{10,11... | collective-permute-start | bytes 589832 | tf_op jit(solution)/shard_map/ppermute | solution.py:131
  35.9 7.8 %collective-permute-start.5 = (bf16[4,2,32,256]{3,2,1,0:T(8,128)(2,1)S(1)}, bf16[4,2,32,256]{3,2,1,0:T(8,128)(2,1)S(1)}, u32[]{:S(2)}, u32[]{:S(2)}) collective-permute-start(bf16[4,2,32,256]{3,2,1,0:T(8,128)(2,1)S(1)} %get-tuple-element.7), channel_id=1, source_target_pairs={{0,1},{1,0},{2,3},{3,2},{4,5},{5,4},{6,7},{7,6},{8,9},{9,8},{10,11... | collective-permute-start | bytes 393224 | tf_op jit(solution)/shard_map/ppermute | solution.py:131
  36.1 1.0 %copy-start = (bf16[16,4,32,256]{3,2,1,0:T(8,128)(2,1)}, bf16[16,4,32,256]{3,2,1,0:T(8,128)(2,1)S(1)}, u32[]{:S(2)}) copy-start(bf16[16,4,32,256]{3,2,1,0:T(8,128)(2,1)S(1)} %all-to-all-done.source_ref) | copy-start | bytes 3145732
  42.1 7.8 %copy-start.1 = (bf16[128,3072]{1,0:T(8,128)(2,1)S(1)}, bf16[128,3072]{1,0:T(8,128)(2,1)}, u32[]{:S(2)}) copy-start(bf16[128,3072]{1,0:T(8,128)(2,1)} %attend_heads.1) | copy-start | bytes 2359300
  43.2 6.7 %collective-permute-start.3 = (bf16[2,32,3072]{2,1,0:T(8,128)(2,1)S(1)}, bf16[2,32,3072]{2,1,0:T(8,128)(2,1)S(1)}, u32[]{:S(2)}, u32[]{:S(2)}) collective-permute-start(bf16[2,32,3072]{2,1,0:T(8,128)(2,1)S(1)} %slice.44), channel_id=1, source_target_pairs={{0,1},{1,0},{2,3},{3,2},{4,5},{5,4},{6,7},{7,6},{8,9},{9,8},{10,11... | collective-permute-start | bytes 1179656 | tf_op jit(solution)/shard_map/ppermute | solution.py:131
  43.7 5.6 %collective-permute-start.6 = (bf16[2,4,32,256]{3,2,1,0:T(8,128)(2,1)S(1)}, bf16[2,4,32,256]{3,2,1,0:T(8,128)(2,1)S(1)}, u32[]{:S(2)}, u32[]{:S(2)}) collective-permute-start(bf16[2,4,32,256]{3,2,1,0:T(8,128)(2,1)S(1)} %fusion.11), channel_id=1, source_target_pairs={{0,2},{2,0},{1,3},{3,1},{4,6},{6,4},{5,7},{7,5},{8,10},{10,8},{9,1... | collective-permute-start | bytes 393224 | tf_op jit(solution)/shard_map/ppermute | solution.py:131
  50.0 6.1 %collective-permute-start.4 = (bf16[32,3072]{1,0:T(8,128)(2,1)S(1)}, bf16[32,3072]{1,0:T(8,128)(2,1)S(1)}, u32[]{:S(2)}, u32[]{:S(2)}) collective-permute-start(bf16[32,3072]{1,0:T(8,128)(2,1)S(1)} %fusion.10), channel_id=1, source_target_pairs={{0,2},{2,0},{1,3},{3,1},{4,6},{6,4},{5,7},{7,5},{8,10},{10,8},{9,1... | collective-permute-start | bytes 589832 | tf_op jit(solution)/shard_map/ppermute | solution.py:131

commit v2 on v0

--- a/solution.py
+++ b/solution.py
@@ -1,9 +1,13 @@
+import functools
 import math
 
 import jax
 import jax.numpy as jnp
 from jax import lax
+from jax.experimental import pallas as pl
+from jax.experimental.pallas import tpu as pltpu
 from jax.sharding import PartitionSpec as P
+
 
 EPSILON = 1e-06
 NEGATIVE = -1e30
@@ -125,9 +129,291 @@
     return (update, new_cache)
 
 
+def swap(values, axis):
+    return lax.ppermute(values, axis, [(0, 1), (1, 0)])
+
+
+MIB = 1 << 20
+VMEM = pl.BlockSpec(memory_space=pltpu.VMEM)
+SMEM = pl.BlockSpec(memory_space=pltpu.SMEM)
+
+
+def kernel_call(body, inputs, outputs, scratch, limit, cost, smem_inputs=0):
+    count = len(inputs)
+    return pl.pallas_call(
+        body,
+        in_specs=[SMEM] * smem_inputs + [VMEM] * (count - smem_inputs),
+        out_specs=[VMEM] * len(outputs),
+        out_shape=outputs,
+        scratch_shapes=scratch,
+        compiler_params=pltpu.CompilerParams(vmem_limit_bytes=limit * MIB),
+        cost_estimate=pl.CostEstimate(flops=cost[0], bytes_accessed=cost[1], transcendentals=cost[2]),
+    )(*inputs)
+
+
+def regroup_kernel(stale_ref, out_ref, wide_ref):
+    rows, heads, both = stale_ref.shape
+    patches, _, per_group = out_ref.shape[:3]
+    for lanes in range(both // 128):
+        columns = slice(lanes * 128, (lanes + 1) * 128)
+        wide_ref[lanes] = stale_ref[:, :, columns].astype(jnp.float32).reshape(rows * heads, 128)
+        for head in range(heads):
+            values = wide_ref[lanes, pl.ds(head, rows, stride=heads), :].astype(jnp.bfloat16)
+            for patch in range(patches):
+                out_ref[patch, head // per_group, head % per_group, :, columns] = values
+
+
+def relayout_kernel(weight_ref, out_ref, wide_ref):
+    depth, heads, width = weight_ref.shape
+    block = wide_ref.shape[1] // heads
+
+    def step(index, carry):
+        rows = pl.ds(pl.multiple_of(index * block, block), block)
+        for lanes in range(width // 128):
+            columns = slice(lanes * 128, (lanes + 1) * 128)
+            values = weight_ref[rows, :, columns].astype(jnp.float32)
+            wide_ref[lanes] = values.reshape(block * heads, 128)
+            for head in range(heads):
+                picked = wide_ref[lanes, pl.ds(head, block, stride=heads), :]
+                out_ref[head, rows, columns] = picked.astype(jnp.bfloat16)
+        return carry
+
+    lax.fori_loop(0, depth // block, step, 0)
+
+
+def normalize_kernel(token_ref, modulation_ref, out_ref):
+    values = normalize_rows(token_ref[...].astype(jnp.float32))
+    shifted = values * (1.0 + modulation_ref[1:2]) + modulation_ref[0:1]
+    out_ref[...] = shifted.astype(jnp.bfloat16)
+
+
+def project_kernel(
+    own_ref, beside_ref, across_ref, diagonal_ref, weight_ref, query_gain_ref, key_gain_ref,
+    query_ref, own_cache_ref, beside_cache_ref, across_cache_ref, normed_ref
+):
+    head_dim = query_gain_ref.shape[1]
+    rows = own_ref.shape[0]
+    for part, ref in enumerate((own_ref, beside_ref, across_ref, diagonal_ref)):
+        normed_ref[part * rows : (part + 1) * rows] = ref[...]
+    caches = (own_cache_ref, beside_cache_ref, across_cache_ref.at[0], across_cache_ref.at[1])
+    for head in range(weight_ref.shape[0]):
+        projected = jnp.dot(normed_ref[...], weight_ref[head], preferred_element_type=jnp.float32)
+        query_ref[head] = rms_gain(projected[:, :head_dim], query_gain_ref[...]).astype(jnp.bfloat16)
+        keys = rms_gain(projected[:, head_dim : 2 * head_dim], key_gain_ref[...]).astype(jnp.bfloat16)
+        values = projected[:, 2 * head_dim :].astype(jnp.bfloat16)
+        for part, cache_ref in enumerate(caches):
+            span = slice(part * rows, (part + 1) * rows)
+            cache_ref[head, :, :head_dim] = keys[span]
+            cache_ref[head, :, head_dim:] = values[span]
+
+
+def collect_kernel(own_ref, beside_ref, across_ref, diagonal_ref, out_ref, part_ref, wide_ref):
+    per_group, rows, both = own_ref.shape
+    heads = out_ref.shape[1]
+    own_chunk = lax.axis_index("head") * 2 + lax.axis_index("rep")
+    for part, ref in enumerate((own_ref, beside_ref, across_ref, diagonal_ref)):
+        part_ref[part] = ref[...]
+    for lanes in range(both // 128):
+        columns = slice(lanes * 128, (lanes + 1) * 128)
+        for head in range(heads):
+            part = own_chunk ^ (head // per_group)
+            values = part_ref[part, head % per_group, :, columns].astype(jnp.float32)
+            wide_ref[lanes, pl.ds(head, rows, stride=heads), :] = values
+        out_ref[:, :, columns] = wide_ref[lanes].reshape(rows, heads, 128).astype(jnp.bfloat16)
+
+
+def add_kernel(kept_ref, received_ref, out_ref):
+    total = kept_ref[...] + received_ref[...].astype(jnp.float32)
+    out_ref[...] = total.astype(out_ref.dtype)
+
+
+def finish_kernel(kept_ref, beside_ref, across_ref, modulation_ref, out_ref):
+    near = kept_ref[...] + beside_ref[...].astype(jnp.float32)
+    total = near + across_ref[...].astype(jnp.float32)
+    out_ref[...] = (modulation_ref[2:3] * total).astype(jnp.bfloat16)
+
+
+def attend_kernel(
+    first, length_ref, query_ref, own_ref, beside_ref, across_ref, source_ref, weight_ref,
+    kept_ref, sent_ref, keys_ref, attended_ref
+):
+    heads, chunk, both = own_ref.shape
+    rows = attended_ref.shape[0]
+    parts = 4
+    head_dim = both // 2
+    patches = source_ref.shape[0] // parts
+    per_patch = parts * chunk
+    scale = 1.0 / math.sqrt(head_dim)
+    own_patch = lax.axis_index("patch")
+    own_chunk = lax.axis_index("head") * 2 + lax.axis_index("rep")
+    index = lax.broadcasted_iota(jnp.int32, (rows, patches * per_patch), 1)
+    mask = index < length_ref[0]
+    for patch in range(1, patches):
+        inside = (index >= patch * per_patch) & (index < patch * per_patch + length_ref[patch])
+        mask = mask | inside
+    caches = (own_ref, beside_ref, across_ref.at[0], across_ref.at[1])
+    for head in range(heads):
+        for source in range(patches * parts):
+            keys_ref[head, source * chunk : (source + 1) * chunk] = source_ref[source, head]
+        for part, cache_ref in enumerate(caches):
+            place = own_patch * parts + (own_chunk ^ part)
+            start = pl.multiple_of(place * chunk, chunk)
+            keys_ref[head, pl.ds(start, chunk)] = cache_ref[head]
+    for head in range(heads):
+        scores = lax.dot_general(
+            query_ref[head, first : first + rows],
+            keys_ref[head, :, :head_dim],
+            (((1,), (1,)), ((), ())),
+            preferred_element_type=jnp.float32,
+        )
+        scores = jnp.where(mask, scores * scale, NEGATIVE)
+        row_max = jnp.max(scores, axis=1, keepdims=True)
+        weights = jnp.where(mask, jnp.exp(scores - row_max), 0.0)
+        denominator = jnp.sum(weights, axis=1, keepdims=True)
+        summed = jnp.dot(
+            weights.astype(jnp.bfloat16), keys_ref[head, :, head_dim:], preferred_element_type=jnp.float32
+        )
+        attended_ref[:, head * head_dim : (head + 1) * head_dim] = (summed / denominator).astype(
+            jnp.bfloat16
+        )
+    partial = jnp.dot(attended_ref[...], weight_ref[...], preferred_element_type=jnp.float32)
+    partial = partial.astype(jnp.bfloat16)
+    kept_ref[...] = partial[:chunk].astype(jnp.float32)
+    sent_ref[...] = partial[chunk:]
+
+
+def attend_half(half, lengths, queries, caches, sources, out_weight):
+    heads, chunk, both = caches[0].shape
+    depth, width = out_weight.shape
+    keys = sources.shape[0] * chunk
+    rows = 2 * chunk
+    return kernel_call(
+        functools.partial(attend_kernel, half * rows),
+        (lengths, queries) + caches + (sources, out_weight),
+        [
+            jax.ShapeDtypeStruct((chunk, width), jnp.float32),
+            jax.ShapeDtypeStruct((chunk, width), jnp.bfloat16),
+        ],
+        [
+            pltpu.VMEM((heads, keys, both), jnp.bfloat16),
+            pltpu.VMEM((rows, depth), jnp.bfloat16),
+        ],
+        12,
+        (2 * rows * depth * width + 4 * rows * keys * depth, 2 * (depth * width + keys * heads * both), 0),
+        smem_inputs=1,
+    )
+
+
+def per_device_pair(
+    tokens, modulation, in_weight, query_gain, key_gain, out_weight, stale_cache, lengths
+):
+    return paired_block(
+        tokens, modulation, in_weight, query_gain, key_gain, out_weight, stale_cache, lengths
+    )
+
+
+def paired_block(
+    tokens, modulation, in_weight, query_gain, key_gain, out_weight, stale_cache, lengths
+):
+    rows, width = tokens.shape
+    _, heads_dev, triple = in_weight.shape
+    head_dim = query_gain.shape[0]
+    patches = lax.axis_size("patch")
+    parts = 4
+    heads = heads_dev * parts
+    both = 2 * head_dim
+    half = jnp.bfloat16
+
+    outgoing = kernel_call(
+        regroup_kernel,
+        (stale_cache,),
+        [jax.ShapeDtypeStruct((patches, parts, heads_dev, rows, both), half)],
+        [pltpu.VMEM((both // 128, rows * heads, 128), jnp.float32)],
+        8,
+        (0, 2 * rows * heads * both * (patches + 1), 0),
+    )[0].reshape(patches * parts, heads_dev, rows, both)
+    sources = lax.all_to_all(
+        outgoing, ("patch", "head", "rep"), split_axis=0, concat_axis=0, tiled=True
+    )
+
+    weight_rows = kernel_call(
+        relayout_kernel,
+        (in_weight,),
+        [jax.ShapeDtypeStruct((heads_dev, width, triple), half)],
+        [pltpu.VMEM((triple // 128, 128 * heads_dev, 128), jnp.float32)],
+        8,
+        (0, 4 * heads_dev * width * triple, 0),
+    )[0]
+    normed = kernel_call(
+        normalize_kernel,
+        (tokens, modulation),
+        [jax.ShapeDtypeStruct((rows, width), half)],
+        [],
+        8,
+        (8 * rows * width, 4 * rows * width, 0),
+    )[0]
+    across = swap(normed, "head")
+    beside = swap(normed, "rep")
+    diagonal = swap(across, "rep")
+    queries, own_cache, beside_cache, across_cache = kernel_call(
+        project_kernel,
+        (normed, beside, across, diagonal, weight_rows, query_gain[None], key_gain[None]),
+        [
+            jax.ShapeDtypeStruct((heads_dev, parts * rows, head_dim), half),
+            jax.ShapeDtypeStruct((heads_dev, rows, both), half),
+            jax.ShapeDtypeStruct((heads_dev, rows, both), half),
+            jax.ShapeDtypeStruct((2, heads_dev, rows, both), half),
+        ],
+        [pltpu.VMEM((parts * rows, width), half)],
+        8,
+        (2 * parts * rows * width * heads_dev * triple, 2 * width * heads_dev * triple, 0),
+    )
+    caches = (own_cache, beside_cache, across_cache)
+
+    from_across = swap(across_cache, "head")
+    from_beside = swap(beside_cache, "rep")
+    from_diagonal = swap(from_across[1], "rep")
+    new_cache = kernel_call(
+        collect_kernel,
+        (own_cache, from_beside, from_across[0], from_diagonal),
+        [jax.ShapeDtypeStruct((rows, heads, both), half)],
+        [
+            pltpu.VMEM((parts, heads_dev, rows, both), half),
+            pltpu.VMEM((both // 128, rows * heads, 128), jnp.float32),
+        ],
+        8,
+        (0, 4 * rows * heads * both, 0),
+    )[0]
+
+    flat_weight = out_weight.reshape(heads_dev * head_dim, width)
+    far_kept, far_sent = attend_half(1, lengths, queries, caches, sources, flat_weight)
+    far_received = swap(far_sent, "rep")
+    far_sum = kernel_call(
+        add_kernel,
+        (far_kept, far_received),
+        [jax.ShapeDtypeStruct((rows, width), half)],
+        [],
+        4,
+        (rows * width, 8 * rows * width, 0),
+    )[0]
+    received = swap(far_sum, "head")
+    near_kept, near_sent = attend_half(0, lengths, queries, caches, sources, flat_weight)
+    near_received = swap(near_sent, "rep")
+    update = kernel_call(
+        finish_kernel,
+        (near_kept, near_received, received, modulation),
+        [jax.ShapeDtypeStruct((rows, width), half)],
+        [],
+        4,
+        (3 * rows * width, 10 * rows * width, 0),
+    )[0]
+    return (update, new_cache)
+
+
 def solution(mesh):
+    paired = mesh.shape["head"] == 2 and mesh.shape["rep"] == 2
     return jax.shard_map(
-        per_device,
+        per_device_pair if paired else per_device,
         mesh=mesh,
         in_specs=(
             P(("clip", "patch", "head", "rep"), None),

time: 128 us -> 51.3 us (0.40)
  local copies, waits for them, and re-layouts: 27.7 us -> 6.38 us
  waiting for transfers between devices: 36.3 us -> 15.7 us
  blocking collectives: 18.5 us -> 0 us
  matrix products: 16.4 us -> 0 us
  Pallas kernels: 0 us -> 15.3 us
  between operations: 14.2 us -> 0.79 us
  other arithmetic: 10.2 us -> 0 us
  starting transfers between devices: 4.28 us -> 12.7 us
    all_gather x1 -> x0, waiting for transfers between devices: 24.1 us -> none  [per_device(): shard_part = lax.all_gather(stale_heads, 'patch', axis=0, tiled=True)]
    dot_general x5 -> x0, matrix products: 16.4 us -> none  [the longest x1 7.79 us: project(): jnp.dot(normed, flat_weight, preferred_element_type=jnp.float32)]
    ppermute x0 -> x9, waiting for transfers between devices: none -> 15.7 us  [swap(): return lax.ppermute(values, axis, [(0, 1), (1, 0)])]
    pallas_call x0 -> x9, Pallas kernels: none -> 15.3 us  [kernel_call(): pl.pallas_call(body, in_specs=[SMEM] * smem_inputs + [VMEM] * (count - sm...]
    dot_general x1 -> x0, local copies, waits for them, and re-layouts: 12.7 us -> none  [project(): jnp.dot(normed, flat_weight, preferred_element_type=jnp.float32)]
    reduce_scatter x1 -> x0, waiting for transfers between devices: 12.1 us -> none  [per_device(): lax.psum_scatter(jnp.dot(flat_rows, flat_weight, preferred_element_type=j...]
    all_gather x1 -> x0, blocking collectives: 9.92 us -> none  [per_device(): lax.all_gather(normed, ('head', 'rep'), axis=0, tiled=True)]
    all_to_all x1 -> x0, blocking collectives: 8.54 us -> none  [per_device(): lax.all_to_all(own_rows, ('head', 'rep'), split_axis=0, concat_axis=1, ti...]
  transfers between devices with their start and end apart: 3 -> 10, of which waited for: 2 -> 3; matrix products, arithmetic and copies ran while one was open for 29% -> 0% of each run, Pallas kernels for 0% -> 20%
where the time goes in v2:
time: 51.3 us; the launch traced here: 50.9 us
  waiting for transfers between devices  15.7 us (31%)
  Pallas kernels  15.3 us (30%)
  starting transfers between devices  12.7 us (25%)
  local copies, waits for them, and re-layouts  6.38 us (12%)
  between operations  0.79 us (2%)
    ppermute x9, waiting for transfers between devices, swap(): return lax.ppermute(values, axis, [(0, 1), (1, 0)])  15.7 us
    pallas_call x9, Pallas kernels, kernel_call(): pl.pallas_call(body, in_specs=[SMEM] * smem_inputs + [VMEM] * (count - sm...  15.3 us
    all_to_all x1, starting transfers between devices, paired_block(): lax.all_to_all(outgoing, ('patch', 'head', 'rep'), split_axis=0, concat_a...  7.44 us
    unnamed x18, local copies, waits for them, and re-layouts  6.37 us
    ppermute x9, starting transfers between devices, swap(): return lax.ppermute(values, axis, [(0, 1), (1, 0)])  5.25 us
  transfers between devices with their start and end apart: 10, of which 3 were waited for; matrix products, arithmetic and copies ran while one was open for 0% of the time, Pallas kernels for 20%

profile of v2, /device:TPU:0, one launch (start us, length us, event | category | flops | bytes accessed | tf_op | source)
XLA Modules:
  0.0 50.9 jit_solution(13631023197317394772)
XLA Ops:
  0.6 0.0 copy-start.2
  0.6 0.9 %copy-done.2 = bf16[32,16,256]{2,1,0:T(8,128)(2,1)S(1)} copy-done((bf16[32,16,256]{2,1,0:T(8,128)(2,1)S(1)}, bf16[32,16,256]{2,1,0:T(8,128)(2,1)}, u32[]{:S(2)}) %copy-start.2) | copy-done | bytes 262168
  1.6 1.3 %shard_map.98 = bf16[4,4,4,32,256]{4,3,2,1,0:T(8,128)(2,1)} custom-call(bf16[32,16,256]{2,1,0:T(8,128)(2,1)S(1)} %copy-done.2), custom_call_target="tpu_custom_call" | custom-call | bytes 1310720 | tf_op jit(solution)/shard_map/pallas_call | solution.py:143
  2.8 7.4 %all-to-all-start = ((bf16[16,4,32,256]{3,2,1,0:T(8,128)(2,1)}), bf16[16,4,32,256]{3,2,1,0:T(8,128)(2,1)}, u32[]{:S(2)}, u32[]{:S(2)}) async-start(bf16[16,4,32,256]{3,2,1,0:T(8,128)(2,1)} %bitcast.2), calls=%async_computation | async-start | bytes 2097152 | tf_op jit(solution)/shard_map/all_to_all | solution.py:335
  10.3 0.0 copy-start.3
  10.3 0.8 %copy-done.3 = f32[3,3072]{1,0:T(4,128)S(1)} copy-done((f32[3,3072]{1,0:T(4,128)S(1)}, f32[3,3072]{1,0:T(4,128)}, u32[]{:S(2)}) %copy-start.3) | copy-done | bytes 36888
  11.1 0.0 copy-start.5
  11.1 0.9 %copy-done.5 = bf16[32,3072]{1,0:T(8,128)(2,1)S(1)} copy-done((bf16[32,3072]{1,0:T(8,128)(2,1)S(1)}, bf16[32,3072]{1,0:T(8,128)(2,1)}, u32[]{:S(2)}) %copy-start.5) | copy-done | bytes 196632
  12.0 0.0 copy-start.7
  12.0 0.0 copy-start.8
  12.0 0.3 shard_map.95.own_ref
  12.3 1.9 %collective-permute-start.1 = (bf16[32,3072]{1,0:T(8,128)(2,1)S(1)}, bf16[32,3072]{1,0:T(8,128)(2,1)S(1)}, u32[]{:S(2)}, u32[]{:S(2)}) collective-permute-start(bf16[32,3072]{1,0:T(8,128)(2,1)S(1)} %shard_map.95.own_ref), channel_id=1, source_target_pairs={{0,2},{2,0},{1,3},{3,1},{4,6},{6,4},{5,7},{7,5},{8,10},{10,8},{9,1... | collective-permute-start | bytes 589832 | tf_op jit(solution)/shard_map/ppermute | solution.py:133
  14.2 0.0 collective-permute-start
  14.3 11.7 %collective-permute-done.1.across_ref = bf16[32,3072]{1,0:T(8,128)(2,1)S(1)} collective-permute-done((bf16[32,3072]{1,0:T(8,128)(2,1)S(1)}, bf16[32,3072]{1,0:T(8,128)(2,1)S(1)}, u32[]{:S(2)}, u32[]{:S(2)}) %collective-permute-start.1) | collective-permute-done | bytes 196640 | tf_op jit(solution)/shard_map/ppermute | solution.py:133
  26.0 0.0 collective-permute-start.2
  26.0 0.0 copy-start.1
  26.0 3.7 %copy-done.1 = bf16[3072,4,384]{2,1,0:T(4,128)(2,1)S(1)} copy-done((bf16[3072,4,384]{2,1,0:T(4,128)(2,1)S(1)}, bf16[3072,4,384]{2,1,0:T(4,128)(2,1)}, u32[]{:S(2)}) %copy-start.1) | copy-done | bytes 9437208
  29.7 3.9 %shard_map.96.weight_ref = bf16[4,3072,384]{2,1,0:T(8,128)(2,1)S(1)} custom-call(bf16[3072,4,384]{2,1,0:T(4,128)(2,1)S(1)} %copy-done.1), custom_call_target="tpu_custom_call" | custom-call | bytes 18874368 | tf_op jit(solution)/shard_map/pallas_call | solution.py:143
  33.6 0.0 copy-start
  33.6 0.0 copy-start.6
  33.6 0.0 collective-permute-done.beside_ref
  33.6 0.0 collective-permute-done.2.diagonal_ref
  33.6 0.0 copy-done.7
  33.6 0.0 copy-done.8
  33.7 2.0 %shard_map.97 = (bf16[4,128,128]{2,1,0:T(8,128)(2,1)S(1)}, bf16[4,32,256]{2,1,0:T(8,128)(2,1)S(1)}, bf16[4,32,256]{2,1,0:T(8,128)(2,1)S(1)}, bf16[2,4,32,256]{3,2,1,0:T(8,128)(2,1)S(1)}) custom-call(bf16[32,3072]{1,0:T(8,128)(2,1)S(1)} %shard_map.95.own_ref, bf16[32,3072]{1,0:T(8,128)(2,1)S(1)} %collective-permute-done.beside_ref, ...), custom_call_target="tpu_custom_call" | custom-call | flops 1207959552 | bytes 9437184 | tf_op jit(solution)/shard_map/pallas_call | solution.py:143
  35.6 0.0 all-to-all-done.source_ref
  35.6 0.0 copy-start.4
  35.6 0.0 copy-done
  35.7 0.0 copy-done.6
  35.7 3.1 %shard_map.100 = (f32[32,3072]{1,0:T(8,128)S(1)}, bf16[32,3072]{1,0:T(8,128)(2,1)S(1)}) custom-call(s32[4]{0:T(128)S(1)} %copy-done.6, bf16[4,128,128]{2,1,0:T(8,128)(2,1)S(1)} %get-tuple-element.10.query_ref, bf16[4,32,256]{2,1,0:T(8,128)(2,1)S(1)} %get-tuple-element.11.own_ref, bf16[4,32,256]{2,1,0:T(8,128)(2,1)S(1)} %get-tuple-element.12.beside_ref, ...), custom_call_target="tpu_custom_call" | custom-call | flops 268435456 | bytes 4194304 | tf_op jit(solution)/shard_map/pallas_call | solution.py:143
  38.7 0.6 %collective-permute-start.4 = (bf16[32,3072]{1,0:T(8,128)(2,1)S(1)}, bf16[32,3072]{1,0:T(8,128)(2,1)S(1)}, u32[]{:S(2)}, u32[]{:S(2)}) collective-permute-start(bf16[32,3072]{1,0:T(8,128)(2,1)S(1)} %get-tuple-element.17), channel_id=1, source_target_pairs={{0,1},{1,0},{2,3},{3,2},{4,5},{5,4},{6,7},{7,6},{8,9},{9,8},{10,11... | collective-permute-start | bytes 589832 | tf_op jit(solution)/shard_map/ppermute | solution.py:133
  39.3 0.0 collective-permute-start.7
  39.3 0.2 collective-permute-start.6
  39.5 3.1 %shard_map.99 = (f32[32,3072]{1,0:T(8,128)S(1)}, bf16[32,3072]{1,0:T(8,128)(2,1)S(1)}) custom-call(s32[4]{0:T(128)S(1)} %copy-done.6, bf16[4,128,128]{2,1,0:T(8,128)(2,1)S(1)} %get-tuple-element.10.query_ref, bf16[4,32,256]{2,1,0:T(8,128)(2,1)S(1)} %get-tuple-element.11.own_ref, bf16[4,32,256]{2,1,0:T(8,128)(2,1)S(1)} %get-tuple-element.12.beside_ref, ...), custom_call_target="tpu_custom_call" | custom-call | flops 268435456 | bytes 4194304 | tf_op jit(solution)/shard_map/pallas_call | solution.py:143
  42.5 0.4 collective-permute-start.3
  42.9 0.0 collective-permute-done.4.received_ref
  43.0 2.1 %collective-permute-start.5 = (bf16[32,3072]{1,0:T(8,128)(2,1)S(1)}, bf16[32,3072]{1,0:T(8,128)(2,1)S(1)}, u32[]{:S(2)}, u32[]{:S(2)}) collective-permute-start(bf16[32,3072]{1,0:T(8,128)(2,1)S(1)} %shard_map.101), channel_id=1, source_target_pairs={{0,2},{2,0},{1,3},{3,1},{4,6},{6,4},{5,7},{7,5},{8,10},{10,8},{9,1... | collective-permute-start | bytes 589832 | tf_op jit(solution)/shard_map/ppermute | solution.py:133
  45.1 0.0 collective-permute-done.7
  45.1 0.1 collective-permute-start.8
  45.2 0.0 collective-permute-done.6.beside_ref
  45.2 1.2 %collective-permute-done.8.diagonal_ref = bf16[4,32,256]{2,1,0:T(8,128)(2,1)S(1)} collective-permute-done((bf16[4,32,256]{2,1,0:T(8,128)(2,1)S(1)}, bf16[4,32,256]{2,1,0:T(8,128)(2,1)S(1)}, u32[]{:S(2)}, u32[]{:S(2)}) %collective-permute-start.8) | collective-permute-done | bytes 65568 | tf_op jit(solution)/shard_map/ppermute | solution.py:133
  46.4 1.0 %shard_map.103 = bf16[32,16,256]{2,1,0:T(8,128)(2,1)} custom-call(bf16[4,32,256]{2,1,0:T(8,128)(2,1)S(1)} %get-tuple-element.11.own_ref, bf16[4,32,256]{2,1,0:T(8,128)(2,1)S(1)} %collective-permute-done.6.beside_ref, bf16[4,32,256]{2,1,0:T(8,128)(2,1)S(1)} %get-tuple-element.19.across_ref, bf16[4,32,256]{2,1,0:T(8,128)(2,1)S(1)} %collective-permute-done.8.diagonal_ref), custom_call_target="tpu_custom_call" | custom-call | bytes 524288 | tf_op jit(solution)/shard_map/pallas_call | solution.py:143
  47.4 0.0 collective-permute-done.3.beside_ref
  47.4 2.8 %collective-permute-done.5.across_ref = bf16[32,3072]{1,0:T(8,128)(2,1)S(1)} collective-permute-done((bf16[32,3072]{1,0:T(8,128)(2,1)S(1)}, bf16[32,3072]{1,0:T(8,128)(2,1)S(1)}, u32[]{:S(2)}, u32[]{:S(2)}) %collective-permute-start.5) | collective-permute-done | bytes 196640 | tf_op jit(solution)/shard_map/ppermute | solution.py:133
  50.2 0.0 copy-done.4
  50.2 0.8 %shard_map.102 = bf16[32,3072]{1,0:T(8,128)(2,1)} custom-call(f32[32,3072]{1,0:T(8,128)S(1)} %get-tuple-element.14.kept_ref, bf16[32,3072]{1,0:T(8,128)(2,1)S(1)} %collective-permute-done.3.beside_ref, bf16[32,3072]{1,0:T(8,128)(2,1)S(1)} %collective-permute-done.5.across_ref, f32[3,3072]{1,0:T(4,128)S(1)} %copy-done.4), custom_call_target="tpu_custom_call" | custom-call | flops 294912 | bytes 983040 | tf_op jit(solution)/shard_map/pallas_call | solution.py:143
  (2 shorter events, 0.0 us)
Async XLA Ops:
  0.6 1.0 %copy-start.2 = (bf16[32,16,256]{2,1,0:T(8,128)(2,1)S(1)}, bf16[32,16,256]{2,1,0:T(8,128)(2,1)}, u32[]{:S(2)}) copy-start(bf16[32,16,256]{2,1,0:T(8,128)(2,1)} %stale_ref.1) | copy-start | bytes 786436
  2.8 32.8 %all-to-all-start = ((bf16[16,4,32,256]{3,2,1,0:T(8,128)(2,1)}), bf16[16,4,32,256]{3,2,1,0:T(8,128)(2,1)}, u32[]{:S(2)}, u32[]{:S(2)}) async-start(bf16[16,4,32,256]{3,2,1,0:T(8,128)(2,1)} %bitcast.2), calls=%async_computation | async-start | bytes 2097152 | tf_op jit(solution)/shard_map/all_to_all | solution.py:335
  10.3 0.8 %copy-start.3 = (f32[3,3072]{1,0:T(4,128)S(1)}, f32[3,3072]{1,0:T(4,128)}, u32[]{:S(2)}) copy-start(f32[3,3072]{1,0:T(4,128)} %modulation_ref.3) | copy-start | bytes 110596
  11.1 0.9 %copy-start.5 = (bf16[32,3072]{1,0:T(8,128)(2,1)S(1)}, bf16[32,3072]{1,0:T(8,128)(2,1)}, u32[]{:S(2)}) copy-start(bf16[32,3072]{1,0:T(8,128)(2,1)} %token_ref.1) | copy-start | bytes 589828
  12.0 21.6 %copy-start.7 = (f32[128]{0:T(128)S(1)}, f32[128]{0:T(128)}, u32[]{:S(2)}) copy-start(f32[128]{0:T(128)} %param.11) | copy-start | bytes 1540
  12.0 21.6 %copy-start.8 = (f32[128]{0:T(128)S(1)}, f32[128]{0:T(128)}, u32[]{:S(2)}) copy-start(f32[128]{0:T(128)} %param.12) | copy-start | bytes 1540
  12.3 13.7 %collective-permute-start.1 = (bf16[32,3072]{1,0:T(8,128)(2,1)S(1)}, bf16[32,3072]{1,0:T(8,128)(2,1)S(1)}, u32[]{:S(2)}, u32[]{:S(2)}) collective-permute-start(bf16[32,3072]{1,0:T(8,128)(2,1)S(1)} %shard_map.95.own_ref), channel_id=1, source_target_pairs={{0,2},{2,0},{1,3},{3,1},{4,6},{6,4},{5,7},{7,5},{8,10},{10,8},{9,1... | collective-permute-start | bytes 589832 | tf_op jit(solution)/shard_map/ppermute | solution.py:133
  14.2 19.4 %collective-permute-start = (bf16[32,3072]{1,0:T(8,128)(2,1)S(1)}, bf16[32,3072]{1,0:T(8,128)(2,1)S(1)}, u32[]{:S(2)}, u32[]{:S(2)}) collective-permute-start(bf16[32,3072]{1,0:T(8,128)(2,1)S(1)} %shard_map.95.own_ref), channel_id=1, source_target_pairs={{0,1},{1,0},{2,3},{3,2},{4,5},{5,4},{6,7},{7,6},{8,9},{9,8},{10,11... | collective-permute-start | bytes 589832 | tf_op jit(solution)/shard_map/ppermute | solution.py:133
  26.0 7.7 %collective-permute-start.2 = (bf16[32,3072]{1,0:T(8,128)(2,1)S(1)}, bf16[32,3072]{1,0:T(8,128)(2,1)S(1)}, u32[]{:S(2)}, u32[]{:S(2)}) collective-permute-start(bf16[32,3072]{1,0:T(8,128)(2,1)S(1)} %collective-permute-done.1.across_ref), channel_id=1, source_target_pairs={{0,1},{1,0},{2,3},{3,2},{4,5},{5,4},{6,7},{7,6},{8,9},{9,8},{10,11... | collective-permute-start | bytes 589832 | tf_op jit(solution)/shard_map/ppermute | solution.py:133
  26.0 3.7 %copy-start.1 = (bf16[3072,4,384]{2,1,0:T(4,128)(2,1)S(1)}, bf16[3072,4,384]{2,1,0:T(4,128)(2,1)}, u32[]{:S(2)}) copy-start(bf16[3072,4,384]{2,1,0:T(4,128)(2,1)} %weight_ref.1) | copy-start | bytes 28311556
  33.6 2.1 %copy-start = (bf16[4,128,3072]{2,1,0:T(8,128)(2,1)S(1)}, bf16[4,128,3072]{2,1,0:T(8,128)(2,1)}, u32[]{:S(2)}) copy-start(bf16[4,128,3072]{2,1,0:T(8,128)(2,1)} %param.13) | copy-start | bytes 9437188
  33.6 2.1 %copy-start.6 = (s32[4]{0:T(128)S(1)}, s32[4]{0:T(128)}, u32[]{:S(2)}) copy-start(s32[4]{0:T(128)} %length_ref.3) | copy-start | bytes 52
  35.6 14.5 %copy-start.4 = (f32[3,3072]{1,0:T(4,128)S(1)}, f32[3,3072]{1,0:T(4,128)}, u32[]{:S(2)}) copy-start(f32[3,3072]{1,0:T(4,128)} %modulation_ref.3) | copy-start | bytes 110596
  38.7 4.2 %collective-permute-start.4 = (bf16[32,3072]{1,0:T(8,128)(2,1)S(1)}, bf16[32,3072]{1,0:T(8,128)(2,1)S(1)}, u32[]{:S(2)}, u32[]{:S(2)}) collective-permute-start(bf16[32,3072]{1,0:T(8,128)(2,1)S(1)} %get-tuple-element.17), channel_id=1, source_target_pairs={{0,1},{1,0},{2,3},{3,2},{4,5},{5,4},{6,7},{7,6},{8,9},{9,8},{10,11... | collective-permute-start | bytes 589832 | tf_op jit(solution)/shard_map/ppermute | solution.py:133
  39.3 5.8 %collective-permute-start.7 = (bf16[2,4,32,256]{3,2,1,0:T(8,128)(2,1)S(1)}, bf16[2,4,32,256]{3,2,1,0:T(8,128)(2,1)S(1)}, u32[]{:S(2)}, u32[]{:S(2)}) collective-permute-start(bf16[2,4,32,256]{3,2,1,0:T(8,128)(2,1)S(1)} %get-tuple-element.13.across_ref), channel_id=1, source_target_pairs={{0,2},{2,0},{1,3},{3,1},{4,6},{6,4},{5,7},{7,5},{8,10},{10,8},{9,1... | collective-permute-start | bytes 393224 | tf_op jit(solution)/shard_map/ppermute | solution.py:133
  39.3 5.9 %collective-permute-start.6 = (bf16[4,32,256]{2,1,0:T(8,128)(2,1)S(1)}, bf16[4,32,256]{2,1,0:T(8,128)(2,1)S(1)}, u32[]{:S(2)}, u32[]{:S(2)}) collective-permute-start(bf16[4,32,256]{2,1,0:T(8,128)(2,1)S(1)} %get-tuple-element.12.beside_ref), channel_id=1, source_target_pairs={{0,1},{1,0},{2,3},{3,2},{4,5},{5,4},{6,7},{7,6},{8,9},{9,8},{10,11... | collective-permute-start | bytes 196616 | tf_op jit(solution)/shard_map/ppermute | solution.py:133
  42.5 4.9 %collective-permute-start.3 = (bf16[32,3072]{1,0:T(8,128)(2,1)S(1)}, bf16[32,3072]{1,0:T(8,128)(2,1)S(1)}, u32[]{:S(2)}, u32[]{:S(2)}) collective-permute-start(bf16[32,3072]{1,0:T(8,128)(2,1)S(1)} %get-tuple-element.15), channel_id=1, source_target_pairs={{0,1},{1,0},{2,3},{3,2},{4,5},{5,4},{6,7},{7,6},{8,9},{9,8},{10,11... | collective-permute-start | bytes 589832 | tf_op jit(solution)/shard_map/ppermute | solution.py:133
  43.0 7.2 %collective-permute-start.5 = (bf16[32,3072]{1,0:T(8,128)(2,1)S(1)}, bf16[32,3072]{1,0:T(8,128)(2,1)S(1)}, u32[]{:S(2)}, u32[]{:S(2)}) collective-permute-start(bf16[32,3072]{1,0:T(8,128)(2,1)S(1)} %shard_map.101), channel_id=1, source_target_pairs={{0,2},{2,0},{1,3},{3,1},{4,6},{6,4},{5,7},{7,5},{8,10},{10,8},{9,1... | collective-permute-start | bytes 589832 | tf_op jit(solution)/shard_map/ppermute | solution.py:133
  45.1 1.3 %collective-permute-start.8 = (bf16[4,32,256]{2,1,0:T(8,128)(2,1)S(1)}, bf16[4,32,256]{2,1,0:T(8,128)(2,1)S(1)}, u32[]{:S(2)}, u32[]{:S(2)}) collective-permute-start(bf16[4,32,256]{2,1,0:T(8,128)(2,1)S(1)} %get-tuple-element.18), channel_id=1, source_target_pairs={{0,1},{1,0},{2,3},{3,2},{4,5},{5,4},{6,7},{7,6},{8,9},{9,8},{10,11... | collective-permute-start | bytes 196616 | tf_op jit(solution)/shard_map/ppermute | solution.py:133

commit v3 on v2

--- a/solution.py
+++ b/solution.py
@@ -151,40 +151,71 @@
     )(*inputs)
 
 
-def regroup_kernel(stale_ref, out_ref, wide_ref):
+def own_chunk_index():
+    return lax.axis_index("head") * 2 + lax.axis_index("rep")
+
+
+def enter_kernel(
+    stale_ref, token_ref, modulation_ref, own_ref, beside_ref, across_ref, normed_ref, wide_ref
+):
     rows, heads, both = stale_ref.shape
-    patches, _, per_group = out_ref.shape[:3]
+    per_group = own_ref.shape[0]
+    own_chunk = own_chunk_index()
+    outs = (own_ref, beside_ref, across_ref.at[0], across_ref.at[1])
     for lanes in range(both // 128):
         columns = slice(lanes * 128, (lanes + 1) * 128)
         wide_ref[lanes] = stale_ref[:, :, columns].astype(jnp.float32).reshape(rows * heads, 128)
-        for head in range(heads):
-            values = wide_ref[lanes, pl.ds(head, rows, stride=heads), :].astype(jnp.bfloat16)
-            for patch in range(patches):
-                out_ref[patch, head // per_group, head % per_group, :, columns] = values
-
-
-def relayout_kernel(weight_ref, out_ref, wide_ref):
+        for part, out_ref in enumerate(outs):
+            for head in range(per_group):
+                first = (own_chunk ^ part) * per_group + head
+                values = wide_ref[lanes, pl.ds(first, rows, stride=heads), :]
+                out_ref[head, :, columns] = values.astype(jnp.bfloat16)
+    values = normalize_rows(token_ref[...].astype(jnp.float32))
+    shifted = values * (1.0 + modulation_ref[1:2]) + modulation_ref[0:1]
+    normed_ref[...] = shifted.astype(jnp.bfloat16)
+
+
+def join_own_kernel(own_ref, beside_ref, out_ref):
+    out_ref[0] = own_ref[...]
+    out_ref[1] = beside_ref[...]
+
+
+def join_other_kernel(across_ref, diagonal_ref, out_ref):
+    out_ref[0] = across_ref[0]
+    out_ref[1] = diagonal_ref[1]
+
+
+def join_forward_kernel(other_ref, came_ref, out_ref):
+    out_ref[0:2] = other_ref[...]
+    out_ref[2:4] = came_ref[...]
+
+
+def relayout_kernel(weight_ref, out_ref, raw_ref, wide_ref, semaphores):
     depth, heads, width = weight_ref.shape
+    steps = semaphores.shape[0]
+    size = depth // steps
     block = wide_ref.shape[1] // heads
 
-    def step(index, carry):
+    def fetch(step):
+        rows = pl.ds(pl.multiple_of(step * size, size), size)
+        return pltpu.make_async_copy(weight_ref.at[rows], raw_ref.at[rows], semaphores.at[step])
+
+    for step in range(steps):
+        fetch(step).start()
+
+    def convert(index, carry):
         rows = pl.ds(pl.multiple_of(index * block, block), block)
+        fetch(index).wait()
         for lanes in range(width // 128):
             columns = slice(lanes * 128, (lanes + 1) * 128)
-            values = weight_ref[rows, :, columns].astype(jnp.float32)
+            values = raw_ref[rows, :, columns].astype(jnp.float32)
             wide_ref[lanes] = values.reshape(block * heads, 128)
             for head in range(heads):
                 picked = wide_ref[lanes, pl.ds(head, block, stride=heads), :]
                 out_ref[head, rows, columns] = picked.astype(jnp.bfloat16)
         return carry
 
-    lax.fori_loop(0, depth // block, step, 0)
-
-
-def normalize_kernel(token_ref, modulation_ref, out_ref):
-    values = normalize_rows(token_ref[...].astype(jnp.float32))
-    shifted = values * (1.0 + modulation_ref[1:2]) + modulation_ref[0:1]
-    out_ref[...] = shifted.astype(jnp.bfloat16)
+    lax.fori_loop(0, steps, convert, 0)
 
 
 def project_kernel(
@@ -210,9 +241,11 @@
 def collect_kernel(own_ref, beside_ref, across_ref, diagonal_ref, out_ref, part_ref, wide_ref):
     per_group, rows, both = own_ref.shape
     heads = out_ref.shape[1]
-    own_chunk = lax.axis_index("head") * 2 + lax.axis_index("rep")
-    for part, ref in enumerate((own_ref, beside_ref, across_ref, diagonal_ref)):
-        part_ref[part] = ref[...]
+    own_chunk = own_chunk_index()
+    part_ref[0] = own_ref[...]
+    part_ref[1] = beside_ref[...]
+    part_ref[2] = across_ref[0]
+    part_ref[3] = diagonal_ref[1]
     for lanes in range(both // 128):
         columns = slice(lanes * 128, (lanes + 1) * 128)
         for head in range(heads):
@@ -234,76 +267,90 @@
 
 
 def attend_kernel(
-    first, length_ref, query_ref, own_ref, beside_ref, across_ref, source_ref, weight_ref,
-    kept_ref, sent_ref, keys_ref, attended_ref
+    first, length_ref, query_ref, own_ref, beside_ref, across_ref, one_own_ref, one_other_ref,
+    two_own_ref, two_other_ref, three_other_ref, weight_ref, kept_ref, sent_ref, attended_ref
 ):
     heads, chunk, both = own_ref.shape
     rows = attended_ref.shape[0]
-    parts = 4
     head_dim = both // 2
-    patches = source_ref.shape[0] // parts
-    per_patch = parts * chunk
     scale = 1.0 / math.sqrt(head_dim)
     own_patch = lax.axis_index("patch")
-    own_chunk = lax.axis_index("head") * 2 + lax.axis_index("rep")
-    index = lax.broadcasted_iota(jnp.int32, (rows, patches * per_patch), 1)
-    mask = index < length_ref[0]
-    for patch in range(1, patches):
-        inside = (index >= patch * per_patch) & (index < patch * per_patch + length_ref[patch])
-        mask = mask | inside
-    caches = (own_ref, beside_ref, across_ref.at[0], across_ref.at[1])
-    for head in range(heads):
-        for source in range(patches * parts):
-            keys_ref[head, source * chunk : (source + 1) * chunk] = source_ref[source, head]
-        for part, cache_ref in enumerate(caches):
-            place = own_patch * parts + (own_chunk ^ part)
-            start = pl.multiple_of(place * chunk, chunk)
-            keys_ref[head, pl.ds(start, chunk)] = cache_ref[head]
-    for head in range(heads):
-        scores = lax.dot_general(
+    own_chunk = own_chunk_index()
+    slots = (
+        own_ref, beside_ref, across_ref.at[0], across_ref.at[1],
+        one_own_ref.at[0], one_own_ref.at[1], one_other_ref.at[0], one_other_ref.at[1],
+        two_own_ref.at[0], two_own_ref.at[1], two_other_ref.at[0], two_other_ref.at[1],
+        one_other_ref.at[2], one_other_ref.at[3], three_other_ref.at[0], three_other_ref.at[1],
+    )
+    index = lax.broadcasted_iota(jnp.int32, (1, len(slots) * chunk), 1)
+    end = jnp.zeros_like(index)
+    for slot in range(len(slots)):
+        place = (own_chunk ^ (slot % 4)) * chunk
+        limit = length_ref[own_patch ^ (slot // 4)] - place + slot * chunk
+        end = jnp.where(index >= slot * chunk, limit, end)
+    mask = jnp.broadcast_to(index < end, (rows, len(slots) * chunk))
+    sources = [jnp.concatenate([ref[head] for ref in slots], axis=0) for head in range(heads)]
+    scores = [
+        lax.dot_general(
             query_ref[head, first : first + rows],
-            keys_ref[head, :, :head_dim],
+            sources[head][:, :head_dim],
             (((1,), (1,)), ((), ())),
             preferred_element_type=jnp.float32,
         )
-        scores = jnp.where(mask, scores * scale, NEGATIVE)
-        row_max = jnp.max(scores, axis=1, keepdims=True)
-        weights = jnp.where(mask, jnp.exp(scores - row_max), 0.0)
-        denominator = jnp.sum(weights, axis=1, keepdims=True)
-        summed = jnp.dot(
-            weights.astype(jnp.bfloat16), keys_ref[head, :, head_dim:], preferred_element_type=jnp.float32
+        for head in range(heads)
+    ]
+    scores = [jnp.where(mask, values * scale, NEGATIVE) for values in scores]
+    maxima = [jnp.max(values, axis=1, keepdims=True) for values in scores]
+    weights = [
+        jnp.where(mask, jnp.exp(values - top), 0.0) for values, top in zip(scores, maxima)
+    ]
+    denominators = [jnp.sum(values, axis=1, keepdims=True) for values in weights]
+    summed = [
+        jnp.dot(
+            values.astype(jnp.bfloat16), source[:, head_dim:], preferred_element_type=jnp.float32
         )
-        attended_ref[:, head * head_dim : (head + 1) * head_dim] = (summed / denominator).astype(
-            jnp.bfloat16
-        )
+        for values, source in zip(weights, sources)
+    ]
+    for head in range(heads):
+        attended_ref[:, head * head_dim : (head + 1) * head_dim] = (
+            summed[head] / denominators[head]
+        ).astype(jnp.bfloat16)
     partial = jnp.dot(attended_ref[...], weight_ref[...], preferred_element_type=jnp.float32)
     partial = partial.astype(jnp.bfloat16)
     kept_ref[...] = partial[:chunk].astype(jnp.float32)
     sent_ref[...] = partial[chunk:]
 
 
-def attend_half(half, lengths, queries, caches, sources, out_weight):
-    heads, chunk, both = caches[0].shape
+def attend_half(half, lengths, queries, sources, out_weight):
+    heads, chunk, both = sources[0].shape
     depth, width = out_weight.shape
-    keys = sources.shape[0] * chunk
     rows = 2 * chunk
+    keys = 16 * chunk
     return kernel_call(
         functools.partial(attend_kernel, half * rows),
-        (lengths, queries) + caches + (sources, out_weight),
+        (lengths, queries) + sources + (out_weight,),
         [
             jax.ShapeDtypeStruct((chunk, width), jnp.float32),
             jax.ShapeDtypeStruct((chunk, width), jnp.bfloat16),
         ],
-        [
-            pltpu.VMEM((heads, keys, both), jnp.bfloat16),
-            pltpu.VMEM((rows, depth), jnp.bfloat16),
-        ],
+        [pltpu.VMEM((rows, depth), jnp.bfloat16)],
         12,
         (2 * rows * depth * width + 4 * rows * keys * depth, 2 * (depth * width + keys * heads * both), 0),
         smem_inputs=1,
     )
 
 
+def small_call(body, inputs, shape):
+    size = math.prod(shape)
+    return kernel_call(
+        body, inputs, [jax.ShapeDtypeStruct(shape, jnp.bfloat16)], [], 4, (0, 4 * size, 0)
+    )[0]
+
+
+def hop(values, distance):
+    return lax.ppermute(values, "patch", [(place, place ^ distance) for place in range(4)])
+
+
 def per_device_pair(
     tokens, modulation, in_weight, query_gain, key_gain, out_weight, stale_cache, lengths
 ):
@@ -318,40 +365,53 @@
     rows, width = tokens.shape
     _, heads_dev, triple = in_weight.shape
     head_dim = query_gain.shape[0]
-    patches = lax.axis_size("patch")
     parts = 4
     heads = heads_dev * parts
     both = 2 * head_dim
     half = jnp.bfloat16
 
-    outgoing = kernel_call(
-        regroup_kernel,
-        (stale_cache,),
-        [jax.ShapeDtypeStruct((patches, parts, heads_dev, rows, both), half)],
+    piece = (heads_dev, rows, both)
+    stale_own, stale_beside, stale_across, normed = kernel_call(
+        enter_kernel,
+        (stale_cache, tokens, modulation),
+        [
+            pltpu.VMEM(piece, half),
+            pltpu.VMEM(piece, half),
+            pltpu.VMEM((2,) + piece, half),
+            pltpu.VMEM((rows, width), half),
+        ],
         [pltpu.VMEM((both // 128, rows * heads, 128), jnp.float32)],
-        8,
-        (0, 2 * rows * heads * both * (patches + 1), 0),
-    )[0].reshape(patches * parts, heads_dev, rows, both)
-    sources = lax.all_to_all(
-        outgoing, ("patch", "head", "rep"), split_axis=0, concat_axis=0, tiled=True
-    )
-
-    weight_rows = kernel_call(
+        60,
+        (8 * rows * width, 4 * rows * (heads * both + width), 0),
+    )
+    came_beside = swap(stale_beside, "rep")
+    came_across = swap(stale_across, "head")
+    chip_rows = small_call(join_own_kernel, (stale_own, came_beside), (2,) + piece)
+    two_own = hop(chip_rows, 2)
+    one_own = hop(chip_rows, 1)
+    came_diagonal = swap(came_across, "rep")
+    other_rows = small_call(join_other_kernel, (came_across, came_diagonal), (2,) + piece)
+    two_other = hop(other_rows, 2)
+    forward = small_call(join_forward_kernel, (other_rows, two_own), (4,) + piece)
+    one_other = hop(forward, 1)
+    three_other = hop(two_other, 1)
+
+    weight_rows = pl.pallas_call(
         relayout_kernel,
-        (in_weight,),
-        [jax.ShapeDtypeStruct((heads_dev, width, triple), half)],
-        [pltpu.VMEM((triple // 128, 128 * heads_dev, 128), jnp.float32)],
-        8,
-        (0, 4 * heads_dev * width * triple, 0),
-    )[0]
-    normed = kernel_call(
-        normalize_kernel,
-        (tokens, modulation),
-        [jax.ShapeDtypeStruct((rows, width), half)],
-        [],
-        8,
-        (8 * rows * width, 4 * rows * width, 0),
-    )[0]
+        in_specs=[pl.BlockSpec(memory_space=pltpu.HBM)],
+        out_specs=VMEM,
+        out_shape=jax.ShapeDtypeStruct((heads_dev, width, triple), half),
+        scratch_shapes=[
+            pltpu.VMEM((width, heads_dev, triple), half),
+            pltpu.VMEM((triple // 128, 128 * heads_dev, 128), jnp.float32),
+            pltpu.SemaphoreType.DMA((width // 128,)),
+        ],
+        compiler_params=pltpu.CompilerParams(vmem_limit_bytes=44 * MIB),
+        cost_estimate=pl.CostEstimate(
+            flops=0, bytes_accessed=4 * heads_dev * width * triple, transcendentals=0
+        ),
+        name="relayout",
+    )(in_weight)
     across = swap(normed, "head")
     beside = swap(normed, "rep")
     diagonal = swap(across, "rep")
@@ -368,14 +428,16 @@
         8,
         (2 * parts * rows * width * heads_dev * triple, 2 * width * heads_dev * triple, 0),
     )
-    caches = (own_cache, beside_cache, across_cache)
+    sources = (
+        own_cache, beside_cache, across_cache, one_own, one_other, two_own, two_other, three_other
+    )
 
     from_across = swap(across_cache, "head")
     from_beside = swap(beside_cache, "rep")
-    from_diagonal = swap(from_across[1], "rep")
+    from_diagonal = swap(from_across, "rep")
     new_cache = kernel_call(
         collect_kernel,
-        (own_cache, from_beside, from_across[0], from_diagonal),
+        (own_cache, from_beside, from_across, from_diagonal),
         [jax.ShapeDtypeStruct((rows, heads, both), half)],
         [
             pltpu.VMEM((parts, heads_dev, rows, both), half),
@@ -386,7 +448,7 @@
     )[0]
 
     flat_weight = out_weight.reshape(heads_dev * head_dim, width)
-    far_kept, far_sent = attend_half(1, lengths, queries, caches, sources, flat_weight)
+    far_kept, far_sent = attend_half(1, lengths, queries, sources, flat_weight)
     far_received = swap(far_sent, "rep")
     far_sum = kernel_call(
         add_kernel,
@@ -397,7 +459,7 @@
         (rows * width, 8 * rows * width, 0),
     )[0]
     received = swap(far_sum, "head")
-    near_kept, near_sent = attend_half(0, lengths, queries, caches, sources, flat_weight)
+    near_kept, near_sent = attend_half(0, lengths, queries, sources, flat_weight)
     near_received = swap(near_sent, "rep")
     update = kernel_call(
         finish_kernel,
@@ -411,7 +473,7 @@
 
 
 def solution(mesh):
-    paired = mesh.shape["head"] == 2 and mesh.shape["rep"] == 2
+    paired = (mesh.shape["patch"], mesh.shape["head"], mesh.shape["rep"]) == (4, 2, 2)
     return jax.shard_map(
         per_device_pair if paired else per_device,
         mesh=mesh,

time: 51.3 us -> 50.1 us (0.977)
  local copies, waits for them, and re-layouts: 6.38 us -> 0.03 us
  waiting for transfers between devices: 15.7 us -> 20.4 us
  starting transfers between devices: 12.7 us -> 15.1 us
  Pallas kernels: 15.3 us -> 13.6 us
    ppermute x0 -> x5, waiting for transfers between devices: none -> 10.9 us  [hop(): lax.ppermute(values, 'patch', [(place, place ^ distance) for place in ran...]
    ppermute x0 -> x5, starting transfers between devices: none -> 8.54 us  [hop(): lax.ppermute(values, 'patch', [(place, place ^ distance) for place in ran...]
    all_to_all x1 -> x0, starting transfers between devices: 7.44 us -> none  [paired_block(): lax.all_to_all(outgoing, ('patch', 'head', 'rep'), split_axis=0, concat_a...]
    pallas_call x9 -> x10, Pallas kernels: 15.3 us -> 8.61 us  [kernel_call(): pl.pallas_call(body, in_specs=[SMEM] * smem_inputs + [VMEM] * (count - sm...]
    unnamed x18 -> x10, local copies, waits for them, and re-layouts: 6.37 us -> 0.03 us
    ppermute x9 -> x12, waiting for transfers between devices: 15.7 us -> 9.47 us  [swap(): return lax.ppermute(values, axis, [(0, 1), (1, 0)])]
    pallas_call x0 -> x1, Pallas kernels: none -> 4.98 us  [paired_block(): pl.pallas_call(relayout_kernel, in_specs=[pl.BlockSpec(memory_space=pltpu...]
    ppermute x9 -> x12, starting transfers between devices: 5.25 us -> 6.58 us  [swap(): return lax.ppermute(values, axis, [(0, 1), (1, 0)])]
  transfers between devices with their start and end apart: 10 -> 17, of which waited for: 3 -> 8; matrix products, arithmetic and copies ran while one was open for 0% -> 0% of each run, Pallas kernels for 20% -> 19%
where the time goes in v3:
time: 50.1 us; the launch traced here: 49.9 us
  waiting for transfers between devices  20.4 us (41%)
  starting transfers between devices  15.1 us (30%)
  Pallas kernels  13.6 us (27%)
  between operations  0.76 us (2%)
    ppermute x5, waiting for transfers between devices, hop(): lax.ppermute(values, 'patch', [(place, place ^ distance) for place in ran...  10.9 us
    ppermute x12, waiting for transfers between devices, swap(): return lax.ppermute(values, axis, [(0, 1), (1, 0)])  9.47 us
    pallas_call x10, Pallas kernels, kernel_call(): pl.pallas_call(body, in_specs=[SMEM] * smem_inputs + [VMEM] * (count - sm...  8.61 us
    ppermute x5, starting transfers between devices, hop(): lax.ppermute(values, 'patch', [(place, place ^ distance) for place in ran...  8.54 us
    ppermute x12, starting transfers between devices, swap(): return lax.ppermute(values, axis, [(0, 1), (1, 0)])  6.58 us
    pallas_call x1, Pallas kernels, paired_block(): pl.pallas_call(relayout_kernel, in_specs=[pl.BlockSpec(memory_space=pltpu...  4.98 us
  transfers between devices with their start and end apart: 17, of which 8 were waited for; matrix products, arithmetic and copies ran while one was open for 0% of the time, Pallas kernels for 19%

profile of v3, /device:TPU:0, one launch (start us, length us, event | category | flops | bytes accessed | tf_op | source)
XLA Modules:
  0.0 49.9 jit_solution(9142608027033569825)
XLA Ops:
  0.6 1.5 %shard_map.95 = (bf16[4,32,256]{2,1,0:T(8,128)(2,1)S(1)}, bf16[4,32,256]{2,1,0:T(8,128)(2,1)S(1)}, bf16[2,4,32,256]{3,2,1,0:T(8,128)(2,1)S(1)}, bf16[32,3072]{1,0:T(8,128)(2,1)S(1)}) custom-call(bf16[32,16,256]{2,1,0:T(8,128)(2,1)} %stale_ref.1, bf16[32,3072]{1,0:T(8,128)(2,1)} %token_ref.1, f32[3,3072]{1,0:T(4,128)} %modulation_ref.3), custom_call_target="tpu_custom_call" | custom-call | flops 786432 | bytes 917504 | tf_op jit(solution)/shard_map/pallas_call | solution.py:143
  2.2 3.0 %collective-permute-start.5 = (bf16[2,4,32,256]{3,2,1,0:T(8,128)(2,1)S(1)}, bf16[2,4,32,256]{3,2,1,0:T(8,128)(2,1)S(1)}, u32[]{:S(2)}, u32[]{:S(2)}) collective-permute-start(bf16[2,4,32,256]{3,2,1,0:T(8,128)(2,1)S(1)} %get-tuple-element.21), channel_id=1, source_target_pairs={{0,2},{2,0},{1,3},{3,1},{4,6},{6,4},{5,7},{7,5},{8,10},{10,8},{9,1... | collective-permute-start | bytes 393224 | tf_op jit(solution)/shard_map/ppermute | solution.py:133
  5.2 0.1 collective-permute-start.1
  5.3 0.0 collective-permute-start.3
  5.3 4.3 %collective-permute-done.5.across_ref = bf16[2,4,32,256]{3,2,1,0:T(8,128)(2,1)S(1)} collective-permute-done((bf16[2,4,32,256]{3,2,1,0:T(8,128)(2,1)S(1)}, bf16[2,4,32,256]{3,2,1,0:T(8,128)(2,1)S(1)}, u32[]{:S(2)}, u32[]{:S(2)}) %collective-permute-start.5) | collective-permute-done | bytes 131104 | tf_op jit(solution)/shard_map/ppermute | solution.py:133
  9.5 0.0 collective-permute-start.6
  9.5 0.0 collective-permute-done.3.beside_ref
  9.6 3.2 %collective-permute-start.7 = (bf16[2,4,32,256]{3,2,1,0:T(8,128)(2,1)S(1)}, bf16[2,4,32,256]{3,2,1,0:T(8,128)(2,1)S(1)}, u32[]{:S(2)}, u32[]{:S(2)}) collective-permute-start(bf16[2,4,32,256]{3,2,1,0:T(8,128)(2,1)S(1)} %shard_map.97), channel_id=1, source_target_pairs={{0,8},{4,12},{8,0},{12,4},{1,9},{5,13},{9,1},{13,5},{2,10},{6,14},... | collective-permute-start | bytes 393224 | tf_op jit(solution)/shard_map/ppermute | solution.py:351
  12.7 0.2 collective-permute-start
  13.0 0.0 collective-permute-done.1.across_ref
  13.0 0.3 collective-permute-start.2
  13.3 0.0 collective-permute-done.6.diagonal_ref
  13.3 2.5 %collective-permute-start.9 = (bf16[2,4,32,256]{3,2,1,0:T(8,128)(2,1)S(1)}, bf16[2,4,32,256]{3,2,1,0:T(8,128)(2,1)S(1)}, u32[]{:S(2)}, u32[]{:S(2)}) collective-permute-start(bf16[2,4,32,256]{3,2,1,0:T(8,128)(2,1)S(1)} %shard_map.98.other_ref), channel_id=1, source_target_pairs={{0,8},{4,12},{8,0},{12,4},{1,9},{5,13},{9,1},{13,5},{2,10},{6,14},... | collective-permute-start | bytes 393224 | tf_op jit(solution)/shard_map/ppermute | solution.py:351
  15.8 6.9 %collective-permute-done.7.came_ref.two_own_ref = bf16[2,4,32,256]{3,2,1,0:T(8,128)(2,1)S(1)} collective-permute-done((bf16[2,4,32,256]{3,2,1,0:T(8,128)(2,1)S(1)}, bf16[2,4,32,256]{3,2,1,0:T(8,128)(2,1)S(1)}, u32[]{:S(2)}, u32[]{:S(2)}) %collective-permute-start.7) | collective-permute-done | bytes 131104 | tf_op jit(solution)/shard_map/ppermute | solution.py:351
  22.7 0.0 copy-start.3
  22.7 0.0 copy-start.4
  22.8 0.6 %collective-permute-start.8 = (bf16[4,4,32,256]{3,2,1,0:T(8,128)(2,1)S(1)}, bf16[4,4,32,256]{3,2,1,0:T(8,128)(2,1)S(1)}, u32[]{:S(2)}, u32[]{:S(2)}) collective-permute-start(bf16[4,4,32,256]{3,2,1,0:T(8,128)(2,1)S(1)} %shard_map.99), channel_id=1, source_target_pairs={{0,4},{4,0},{8,12},{12,8},{1,5},{5,1},{9,13},{13,9},{2,6},{6,2},{1... | collective-permute-start | bytes 786440 | tf_op jit(solution)/shard_map/ppermute | solution.py:351
  23.4 1.4 %collective-permute-start.4 = (bf16[2,4,32,256]{3,2,1,0:T(8,128)(2,1)S(1)}, bf16[2,4,32,256]{3,2,1,0:T(8,128)(2,1)S(1)}, u32[]{:S(2)}, u32[]{:S(2)}) collective-permute-start(bf16[2,4,32,256]{3,2,1,0:T(8,128)(2,1)S(1)} %shard_map.97), channel_id=1, source_target_pairs={{0,4},{4,0},{8,12},{12,8},{1,5},{5,1},{9,13},{13,9},{2,6},{6,2},{1... | collective-permute-start | bytes 393224 | tf_op jit(solution)/shard_map/ppermute | solution.py:351
  24.9 0.5 %collective-permute-done.9.two_other_ref = bf16[2,4,32,256]{3,2,1,0:T(8,128)(2,1)S(1)} collective-permute-done((bf16[2,4,32,256]{3,2,1,0:T(8,128)(2,1)S(1)}, bf16[2,4,32,256]{3,2,1,0:T(8,128)(2,1)S(1)}, u32[]{:S(2)}, u32[]{:S(2)}) %collective-permute-start.9) | collective-permute-done | bytes 131104 | tf_op jit(solution)/shard_map/ppermute | solution.py:351
  25.4 0.7 %collective-permute-start.10 = (bf16[2,4,32,256]{3,2,1,0:T(8,128)(2,1)S(1)}, bf16[2,4,32,256]{3,2,1,0:T(8,128)(2,1)S(1)}, u32[]{:S(2)}, u32[]{:S(2)}) collective-permute-start(bf16[2,4,32,256]{3,2,1,0:T(8,128)(2,1)S(1)} %collective-permute-done.9.two_other_ref), channel_id=1, source_target_pairs={{0,4},{4,0},{8,12},{12,8},{1,5},{5,1},{9,13},{13,9},{2,6},{6,2},{1... | collective-permute-start | bytes 393224 | tf_op jit(solution)/shard_map/ppermute | solution.py:351
  26.1 5.0 %relayout.1.weight_ref = bf16[4,3072,384]{2,1,0:T(8,128)(2,1)S(1)} custom-call(bf16[3072,4,384]{2,1,0:T(4,128)(2,1)} %weight_ref.1), custom_call_target="tpu_custom_call" | custom-call | bytes 18874368 | tf_op jit(solution)/shard_map/relayout/pallas_call | solution.py:399
  31.1 0.0 copy-start
  31.1 0.0 copy-start.2
  31.1 0.0 collective-permute-done.beside_ref
  31.1 0.0 collective-permute-done.2.diagonal_ref
  31.1 0.0 copy-done.3
  31.1 0.0 copy-done.4
  31.1 0.0 copy-start.1
  31.2 1.9 %shard_map.96 = (bf16[4,128,128]{2,1,0:T(8,128)(2,1)S(1)}, bf16[4,32,256]{2,1,0:T(8,128)(2,1)S(1)}, bf16[4,32,256]{2,1,0:T(8,128)(2,1)S(1)}, bf16[2,4,32,256]{3,2,1,0:T(8,128)(2,1)S(1)}) custom-call(bf16[32,3072]{1,0:T(8,128)(2,1)S(1)} %get-tuple-element.14.own_ref, bf16[32,3072]{1,0:T(8,128)(2,1)S(1)} %collective-permute-done.beside_ref, ...), custom_call_target="tpu_custom_call" | custom-call | flops 1207959552 | bytes 9437184 | tf_op jit(solution)/shard_map/pallas_call | solution.py:143
  33.0 1.8 %collective-permute-done.4.one_own_ref = bf16[2,4,32,256]{3,2,1,0:T(8,128)(2,1)S(1)} collective-permute-done((bf16[2,4,32,256]{3,2,1,0:T(8,128)(2,1)S(1)}, bf16[2,4,32,256]{3,2,1,0:T(8,128)(2,1)S(1)}, u32[]{:S(2)}, u32[]{:S(2)}) %collective-permute-start.4) | collective-permute-done | bytes 131104 | tf_op jit(solution)/shard_map/ppermute | solution.py:351
  34.8 0.0 collective-permute-done.8.one_other_ref
  34.8 1.8 %collective-permute-done.10.three_other_ref = bf16[2,4,32,256]{3,2,1,0:T(8,128)(2,1)S(1)} collective-permute-done((bf16[2,4,32,256]{3,2,1,0:T(8,128)(2,1)S(1)}, bf16[2,4,32,256]{3,2,1,0:T(8,128)(2,1)S(1)}, u32[]{:S(2)}, u32[]{:S(2)}) %collective-permute-start.10) | collective-permute-done | bytes 131104 | tf_op jit(solution)/shard_map/ppermute | solution.py:351
  36.6 0.0 copy-done
  36.6 0.0 copy-done.2
  36.6 1.7 %shard_map.101 = (f32[32,3072]{1,0:T(8,128)S(1)}, bf16[32,3072]{1,0:T(8,128)(2,1)S(1)}) custom-call(s32[4]{0:T(128)S(1)} %copy-done.2, bf16[4,128,128]{2,1,0:T(8,128)(2,1)S(1)} %get-tuple-element.15.query_ref, bf16[4,32,256]{2,1,0:T(8,128)(2,1)S(1)} %get-tuple-element.16.own_ref, bf16[4,32,256]{2,1,0:T(8,128)(2,1)S(1)} %get-tuple-element.17.beside_ref, ...), custom_call_target="tpu_custom_call" | custom-call | flops 268435456 | bytes 4194304 | tf_op jit(solution)/shard_map/pallas_call | solution.py:143
  38.3 0.1 collective-permute-start.12
  38.3 1.6 %collective-permute-start.15 = (bf16[2,4,32,256]{3,2,1,0:T(8,128)(2,1)S(1)}, bf16[2,4,32,256]{3,2,1,0:T(8,128)(2,1)S(1)}, u32[]{:S(2)}, u32[]{:S(2)}) collective-permute-start(bf16[2,4,32,256]{3,2,1,0:T(8,128)(2,1)S(1)} %get-tuple-element.18.across_ref), channel_id=1, source_target_pairs={{0,2},{2,0},{1,3},{3,1},{4,6},{6,4},{5,7},{7,5},{8,10},{10,8},{9,1... | collective-permute-start | bytes 393224 | tf_op jit(solution)/shard_map/ppermute | solution.py:133
  40.0 1.7 %shard_map.100 = (f32[32,3072]{1,0:T(8,128)S(1)}, bf16[32,3072]{1,0:T(8,128)(2,1)S(1)}) custom-call(s32[4]{0:T(128)S(1)} %copy-done.2, bf16[4,128,128]{2,1,0:T(8,128)(2,1)S(1)} %get-tuple-element.15.query_ref, bf16[4,32,256]{2,1,0:T(8,128)(2,1)S(1)} %get-tuple-element.16.own_ref, bf16[4,32,256]{2,1,0:T(8,128)(2,1)S(1)} %get-tuple-element.17.beside_ref, ...), custom_call_target="tpu_custom_call" | custom-call | flops 268435456 | bytes 4194304 | tf_op jit(solution)/shard_map/pallas_call | solution.py:143
  41.6 0.2 collective-permute-start.11
  41.9 0.0 collective-permute-done.12.received_ref
  41.9 0.6 %collective-permute-start.13 = (bf16[32,3072]{1,0:T(8,128)(2,1)S(1)}, bf16[32,3072]{1,0:T(8,128)(2,1)S(1)}, u32[]{:S(2)}, u32[]{:S(2)}) collective-permute-start(bf16[32,3072]{1,0:T(8,128)(2,1)S(1)} %shard_map.102), channel_id=1, source_target_pairs={{0,2},{2,0},{1,3},{3,1},{4,6},{6,4},{5,7},{7,5},{8,10},{10,8},{9,1... | collective-permute-start | bytes 589832 | tf_op jit(solution)/shard_map/ppermute | solution.py:133
  42.5 1.8 %collective-permute-done.15.across_ref = bf16[2,4,32,256]{3,2,1,0:T(8,128)(2,1)S(1)} collective-permute-done((bf16[2,4,32,256]{3,2,1,0:T(8,128)(2,1)S(1)}, bf16[2,4,32,256]{3,2,1,0:T(8,128)(2,1)S(1)}, u32[]{:S(2)}, u32[]{:S(2)}) %collective-permute-start.15) | collective-permute-done | bytes 131104 | tf_op jit(solution)/shard_map/ppermute | solution.py:133
  44.2 0.0 collective-permute-start.16
  44.2 0.5 %collective-permute-start.14 = (bf16[4,32,256]{2,1,0:T(8,128)(2,1)S(1)}, bf16[4,32,256]{2,1,0:T(8,128)(2,1)S(1)}, u32[]{:S(2)}, u32[]{:S(2)}) collective-permute-start(bf16[4,32,256]{2,1,0:T(8,128)(2,1)S(1)} %get-tuple-element.17.beside_ref), channel_id=1, source_target_pairs={{0,1},{1,0},{2,3},{3,2},{4,5},{5,4},{6,7},{7,6},{8,9},{9,8},{10,11... | collective-permute-start | bytes 196616 | tf_op jit(solution)/shard_map/ppermute | solution.py:133
  44.8 0.9 %collective-permute-done.14.beside_ref = bf16[4,32,256]{2,1,0:T(8,128)(2,1)S(1)} collective-permute-done((bf16[4,32,256]{2,1,0:T(8,128)(2,1)S(1)}, bf16[4,32,256]{2,1,0:T(8,128)(2,1)S(1)}, u32[]{:S(2)}, u32[]{:S(2)}) %collective-permute-start.14) | collective-permute-done | bytes 65568 | tf_op jit(solution)/shard_map/ppermute | solution.py:133
  45.7 0.0 collective-permute-done.16.diagonal_ref
  45.7 1.0 %shard_map.104 = bf16[32,16,256]{2,1,0:T(8,128)(2,1)} custom-call(bf16[4,32,256]{2,1,0:T(8,128)(2,1)S(1)} %get-tuple-element.16.own_ref, bf16[4,32,256]{2,1,0:T(8,128)(2,1)S(1)} %collective-permute-done.14.beside_ref, bf16[2,4,32,256]{3,2,1,0:T(8,128)(2,1)S(1)} %collective-permute-done.15.across_ref, ...), custom_call_target="tpu_custom_call" | custom-call | bytes 524288 | tf_op jit(solution)/shard_map/pallas_call | solution.py:143
  46.7 0.0 collective-permute-done.11.beside_ref
  46.7 2.5 %collective-permute-done.13.across_ref = bf16[32,3072]{1,0:T(8,128)(2,1)S(1)} collective-permute-done((bf16[32,3072]{1,0:T(8,128)(2,1)S(1)}, bf16[32,3072]{1,0:T(8,128)(2,1)S(1)}, u32[]{:S(2)}, u32[]{:S(2)}) %collective-permute-start.13) | collective-permute-done | bytes 196640 | tf_op jit(solution)/shard_map/ppermute | solution.py:133
  49.1 0.0 copy-done.1
  49.1 0.8 %shard_map.103 = bf16[32,3072]{1,0:T(8,128)(2,1)} custom-call(f32[32,3072]{1,0:T(8,128)S(1)} %get-tuple-element.22.kept_ref, bf16[32,3072]{1,0:T(8,128)(2,1)S(1)} %collective-permute-done.11.beside_ref, bf16[32,3072]{1,0:T(8,128)(2,1)S(1)} %collective-permute-done.13.across_ref, f32[3,3072]{1,0:T(4,128)S(1)} %copy-done.1), custom_call_target="tpu_custom_call" | custom-call | flops 294912 | bytes 983040 | tf_op jit(solution)/shard_map/pallas_call | solution.py:143
  (4 shorter events, 0.1 us)
Async XLA Ops:
  2.2 7.4 %collective-permute-start.5 = (bf16[2,4,32,256]{3,2,1,0:T(8,128)(2,1)S(1)}, bf16[2,4,32,256]{3,2,1,0:T(8,128)(2,1)S(1)}, u32[]{:S(2)}, u32[]{:S(2)}) collective-permute-start(bf16[2,4,32,256]{3,2,1,0:T(8,128)(2,1)S(1)} %get-tuple-element.21), channel_id=1, source_target_pairs={{0,2},{2,0},{1,3},{3,1},{4,6},{6,4},{5,7},{7,5},{8,10},{10,8},{9,1... | collective-permute-start | bytes 393224 | tf_op jit(solution)/shard_map/ppermute | solution.py:133
  5.2 7.8 %collective-permute-start.1 = (bf16[32,3072]{1,0:T(8,128)(2,1)S(1)}, bf16[32,3072]{1,0:T(8,128)(2,1)S(1)}, u32[]{:S(2)}, u32[]{:S(2)}) collective-permute-start(bf16[32,3072]{1,0:T(8,128)(2,1)S(1)} %get-tuple-element.14.own_ref), channel_id=1, source_target_pairs={{0,2},{2,0},{1,3},{3,1},{4,6},{6,4},{5,7},{7,5},{8,10},{10,8},{9,1... | collective-permute-start | bytes 589832 | tf_op jit(solution)/shard_map/ppermute | solution.py:133
  5.3 4.3 %collective-permute-start.3 = (bf16[4,32,256]{2,1,0:T(8,128)(2,1)S(1)}, bf16[4,32,256]{2,1,0:T(8,128)(2,1)S(1)}, u32[]{:S(2)}, u32[]{:S(2)}) collective-permute-start(bf16[4,32,256]{2,1,0:T(8,128)(2,1)S(1)} %get-tuple-element.20), channel_id=1, source_target_pairs={{0,1},{1,0},{2,3},{3,2},{4,5},{5,4},{6,7},{7,6},{8,9},{9,8},{10,11... | collective-permute-start | bytes 196616 | tf_op jit(solution)/shard_map/ppermute | solution.py:133
  9.5 3.7 %collective-permute-start.6 = (bf16[2,4,32,256]{3,2,1,0:T(8,128)(2,1)S(1)}, bf16[2,4,32,256]{3,2,1,0:T(8,128)(2,1)S(1)}, u32[]{:S(2)}, u32[]{:S(2)}) collective-permute-start(bf16[2,4,32,256]{3,2,1,0:T(8,128)(2,1)S(1)} %collective-permute-done.5.across_ref), channel_id=1, source_target_pairs={{0,1},{1,0},{2,3},{3,2},{4,5},{5,4},{6,7},{7,6},{8,9},{9,8},{10,11... | collective-permute-start | bytes 393224 | tf_op jit(solution)/shard_map/ppermute | solution.py:133
  9.6 13.2 %collective-permute-start.7 = (bf16[2,4,32,256]{3,2,1,0:T(8,128)(2,1)S(1)}, bf16[2,4,32,256]{3,2,1,0:T(8,128)(2,1)S(1)}, u32[]{:S(2)}, u32[]{:S(2)}) collective-permute-start(bf16[2,4,32,256]{3,2,1,0:T(8,128)(2,1)S(1)} %shard_map.97), channel_id=1, source_target_pairs={{0,8},{4,12},{8,0},{12,4},{1,9},{5,13},{9,1},{13,5},{2,10},{6,14},... | collective-permute-start | bytes 393224 | tf_op jit(solution)/shard_map/ppermute | solution.py:351
  12.7 18.4 %collective-permute-start = (bf16[32,3072]{1,0:T(8,128)(2,1)S(1)}, bf16[32,3072]{1,0:T(8,128)(2,1)S(1)}, u32[]{:S(2)}, u32[]{:S(2)}) collective-permute-start(bf16[32,3072]{1,0:T(8,128)(2,1)S(1)} %get-tuple-element.14.own_ref), channel_id=1, source_target_pairs={{0,1},{1,0},{2,3},{3,2},{4,5},{5,4},{6,7},{7,6},{8,9},{9,8},{10,11... | collective-permute-start | bytes 589832 | tf_op jit(solution)/shard_map/ppermute | solution.py:133
  13.0 18.1 %collective-permute-start.2 = (bf16[32,3072]{1,0:T(8,128)(2,1)S(1)}, bf16[32,3072]{1,0:T(8,128)(2,1)S(1)}, u32[]{:S(2)}, u32[]{:S(2)}) collective-permute-start(bf16[32,3072]{1,0:T(8,128)(2,1)S(1)} %collective-permute-done.1.across_ref), channel_id=1, source_target_pairs={{0,1},{1,0},{2,3},{3,2},{4,5},{5,4},{6,7},{7,6},{8,9},{9,8},{10,11... | collective-permute-start | bytes 589832 | tf_op jit(solution)/shard_map/ppermute | solution.py:133
  13.3 12.1 %collective-permute-start.9 = (bf16[2,4,32,256]{3,2,1,0:T(8,128)(2,1)S(1)}, bf16[2,4,32,256]{3,2,1,0:T(8,128)(2,1)S(1)}, u32[]{:S(2)}, u32[]{:S(2)}) collective-permute-start(bf16[2,4,32,256]{3,2,1,0:T(8,128)(2,1)S(1)} %shard_map.98.other_ref), channel_id=1, source_target_pairs={{0,8},{4,12},{8,0},{12,4},{1,9},{5,13},{9,1},{13,5},{2,10},{6,14},... | collective-permute-start | bytes 393224 | tf_op jit(solution)/shard_map/ppermute | solution.py:351
  22.7 8.4 %copy-start.3 = (f32[128]{0:T(128)S(1)}, f32[128]{0:T(128)}, u32[]{:S(2)}) copy-start(f32[128]{0:T(128)} %param.11) | copy-start | bytes 1540
  22.7 8.4 %copy-start.4 = (f32[128]{0:T(128)S(1)}, f32[128]{0:T(128)}, u32[]{:S(2)}) copy-start(f32[128]{0:T(128)} %param.12) | copy-start | bytes 1540
  22.8 12.1 %collective-permute-start.8 = (bf16[4,4,32,256]{3,2,1,0:T(8,128)(2,1)S(1)}, bf16[4,4,32,256]{3,2,1,0:T(8,128)(2,1)S(1)}, u32[]{:S(2)}, u32[]{:S(2)}) collective-permute-start(bf16[4,4,32,256]{3,2,1,0:T(8,128)(2,1)S(1)} %shard_map.99), channel_id=1, source_target_pairs={{0,4},{4,0},{8,12},{12,8},{1,5},{5,1},{9,13},{13,9},{2,6},{6,2},{1... | collective-permute-start | bytes 786440 | tf_op jit(solution)/shard_map/ppermute | solution.py:351
  23.4 11.4 %collective-permute-start.4 = (bf16[2,4,32,256]{3,2,1,0:T(8,128)(2,1)S(1)}, bf16[2,4,32,256]{3,2,1,0:T(8,128)(2,1)S(1)}, u32[]{:S(2)}, u32[]{:S(2)}) collective-permute-start(bf16[2,4,32,256]{3,2,1,0:T(8,128)(2,1)S(1)} %shard_map.97), channel_id=1, source_target_pairs={{0,4},{4,0},{8,12},{12,8},{1,5},{5,1},{9,13},{13,9},{2,6},{6,2},{1... | collective-permute-start | bytes 393224 | tf_op jit(solution)/shard_map/ppermute | solution.py:351
  25.4 11.2 %collective-permute-start.10 = (bf16[2,4,32,256]{3,2,1,0:T(8,128)(2,1)S(1)}, bf16[2,4,32,256]{3,2,1,0:T(8,128)(2,1)S(1)}, u32[]{:S(2)}, u32[]{:S(2)}) collective-permute-start(bf16[2,4,32,256]{3,2,1,0:T(8,128)(2,1)S(1)} %collective-permute-done.9.two_other_ref), channel_id=1, source_target_pairs={{0,4},{4,0},{8,12},{12,8},{1,5},{5,1},{9,13},{13,9},{2,6},{6,2},{1... | collective-permute-start | bytes 393224 | tf_op jit(solution)/shard_map/ppermute | solution.py:351
  31.1 5.5 %copy-start = (bf16[4,128,3072]{2,1,0:T(8,128)(2,1)S(1)}, bf16[4,128,3072]{2,1,0:T(8,128)(2,1)}, u32[]{:S(2)}) copy-start(bf16[4,128,3072]{2,1,0:T(8,128)(2,1)} %param.13) | copy-start | bytes 9437188
  31.1 5.5 %copy-start.2 = (s32[4]{0:T(128)S(1)}, s32[4]{0:T(128)}, u32[]{:S(2)}) copy-start(s32[4]{0:T(128)} %length_ref.3) | copy-start | bytes 52
  31.1 18.0 %copy-start.1 = (f32[3,3072]{1,0:T(4,128)S(1)}, f32[3,3072]{1,0:T(4,128)}, u32[]{:S(2)}) copy-start(f32[3,3072]{1,0:T(4,128)} %modulation_ref.3) | copy-start | bytes 110596
  38.3 3.6 %collective-permute-start.12 = (bf16[32,3072]{1,0:T(8,128)(2,1)S(1)}, bf16[32,3072]{1,0:T(8,128)(2,1)S(1)}, u32[]{:S(2)}, u32[]{:S(2)}) collective-permute-start(bf16[32,3072]{1,0:T(8,128)(2,1)S(1)} %get-tuple-element.25), channel_id=1, source_target_pairs={{0,1},{1,0},{2,3},{3,2},{4,5},{5,4},{6,7},{7,6},{8,9},{9,8},{10,11... | collective-permute-start | bytes 589832 | tf_op jit(solution)/shard_map/ppermute | solution.py:133
  38.3 5.9 %collective-permute-start.15 = (bf16[2,4,32,256]{3,2,1,0:T(8,128)(2,1)S(1)}, bf16[2,4,32,256]{3,2,1,0:T(8,128)(2,1)S(1)}, u32[]{:S(2)}, u32[]{:S(2)}) collective-permute-start(bf16[2,4,32,256]{3,2,1,0:T(8,128)(2,1)S(1)} %get-tuple-element.18.across_ref), channel_id=1, source_target_pairs={{0,2},{2,0},{1,3},{3,1},{4,6},{6,4},{5,7},{7,5},{8,10},{10,8},{9,1... | collective-permute-start | bytes 393224 | tf_op jit(solution)/shard_map/ppermute | solution.py:133
  41.6 5.0 %collective-permute-start.11 = (bf16[32,3072]{1,0:T(8,128)(2,1)S(1)}, bf16[32,3072]{1,0:T(8,128)(2,1)S(1)}, u32[]{:S(2)}, u32[]{:S(2)}) collective-permute-start(bf16[32,3072]{1,0:T(8,128)(2,1)S(1)} %get-tuple-element.23), channel_id=1, source_target_pairs={{0,1},{1,0},{2,3},{3,2},{4,5},{5,4},{6,7},{7,6},{8,9},{9,8},{10,11... | collective-permute-start | bytes 589832 | tf_op jit(solution)/shard_map/ppermute | solution.py:133
  41.9 7.2 %collective-permute-start.13 = (bf16[32,3072]{1,0:T(8,128)(2,1)S(1)}, bf16[32,3072]{1,0:T(8,128)(2,1)S(1)}, u32[]{:S(2)}, u32[]{:S(2)}) collective-permute-start(bf16[32,3072]{1,0:T(8,128)(2,1)S(1)} %shard_map.102), channel_id=1, source_target_pairs={{0,2},{2,0},{1,3},{3,1},{4,6},{6,4},{5,7},{7,5},{8,10},{10,8},{9,1... | collective-permute-start | bytes 589832 | tf_op jit(solution)/shard_map/ppermute | solution.py:133
  44.2 1.4 %collective-permute-start.16 = (bf16[2,4,32,256]{3,2,1,0:T(8,128)(2,1)S(1)}, bf16[2,4,32,256]{3,2,1,0:T(8,128)(2,1)S(1)}, u32[]{:S(2)}, u32[]{:S(2)}) collective-permute-start(bf16[2,4,32,256]{3,2,1,0:T(8,128)(2,1)S(1)} %collective-permute-done.15.across_ref), channel_id=1, source_target_pairs={{0,1},{1,0},{2,3},{3,2},{4,5},{5,4},{6,7},{7,6},{8,9},{9,8},{10,11... | collective-permute-start | bytes 393224 | tf_op jit(solution)/shard_map/ppermute | solution.py:133
  44.2 1.4 %collective-permute-start.14 = (bf16[4,32,256]{2,1,0:T(8,128)(2,1)S(1)}, bf16[4,32,256]{2,1,0:T(8,128)(2,1)S(1)}, u32[]{:S(2)}, u32[]{:S(2)}) collective-permute-start(bf16[4,32,256]{2,1,0:T(8,128)(2,1)S(1)} %get-tuple-element.17.beside_ref), channel_id=1, source_target_pairs={{0,1},{1,0},{2,3},{3,2},{4,5},{5,4},{6,7},{7,6},{8,9},{9,8},{10,11... | collective-permute-start | bytes 196616 | tf_op jit(solution)/shard_map/ppermute | solution.py:133

commit v4 on v3

--- a/solution.py
+++ b/solution.py
@@ -266,77 +266,139 @@
     out_ref[...] = (modulation_ref[2:3] * total).astype(jnp.bfloat16)
 
 
-def attend_kernel(
-    first, length_ref, query_ref, own_ref, beside_ref, across_ref, one_own_ref, one_other_ref,
-    two_own_ref, two_other_ref, three_other_ref, weight_ref, kept_ref, sent_ref, attended_ref
-):
-    heads, chunk, both = own_ref.shape
-    rows = attended_ref.shape[0]
-    head_dim = both // 2
-    scale = 1.0 / math.sqrt(head_dim)
+def key_mask(length_ref, slots, chunk):
     own_patch = lax.axis_index("patch")
     own_chunk = own_chunk_index()
-    slots = (
+    index = lax.broadcasted_iota(jnp.int32, (1, len(slots) * chunk), 1)
+    end = jnp.zeros_like(index)
+    for slot, (distance, part) in enumerate(slots):
+        limit = length_ref[own_patch ^ distance] + (slot - (own_chunk ^ part)) * chunk
+        end = jnp.where(index >= slot * chunk, limit, end)
+    return index < end
+
+
+def masked_scores(queries, keys, mask):
+    scores = lax.dot_general(
+        queries, keys, (((1,), (1,)), ((), ())), preferred_element_type=jnp.float32
+    )
+    return jnp.where(mask, scores * (1.0 / math.sqrt(keys.shape[1])), NEGATIVE)
+
+
+def early_kernel(
+    length_ref, query_ref, own_ref, beside_ref, across_ref, one_own_ref, one_other_ref,
+    two_own_ref, two_other_ref, max_ref, denominator_ref, weighted_ref, late_ref
+):
+    heads, chunk, both = own_ref.shape
+    rows = query_ref.shape[1]
+    head_dim = both // 2
+    refs = (
         own_ref, beside_ref, across_ref.at[0], across_ref.at[1],
         one_own_ref.at[0], one_own_ref.at[1], one_other_ref.at[0], one_other_ref.at[1],
         two_own_ref.at[0], two_own_ref.at[1], two_other_ref.at[0], two_other_ref.at[1],
-        one_other_ref.at[2], one_other_ref.at[3], three_other_ref.at[0], three_other_ref.at[1],
-    )
-    index = lax.broadcasted_iota(jnp.int32, (1, len(slots) * chunk), 1)
-    end = jnp.zeros_like(index)
-    for slot in range(len(slots)):
-        place = (own_chunk ^ (slot % 4)) * chunk
-        limit = length_ref[own_patch ^ (slot // 4)] - place + slot * chunk
-        end = jnp.where(index >= slot * chunk, limit, end)
-    mask = jnp.broadcast_to(index < end, (rows, len(slots) * chunk))
-    sources = [jnp.concatenate([ref[head] for ref in slots], axis=0) for head in range(heads)]
+        one_other_ref.at[2], one_other_ref.at[3],
+    )
+    slots = [(slot // 4, slot % 4) for slot in range(len(refs))]
+    late_ref[...] = key_mask(length_ref, [(3, 2), (3, 3)], chunk).astype(jnp.int32)
+    mask = key_mask(length_ref, slots, chunk)
+    mask = jnp.broadcast_to(mask, (rows, mask.shape[1]))
+    sources = [jnp.concatenate([ref[head] for ref in refs], axis=0) for head in range(heads)]
     scores = [
-        lax.dot_general(
-            query_ref[head, first : first + rows],
-            sources[head][:, :head_dim],
-            (((1,), (1,)), ((), ())),
+        masked_scores(query_ref[head], sources[head][:, :head_dim], mask) for head in range(heads)
+    ]
+    maxima = [jnp.max(values, axis=1, keepdims=True) for values in scores]
+    weights = [
+        jnp.where(mask, jnp.exp(values - top), 0.0) for values, top in zip(scores, maxima)
+    ]
+    for head in range(heads):
+        max_ref[head] = maxima[head]
+        denominator_ref[head] = jnp.sum(weights[head], axis=1, keepdims=True)
+        weighted_ref[head] = jnp.dot(
+            weights[head].astype(jnp.bfloat16),
+            sources[head][:, head_dim:],
+            preferred_element_type=jnp.float32,
+        )
+
+
+def late_kernel(
+    first, query_ref, max_ref, denominator_ref, weighted_ref, late_ref, three_other_ref, weight_ref,
+    kept_ref, sent_ref, attended_ref
+):
+    _, heads, chunk, both = three_other_ref.shape
+    rows = attended_ref.shape[0]
+    head_dim = both // 2
+    span = slice(first, first + rows)
+    mask = jnp.broadcast_to(late_ref[...] > 0, (rows, 2 * chunk))
+    sources = [
+        jnp.concatenate([three_other_ref[0, head], three_other_ref[1, head]], axis=0)
+        for head in range(heads)
+    ]
+    scores = [
+        masked_scores(query_ref[head, span], sources[head][:, :head_dim], mask)
+        for head in range(heads)
+    ]
+    maxima = [
+        jnp.maximum(max_ref[head, span], jnp.max(scores[head], axis=1, keepdims=True))
+        for head in range(heads)
+    ]
+    weights = [
+        jnp.where(mask, jnp.exp(values - top), 0.0) for values, top in zip(scores, maxima)
+    ]
+    summed = [
+        jnp.dot(
+            weights[head].astype(jnp.bfloat16),
+            sources[head][:, head_dim:],
             preferred_element_type=jnp.float32,
         )
         for head in range(heads)
     ]
-    scores = [jnp.where(mask, values * scale, NEGATIVE) for values in scores]
-    maxima = [jnp.max(values, axis=1, keepdims=True) for values in scores]
-    weights = [
-        jnp.where(mask, jnp.exp(values - top), 0.0) for values, top in zip(scores, maxima)
-    ]
-    denominators = [jnp.sum(values, axis=1, keepdims=True) for values in weights]
-    summed = [
-        jnp.dot(
-            values.astype(jnp.bfloat16), source[:, head_dim:], preferred_element_type=jnp.float32
+    for head in range(heads):
+        factor = jnp.exp(max_ref[head, span] - maxima[head])
+        denominator = denominator_ref[head, span] * factor
+        denominator = denominator + jnp.sum(weights[head], axis=1, keepdims=True)
+        total = weighted_ref[head, span] * factor + summed[head]
+        attended_ref[:, head * head_dim : (head + 1) * head_dim] = (total / denominator).astype(
+            jnp.bfloat16
         )
-        for values, source in zip(weights, sources)
-    ]
-    for head in range(heads):
-        attended_ref[:, head * head_dim : (head + 1) * head_dim] = (
-            summed[head] / denominators[head]
-        ).astype(jnp.bfloat16)
     partial = jnp.dot(attended_ref[...], weight_ref[...], preferred_element_type=jnp.float32)
     partial = partial.astype(jnp.bfloat16)
     kept_ref[...] = partial[:chunk].astype(jnp.float32)
     sent_ref[...] = partial[chunk:]
 
 
-def attend_half(half, lengths, queries, sources, out_weight):
-    heads, chunk, both = sources[0].shape
+def attend_early(lengths, queries, sources):
+    heads, rows, head_dim = queries.shape
+    keys = 14 * rows // 4
+    column = jax.ShapeDtypeStruct((heads, rows, 1), jnp.float32)
+    return kernel_call(
+        early_kernel,
+        (lengths, queries) + sources,
+        [
+            column,
+            column,
+            jax.ShapeDtypeStruct((heads, rows, head_dim), jnp.float32),
+            jax.ShapeDtypeStruct((1, rows // 2), jnp.int32),
+        ],
+        [],
+        12,
+        (4 * rows * keys * heads * head_dim, 4 * keys * heads * head_dim, rows * keys * heads),
+        smem_inputs=1,
+    )
+
+
+def attend_half(half, queries, state, last_source, out_weight):
+    _, _, chunk, _ = last_source.shape
     depth, width = out_weight.shape
     rows = 2 * chunk
-    keys = 16 * chunk
     return kernel_call(
-        functools.partial(attend_kernel, half * rows),
-        (lengths, queries) + sources + (out_weight,),
+        functools.partial(late_kernel, half * rows),
+        (queries,) + state + (last_source, out_weight),
         [
             jax.ShapeDtypeStruct((chunk, width), jnp.float32),
             jax.ShapeDtypeStruct((chunk, width), jnp.bfloat16),
         ],
         [pltpu.VMEM((rows, depth), jnp.bfloat16)],
         12,
-        (2 * rows * depth * width + 4 * rows * keys * depth, 2 * (depth * width + keys * heads * both), 0),
-        smem_inputs=1,
+        (2 * rows * depth * width, 2 * depth * width, 0),
     )
 
 
@@ -428,9 +490,8 @@
         8,
         (2 * parts * rows * width * heads_dev * triple, 2 * width * heads_dev * triple, 0),
     )
-    sources = (
-        own_cache, beside_cache, across_cache, one_own, one_other, two_own, two_other, three_other
-    )
+    sources = (own_cache, beside_cache, across_cache, one_own, one_other, two_own, two_other)
+    state = tuple(attend_early(lengths, queries, sources))
 
     from_across = swap(across_cache, "head")
     from_beside = swap(beside_cache, "rep")
@@ -448,7 +509,7 @@
     )[0]
 
     flat_weight = out_weight.reshape(heads_dev * head_dim, width)
-    far_kept, far_sent = attend_half(1, lengths, queries, sources, flat_weight)
+    far_kept, far_sent = attend_half(1, queries, state, three_other, flat_weight)
     far_received = swap(far_sent, "rep")
     far_sum = kernel_call(
         add_kernel,
@@ -459,7 +520,7 @@
         (rows * width, 8 * rows * width, 0),
     )[0]
     received = swap(far_sum, "head")
-    near_kept, near_sent = attend_half(0, lengths, queries, sources, flat_weight)
+    near_kept, near_sent = attend_half(0, queries, state, three_other, flat_weight)
     near_received = swap(near_sent, "rep")
     update = kernel_call(
         finish_kernel,

time: 50.1 us -> 54.5 us (1.088)
  starting transfers between devices: 15.1 us -> 17.8 us
  waiting for transfers between devices: 20.4 us -> 21.9 us
    ppermute x5, starting transfers between devices: 8.54 us -> 11.2 us  [hop(): lax.ppermute(values, 'patch', [(place, place ^ distance) for place in ran...]
    ppermute x5, waiting for transfers between devices: 10.9 us -> 12.5 us  [hop(): lax.ppermute(values, 'patch', [(place, place ^ distance) for place in ran...]
    pallas_call x10 -> x11, Pallas kernels: 8.61 us -> 8.73 us  [kernel_call(): pl.pallas_call(body, in_specs=[SMEM] * smem_inputs + [VMEM] * (count - sm...]
  transfers between devices with their start and end apart: 17 -> 17, of which waited for: 8 -> 6; matrix products, arithmetic and copies ran while one was open for 0% -> 0% of each run, Pallas kernels for 19% -> 19%
where the time goes in v4:
time: 54.5 us; the launch traced here: 54.3 us
  waiting for transfers between devices  21.9 us (40%)
  starting transfers between devices  17.8 us (33%)
  Pallas kernels  13.7 us (25%)
  between operations  0.82 us (2%)
    ppermute x5, waiting for transfers between devices, hop(): lax.ppermute(values, 'patch', [(place, place ^ distance) for place in ran...  12.5 us
    ppermute x5, starting transfers between devices, hop(): lax.ppermute(values, 'patch', [(place, place ^ distance) for place in ran...  11.2 us
    ppermute x12, waiting for transfers between devices, swap(): return lax.ppermute(values, axis, [(0, 1), (1, 0)])  9.42 us
    pallas_call x11, Pallas kernels, kernel_call(): pl.pallas_call(body, in_specs=[SMEM] * smem_inputs + [VMEM] * (count - sm...  8.73 us
    ppermute x12, starting transfers between devices, swap(): return lax.ppermute(values, axis, [(0, 1), (1, 0)])  6.58 us
    pallas_call x1, Pallas kernels, paired_block(): pl.pallas_call(relayout_kernel, in_specs=[pl.BlockSpec(memory_space=pltpu...  4.98 us
  transfers between devices with their start and end apart: 17, of which 6 were waited for; matrix products, arithmetic and copies ran while one was open for 0% of the time, Pallas kernels for 19%

profile of v4, /device:TPU:0, one launch (start us, length us, event | category | flops | bytes accessed | tf_op | source)
XLA Modules:
  0.0 54.3 jit_solution(10763082567583093690)
XLA Ops:
  0.6 1.5 %shard_map.95 = (bf16[4,32,256]{2,1,0:T(8,128)(2,1)S(1)}, bf16[4,32,256]{2,1,0:T(8,128)(2,1)S(1)}, bf16[2,4,32,256]{3,2,1,0:T(8,128)(2,1)S(1)}, bf16[32,3072]{1,0:T(8,128)(2,1)S(1)}) custom-call(bf16[32,16,256]{2,1,0:T(8,128)(2,1)} %stale_ref.1, bf16[32,3072]{1,0:T(8,128)(2,1)} %token_ref.1, f32[3,3072]{1,0:T(4,128)} %modulation_ref.3), custom_call_target="tpu_custom_call" | custom-call | flops 786432 | bytes 917504 | tf_op jit(solution)/shard_map/pallas_call | solution.py:143
  2.2 3.0 %collective-permute-start.5 = (bf16[2,4,32,256]{3,2,1,0:T(8,128)(2,1)S(1)}, bf16[2,4,32,256]{3,2,1,0:T(8,128)(2,1)S(1)}, u32[]{:S(2)}, u32[]{:S(2)}) collective-permute-start(bf16[2,4,32,256]{3,2,1,0:T(8,128)(2,1)S(1)} %get-tuple-element.25), channel_id=1, source_target_pairs={{0,2},{2,0},{1,3},{3,1},{4,6},{6,4},{5,7},{7,5},{8,10},{10,8},{9,1... | collective-permute-start | bytes 393224 | tf_op jit(solution)/shard_map/ppermute | solution.py:133
  5.2 0.1 collective-permute-start.1
  5.3 0.0 collective-permute-start.3
  5.3 4.3 %collective-permute-done.5.across_ref = bf16[2,4,32,256]{3,2,1,0:T(8,128)(2,1)S(1)} collective-permute-done((bf16[2,4,32,256]{3,2,1,0:T(8,128)(2,1)S(1)}, bf16[2,4,32,256]{3,2,1,0:T(8,128)(2,1)S(1)}, u32[]{:S(2)}, u32[]{:S(2)}) %collective-permute-start.5) | collective-permute-done | bytes 131104 | tf_op jit(solution)/shard_map/ppermute | solution.py:133
  9.5 0.0 collective-permute-start.6
  9.5 0.0 collective-permute-done.3.beside_ref
  9.6 3.2 %collective-permute-start.7 = (bf16[2,4,32,256]{3,2,1,0:T(8,128)(2,1)S(1)}, bf16[2,4,32,256]{3,2,1,0:T(8,128)(2,1)S(1)}, u32[]{:S(2)}, u32[]{:S(2)}) collective-permute-start(bf16[2,4,32,256]{3,2,1,0:T(8,128)(2,1)S(1)} %shard_map.97), channel_id=1, source_target_pairs={{0,8},{4,12},{8,0},{12,4},{1,9},{5,13},{9,1},{13,5},{2,10},{6,14},... | collective-permute-start | bytes 393224 | tf_op jit(solution)/shard_map/ppermute | solution.py:413
  12.7 0.2 collective-permute-start
  13.0 0.0 collective-permute-done.1.across_ref
  13.0 0.3 collective-permute-start.2
  13.3 0.0 collective-permute-done.6.diagonal_ref
  13.3 6.4 %collective-permute-done.7.came_ref.two_own_ref = bf16[2,4,32,256]{3,2,1,0:T(8,128)(2,1)S(1)} collective-permute-done((bf16[2,4,32,256]{3,2,1,0:T(8,128)(2,1)S(1)}, bf16[2,4,32,256]{3,2,1,0:T(8,128)(2,1)S(1)}, u32[]{:S(2)}, u32[]{:S(2)}) %collective-permute-start.7) | collective-permute-done | bytes 131104 | tf_op jit(solution)/shard_map/ppermute | solution.py:413
  19.7 0.0 copy-start.3
  19.8 0.0 copy-start.4
  19.8 0.8 %collective-permute-start.8 = (bf16[4,4,32,256]{3,2,1,0:T(8,128)(2,1)S(1)}, bf16[4,4,32,256]{3,2,1,0:T(8,128)(2,1)S(1)}, u32[]{:S(2)}, u32[]{:S(2)}) collective-permute-start(bf16[4,4,32,256]{3,2,1,0:T(8,128)(2,1)S(1)} %shard_map.99), channel_id=1, source_target_pairs={{0,4},{4,0},{8,12},{12,8},{1,5},{5,1},{9,13},{13,9},{2,6},{6,2},{1... | collective-permute-start | bytes 786440 | tf_op jit(solution)/shard_map/ppermute | solution.py:413
  20.6 3.4 %collective-permute-start.9 = (bf16[2,4,32,256]{3,2,1,0:T(8,128)(2,1)S(1)}, bf16[2,4,32,256]{3,2,1,0:T(8,128)(2,1)S(1)}, u32[]{:S(2)}, u32[]{:S(2)}) collective-permute-start(bf16[2,4,32,256]{3,2,1,0:T(8,128)(2,1)S(1)} %shard_map.98.other_ref), channel_id=1, source_target_pairs={{0,8},{4,12},{8,0},{12,4},{1,9},{5,13},{9,1},{13,5},{2,10},{6,14},... | collective-permute-start | bytes 393224 | tf_op jit(solution)/shard_map/ppermute | solution.py:413
  23.9 0.1 collective-permute-start.4
  24.0 6.1 %collective-permute-done.9.two_other_ref = bf16[2,4,32,256]{3,2,1,0:T(8,128)(2,1)S(1)} collective-permute-done((bf16[2,4,32,256]{3,2,1,0:T(8,128)(2,1)S(1)}, bf16[2,4,32,256]{3,2,1,0:T(8,128)(2,1)S(1)}, u32[]{:S(2)}, u32[]{:S(2)}) %collective-permute-start.9) | collective-permute-done | bytes 131104 | tf_op jit(solution)/shard_map/ppermute | solution.py:413
  30.1 3.8 %collective-permute-start.10 = (bf16[2,4,32,256]{3,2,1,0:T(8,128)(2,1)S(1)}, bf16[2,4,32,256]{3,2,1,0:T(8,128)(2,1)S(1)}, u32[]{:S(2)}, u32[]{:S(2)}) collective-permute-start(bf16[2,4,32,256]{3,2,1,0:T(8,128)(2,1)S(1)} %collective-permute-done.9.two_other_ref), channel_id=1, source_target_pairs={{0,4},{4,0},{8,12},{12,8},{1,5},{5,1},{9,13},{13,9},{2,6},{6,2},{1... | collective-permute-start | bytes 393224 | tf_op jit(solution)/shard_map/ppermute | solution.py:413
  33.9 5.0 %relayout.1.weight_ref = bf16[4,3072,384]{2,1,0:T(8,128)(2,1)S(1)} custom-call(bf16[3072,4,384]{2,1,0:T(4,128)(2,1)} %weight_ref.1), custom_call_target="tpu_custom_call" | custom-call | bytes 18874368 | tf_op jit(solution)/shard_map/relayout/pallas_call | solution.py:461
  38.9 0.0 copy-start.2
  38.9 0.0 copy-start
  38.9 0.0 collective-permute-done.beside_ref
  38.9 0.0 collective-permute-done.2.diagonal_ref
  38.9 0.0 copy-done.3
  38.9 0.0 copy-done.4
  39.0 0.0 copy-start.1
  39.0 1.9 %shard_map.96 = (bf16[4,128,128]{2,1,0:T(8,128)(2,1)S(1)}, bf16[4,32,256]{2,1,0:T(8,128)(2,1)S(1)}, bf16[4,32,256]{2,1,0:T(8,128)(2,1)S(1)}, bf16[2,4,32,256]{3,2,1,0:T(8,128)(2,1)S(1)}) custom-call(bf16[32,3072]{1,0:T(8,128)(2,1)S(1)} %get-tuple-element.18.own_ref, bf16[32,3072]{1,0:T(8,128)(2,1)S(1)} %collective-permute-done.beside_ref, ...), custom_call_target="tpu_custom_call" | custom-call | flops 1207959552 | bytes 9437184 | tf_op jit(solution)/shard_map/pallas_call | solution.py:143
  40.9 0.0 collective-permute-done.4.one_own_ref
  40.9 0.0 collective-permute-done.8.one_other_ref
  40.9 0.0 copy-done.2
  40.9 1.2 %shard_map.100 = (f32[4,128,1]{2,1,0:T(8,128)S(1)}, f32[4,128,1]{2,1,0:T(8,128)S(1)}, f32[4,128,128]{2,1,0:T(8,128)S(1)}, s32[1,64]{1,0:T(1,128)S(1)}) custom-call(s32[4]{0:T(128)S(1)} %copy-done.2, bf16[4,128,128]{2,1,0:T(8,128)(2,1)S(1)} %get-tuple-element.19.query_ref, bf16[4,32,256]{2,1,0:T(8,128)(2,1)S(1)} %get-tuple-element.20.own_ref, ...), custom_call_target="tpu_custom_call" | custom-call | flops 117440512 | bytes 917504 | tf_op jit(solution)/shard_map/pallas_call | solution.py:143
  42.1 0.0 collective-permute-done.10.three_other_ref
  42.1 0.0 copy-done
  42.1 1.2 %shard_map.102 = (f32[32,3072]{1,0:T(8,128)S(1)}, bf16[32,3072]{1,0:T(8,128)(2,1)S(1)}) custom-call(bf16[4,128,128]{2,1,0:T(8,128)(2,1)S(1)} %get-tuple-element.19.query_ref, f32[4,128,1]{2,1,0:T(8,128)S(1)} %get-tuple-element.26.max_ref, f32[4,128,1]{2,1,0:T(8,128)S(1)} %get-tuple-element.27.denominator_ref, ...), custom_call_target="tpu_custom_call" | custom-call | flops 201326592 | bytes 3145728 | tf_op jit(solution)/shard_map/pallas_call | solution.py:143
  43.3 0.1 collective-permute-start.12
  43.4 1.6 %collective-permute-start.15 = (bf16[2,4,32,256]{3,2,1,0:T(8,128)(2,1)S(1)}, bf16[2,4,32,256]{3,2,1,0:T(8,128)(2,1)S(1)}, u32[]{:S(2)}, u32[]{:S(2)}) collective-permute-start(bf16[2,4,32,256]{3,2,1,0:T(8,128)(2,1)S(1)} %get-tuple-element.22.across_ref), channel_id=1, source_target_pairs={{0,2},{2,0},{1,3},{3,1},{4,6},{6,4},{5,7},{7,5},{8,10},{10,8},{9,1... | collective-permute-start | bytes 393224 | tf_op jit(solution)/shard_map/ppermute | solution.py:133
  44.9 1.1 %shard_map.101 = (f32[32,3072]{1,0:T(8,128)S(1)}, bf16[32,3072]{1,0:T(8,128)(2,1)S(1)}) custom-call(bf16[4,128,128]{2,1,0:T(8,128)(2,1)S(1)} %get-tuple-element.19.query_ref, f32[4,128,1]{2,1,0:T(8,128)S(1)} %get-tuple-element.26.max_ref, f32[4,128,1]{2,1,0:T(8,128)S(1)} %get-tuple-element.27.denominator_ref, ...), custom_call_target="tpu_custom_call" | custom-call | flops 201326592 | bytes 3145728 | tf_op jit(solution)/shard_map/pallas_call | solution.py:143
  46.1 0.2 collective-permute-start.11
  46.3 0.0 collective-permute-done.12.received_ref
  46.4 0.6 %collective-permute-start.13 = (bf16[32,3072]{1,0:T(8,128)(2,1)S(1)}, bf16[32,3072]{1,0:T(8,128)(2,1)S(1)}, u32[]{:S(2)}, u32[]{:S(2)}) collective-permute-start(bf16[32,3072]{1,0:T(8,128)(2,1)S(1)} %shard_map.103), channel_id=1, source_target_pairs={{0,2},{2,0},{1,3},{3,1},{4,6},{6,4},{5,7},{7,5},{8,10},{10,8},{9,1... | collective-permute-start | bytes 589832 | tf_op jit(solution)/shard_map/ppermute | solution.py:133
  46.9 2.3 %collective-permute-done.15.across_ref = bf16[2,4,32,256]{3,2,1,0:T(8,128)(2,1)S(1)} collective-permute-done((bf16[2,4,32,256]{3,2,1,0:T(8,128)(2,1)S(1)}, bf16[2,4,32,256]{3,2,1,0:T(8,128)(2,1)S(1)}, u32[]{:S(2)}, u32[]{:S(2)}) %collective-permute-start.15) | collective-permute-done | bytes 131104 | tf_op jit(solution)/shard_map/ppermute | solution.py:133
  49.3 0.0 collective-permute-start.16
  49.3 0.5 collective-permute-start.14
  49.8 0.9 %collective-permute-done.14.beside_ref = bf16[4,32,256]{2,1,0:T(8,128)(2,1)S(1)} collective-permute-done((bf16[4,32,256]{2,1,0:T(8,128)(2,1)S(1)}, bf16[4,32,256]{2,1,0:T(8,128)(2,1)S(1)}, u32[]{:S(2)}, u32[]{:S(2)}) %collective-permute-start.14) | collective-permute-done | bytes 65568 | tf_op jit(solution)/shard_map/ppermute | solution.py:133
  50.7 0.0 collective-permute-done.16.diagonal_ref
  50.7 1.0 %shard_map.105 = bf16[32,16,256]{2,1,0:T(8,128)(2,1)} custom-call(bf16[4,32,256]{2,1,0:T(8,128)(2,1)S(1)} %get-tuple-element.20.own_ref, bf16[4,32,256]{2,1,0:T(8,128)(2,1)S(1)} %collective-permute-done.14.beside_ref, bf16[2,4,32,256]{3,2,1,0:T(8,128)(2,1)S(1)} %collective-permute-done.15.across_ref, ...), custom_call_target="tpu_custom_call" | custom-call | bytes 524288 | tf_op jit(solution)/shard_map/pallas_call | solution.py:143
  51.7 0.0 collective-permute-done.11.beside_ref
  51.7 1.9 %collective-permute-done.13.across_ref = bf16[32,3072]{1,0:T(8,128)(2,1)S(1)} collective-permute-done((bf16[32,3072]{1,0:T(8,128)(2,1)S(1)}, bf16[32,3072]{1,0:T(8,128)(2,1)S(1)}, u32[]{:S(2)}, u32[]{:S(2)}) %collective-permute-start.13) | collective-permute-done | bytes 196640 | tf_op jit(solution)/shard_map/ppermute | solution.py:133
  53.6 0.0 copy-done.1
  53.6 0.8 %shard_map.104 = bf16[32,3072]{1,0:T(8,128)(2,1)} custom-call(f32[32,3072]{1,0:T(8,128)S(1)} %get-tuple-element.30.kept_ref, bf16[32,3072]{1,0:T(8,128)(2,1)S(1)} %collective-permute-done.11.beside_ref, bf16[32,3072]{1,0:T(8,128)(2,1)S(1)} %collective-permute-done.13.across_ref, f32[3,3072]{1,0:T(4,128)S(1)} %copy-done.1), custom_call_target="tpu_custom_call" | custom-call | flops 294912 | bytes 983040 | tf_op jit(solution)/shard_map/pallas_call | solution.py:143
  (4 shorter events, 0.1 us)
Async XLA Ops:
  2.2 7.4 %collective-permute-start.5 = (bf16[2,4,32,256]{3,2,1,0:T(8,128)(2,1)S(1)}, bf16[2,4,32,256]{3,2,1,0:T(8,128)(2,1)S(1)}, u32[]{:S(2)}, u32[]{:S(2)}) collective-permute-start(bf16[2,4,32,256]{3,2,1,0:T(8,128)(2,1)S(1)} %get-tuple-element.25), channel_id=1, source_target_pairs={{0,2},{2,0},{1,3},{3,1},{4,6},{6,4},{5,7},{7,5},{8,10},{10,8},{9,1... | collective-permute-start | bytes 393224 | tf_op jit(solution)/shard_map/ppermute | solution.py:133
  5.2 7.8 %collective-permute-start.1 = (bf16[32,3072]{1,0:T(8,128)(2,1)S(1)}, bf16[32,3072]{1,0:T(8,128)(2,1)S(1)}, u32[]{:S(2)}, u32[]{:S(2)}) collective-permute-start(bf16[32,3072]{1,0:T(8,128)(2,1)S(1)} %get-tuple-element.18.own_ref), channel_id=1, source_target_pairs={{0,2},{2,0},{1,3},{3,1},{4,6},{6,4},{5,7},{7,5},{8,10},{10,8},{9,1... | collective-permute-start | bytes 589832 | tf_op jit(solution)/shard_map/ppermute | solution.py:133
  5.3 4.3 %collective-permute-start.3 = (bf16[4,32,256]{2,1,0:T(8,128)(2,1)S(1)}, bf16[4,32,256]{2,1,0:T(8,128)(2,1)S(1)}, u32[]{:S(2)}, u32[]{:S(2)}) collective-permute-start(bf16[4,32,256]{2,1,0:T(8,128)(2,1)S(1)} %get-tuple-element.24), channel_id=1, source_target_pairs={{0,1},{1,0},{2,3},{3,2},{4,5},{5,4},{6,7},{7,6},{8,9},{9,8},{10,11... | collective-permute-start | bytes 196616 | tf_op jit(solution)/shard_map/ppermute | solution.py:133
  9.5 3.7 %collective-permute-start.6 = (bf16[2,4,32,256]{3,2,1,0:T(8,128)(2,1)S(1)}, bf16[2,4,32,256]{3,2,1,0:T(8,128)(2,1)S(1)}, u32[]{:S(2)}, u32[]{:S(2)}) collective-permute-start(bf16[2,4,32,256]{3,2,1,0:T(8,128)(2,1)S(1)} %collective-permute-done.5.across_ref), channel_id=1, source_target_pairs={{0,1},{1,0},{2,3},{3,2},{4,5},{5,4},{6,7},{7,6},{8,9},{9,8},{10,11... | collective-permute-start | bytes 393224 | tf_op jit(solution)/shard_map/ppermute | solution.py:133
  9.6 10.2 %collective-permute-start.7 = (bf16[2,4,32,256]{3,2,1,0:T(8,128)(2,1)S(1)}, bf16[2,4,32,256]{3,2,1,0:T(8,128)(2,1)S(1)}, u32[]{:S(2)}, u32[]{:S(2)}) collective-permute-start(bf16[2,4,32,256]{3,2,1,0:T(8,128)(2,1)S(1)} %shard_map.97), channel_id=1, source_target_pairs={{0,8},{4,12},{8,0},{12,4},{1,9},{5,13},{9,1},{13,5},{2,10},{6,14},... | collective-permute-start | bytes 393224 | tf_op jit(solution)/shard_map/ppermute | solution.py:413
  12.7 26.2 %collective-permute-start = (bf16[32,3072]{1,0:T(8,128)(2,1)S(1)}, bf16[32,3072]{1,0:T(8,128)(2,1)S(1)}, u32[]{:S(2)}, u32[]{:S(2)}) collective-permute-start(bf16[32,3072]{1,0:T(8,128)(2,1)S(1)} %get-tuple-element.18.own_ref), channel_id=1, source_target_pairs={{0,1},{1,0},{2,3},{3,2},{4,5},{5,4},{6,7},{7,6},{8,9},{9,8},{10,11... | collective-permute-start | bytes 589832 | tf_op jit(solution)/shard_map/ppermute | solution.py:133
  13.0 26.0 %collective-permute-start.2 = (bf16[32,3072]{1,0:T(8,128)(2,1)S(1)}, bf16[32,3072]{1,0:T(8,128)(2,1)S(1)}, u32[]{:S(2)}, u32[]{:S(2)}) collective-permute-start(bf16[32,3072]{1,0:T(8,128)(2,1)S(1)} %collective-permute-done.1.across_ref), channel_id=1, source_target_pairs={{0,1},{1,0},{2,3},{3,2},{4,5},{5,4},{6,7},{7,6},{8,9},{9,8},{10,11... | collective-permute-start | bytes 589832 | tf_op jit(solution)/shard_map/ppermute | solution.py:133
  19.7 19.2 %copy-start.3 = (f32[128]{0:T(128)S(1)}, f32[128]{0:T(128)}, u32[]{:S(2)}) copy-start(f32[128]{0:T(128)} %param.11) | copy-start | bytes 1540
  19.8 19.2 %copy-start.4 = (f32[128]{0:T(128)S(1)}, f32[128]{0:T(128)}, u32[]{:S(2)}) copy-start(f32[128]{0:T(128)} %param.12) | copy-start | bytes 1540
  19.8 21.1 %collective-permute-start.8 = (bf16[4,4,32,256]{3,2,1,0:T(8,128)(2,1)S(1)}, bf16[4,4,32,256]{3,2,1,0:T(8,128)(2,1)S(1)}, u32[]{:S(2)}, u32[]{:S(2)}) collective-permute-start(bf16[4,4,32,256]{3,2,1,0:T(8,128)(2,1)S(1)} %shard_map.99), channel_id=1, source_target_pairs={{0,4},{4,0},{8,12},{12,8},{1,5},{5,1},{9,13},{13,9},{2,6},{6,2},{1... | collective-permute-start | bytes 786440 | tf_op jit(solution)/shard_map/ppermute | solution.py:413
  20.6 9.5 %collective-permute-start.9 = (bf16[2,4,32,256]{3,2,1,0:T(8,128)(2,1)S(1)}, bf16[2,4,32,256]{3,2,1,0:T(8,128)(2,1)S(1)}, u32[]{:S(2)}, u32[]{:S(2)}) collective-permute-start(bf16[2,4,32,256]{3,2,1,0:T(8,128)(2,1)S(1)} %shard_map.98.other_ref), channel_id=1, source_target_pairs={{0,8},{4,12},{8,0},{12,4},{1,9},{5,13},{9,1},{13,5},{2,10},{6,14},... | collective-permute-start | bytes 393224 | tf_op jit(solution)/shard_map/ppermute | solution.py:413
  23.9 16.9 %collective-permute-start.4 = (bf16[2,4,32,256]{3,2,1,0:T(8,128)(2,1)S(1)}, bf16[2,4,32,256]{3,2,1,0:T(8,128)(2,1)S(1)}, u32[]{:S(2)}, u32[]{:S(2)}) collective-permute-start(bf16[2,4,32,256]{3,2,1,0:T(8,128)(2,1)S(1)} %shard_map.97), channel_id=1, source_target_pairs={{0,4},{4,0},{8,12},{12,8},{1,5},{5,1},{9,13},{13,9},{2,6},{6,2},{1... | collective-permute-start | bytes 393224 | tf_op jit(solution)/shard_map/ppermute | solution.py:413
  30.1 12.0 %collective-permute-start.10 = (bf16[2,4,32,256]{3,2,1,0:T(8,128)(2,1)S(1)}, bf16[2,4,32,256]{3,2,1,0:T(8,128)(2,1)S(1)}, u32[]{:S(2)}, u32[]{:S(2)}) collective-permute-start(bf16[2,4,32,256]{3,2,1,0:T(8,128)(2,1)S(1)} %collective-permute-done.9.two_other_ref), channel_id=1, source_target_pairs={{0,4},{4,0},{8,12},{12,8},{1,5},{5,1},{9,13},{13,9},{2,6},{6,2},{1... | collective-permute-start | bytes 393224 | tf_op jit(solution)/shard_map/ppermute | solution.py:413
  38.9 2.0 %copy-start.2 = (s32[4]{0:T(128)S(1)}, s32[4]{0:T(128)}, u32[]{:S(2)}) copy-start(s32[4]{0:T(128)} %length_ref.1) | copy-start | bytes 52
  38.9 3.2 %copy-start = (bf16[4,128,3072]{2,1,0:T(8,128)(2,1)S(1)}, bf16[4,128,3072]{2,1,0:T(8,128)(2,1)}, u32[]{:S(2)}) copy-start(bf16[4,128,3072]{2,1,0:T(8,128)(2,1)} %param.13) | copy-start | bytes 9437188
  39.0 14.6 %copy-start.1 = (f32[3,3072]{1,0:T(4,128)S(1)}, f32[3,3072]{1,0:T(4,128)}, u32[]{:S(2)}) copy-start(f32[3,3072]{1,0:T(4,128)} %modulation_ref.3) | copy-start | bytes 110596
  43.3 3.0 %collective-permute-start.12 = (bf16[32,3072]{1,0:T(8,128)(2,1)S(1)}, bf16[32,3072]{1,0:T(8,128)(2,1)S(1)}, u32[]{:S(2)}, u32[]{:S(2)}) collective-permute-start(bf16[32,3072]{1,0:T(8,128)(2,1)S(1)} %get-tuple-element.33), channel_id=1, source_target_pairs={{0,1},{1,0},{2,3},{3,2},{4,5},{5,4},{6,7},{7,6},{8,9},{9,8},{10,11... | collective-permute-start | bytes 589832 | tf_op jit(solution)/shard_map/ppermute | solution.py:133
  43.4 5.9 %collective-permute-start.15 = (bf16[2,4,32,256]{3,2,1,0:T(8,128)(2,1)S(1)}, bf16[2,4,32,256]{3,2,1,0:T(8,128)(2,1)S(1)}, u32[]{:S(2)}, u32[]{:S(2)}) collective-permute-start(bf16[2,4,32,256]{3,2,1,0:T(8,128)(2,1)S(1)} %get-tuple-element.22.across_ref), channel_id=1, source_target_pairs={{0,2},{2,0},{1,3},{3,1},{4,6},{6,4},{5,7},{7,5},{8,10},{10,8},{9,1... | collective-permute-start | bytes 393224 | tf_op jit(solution)/shard_map/ppermute | solution.py:133
  46.1 5.6 %collective-permute-start.11 = (bf16[32,3072]{1,0:T(8,128)(2,1)S(1)}, bf16[32,3072]{1,0:T(8,128)(2,1)S(1)}, u32[]{:S(2)}, u32[]{:S(2)}) collective-permute-start(bf16[32,3072]{1,0:T(8,128)(2,1)S(1)} %get-tuple-element.31), channel_id=1, source_target_pairs={{0,1},{1,0},{2,3},{3,2},{4,5},{5,4},{6,7},{7,6},{8,9},{9,8},{10,11... | collective-permute-start | bytes 589832 | tf_op jit(solution)/shard_map/ppermute | solution.py:133
  46.4 7.2 %collective-permute-start.13 = (bf16[32,3072]{1,0:T(8,128)(2,1)S(1)}, bf16[32,3072]{1,0:T(8,128)(2,1)S(1)}, u32[]{:S(2)}, u32[]{:S(2)}) collective-permute-start(bf16[32,3072]{1,0:T(8,128)(2,1)S(1)} %shard_map.103), channel_id=1, source_target_pairs={{0,2},{2,0},{1,3},{3,1},{4,6},{6,4},{5,7},{7,5},{8,10},{10,8},{9,1... | collective-permute-start | bytes 589832 | tf_op jit(solution)/shard_map/ppermute | solution.py:133
  49.3 1.4 %collective-permute-start.16 = (bf16[2,4,32,256]{3,2,1,0:T(8,128)(2,1)S(1)}, bf16[2,4,32,256]{3,2,1,0:T(8,128)(2,1)S(1)}, u32[]{:S(2)}, u32[]{:S(2)}) collective-permute-start(bf16[2,4,32,256]{3,2,1,0:T(8,128)(2,1)S(1)} %collective-permute-done.15.across_ref), channel_id=1, source_target_pairs={{0,1},{1,0},{2,3},{3,2},{4,5},{5,4},{6,7},{7,6},{8,9},{9,8},{10,11... | collective-permute-start | bytes 393224 | tf_op jit(solution)/shard_map/ppermute | solution.py:133
  49.3 1.4 %collective-permute-start.14 = (bf16[4,32,256]{2,1,0:T(8,128)(2,1)S(1)}, bf16[4,32,256]{2,1,0:T(8,128)(2,1)S(1)}, u32[]{:S(2)}, u32[]{:S(2)}) collective-permute-start(bf16[4,32,256]{2,1,0:T(8,128)(2,1)S(1)} %get-tuple-element.21.beside_ref), channel_id=1, source_target_pairs={{0,1},{1,0},{2,3},{3,2},{4,5},{5,4},{6,7},{7,6},{8,9},{9,8},{10,11... | collective-permute-start | bytes 196616 | tf_op jit(solution)/shard_map/ppermute | solution.py:133

commit v5 on v4

--- a/solution.py
+++ b/solution.py
@@ -156,23 +156,42 @@
 
 
 def enter_kernel(
-    stale_ref, token_ref, modulation_ref, own_ref, beside_ref, across_ref, normed_ref, wide_ref
-):
-    rows, heads, both = stale_ref.shape
+    stale_ref, token_ref, modulation_ref, own_ref, beside_ref, across_ref, token_out_ref,
+    modulation_out_ref, raw_ref, wide_ref, semaphores
+):
+    rows, heads, both = raw_ref.shape
     per_group = own_ref.shape[0]
     own_chunk = own_chunk_index()
+    copies = [
+        pltpu.make_async_copy(source, target, semaphores.at[index])
+        for index, (source, target) in enumerate(
+            (
+                (stale_ref, raw_ref),
+                (token_ref, token_out_ref),
+                (modulation_ref, modulation_out_ref),
+            )
+        )
+    ]
+    for copy in copies:
+        copy.start()
+    copies[0].wait()
     outs = (own_ref, beside_ref, across_ref.at[0], across_ref.at[1])
     for lanes in range(both // 128):
         columns = slice(lanes * 128, (lanes + 1) * 128)
-        wide_ref[lanes] = stale_ref[:, :, columns].astype(jnp.float32).reshape(rows * heads, 128)
+        wide_ref[lanes] = raw_ref[:, :, columns].astype(jnp.float32).reshape(rows * heads, 128)
         for part, out_ref in enumerate(outs):
             for head in range(per_group):
                 first = (own_chunk ^ part) * per_group + head
                 values = wide_ref[lanes, pl.ds(first, rows, stride=heads), :]
                 out_ref[head, :, columns] = values.astype(jnp.bfloat16)
+    for copy in copies[1:]:
+        copy.wait()
+
+
+def normalize_kernel(token_ref, modulation_ref, out_ref):
     values = normalize_rows(token_ref[...].astype(jnp.float32))
     shifted = values * (1.0 + modulation_ref[1:2]) + modulation_ref[0:1]
-    normed_ref[...] = shifted.astype(jnp.bfloat16)
+    out_ref[...] = shifted.astype(jnp.bfloat16)
 
 
 def join_own_kernel(own_ref, beside_ref, out_ref):
@@ -260,10 +279,39 @@
     out_ref[...] = total.astype(out_ref.dtype)
 
 
-def finish_kernel(kept_ref, beside_ref, across_ref, modulation_ref, out_ref):
+def finish_low_kernel(
+    kept_ref, beside_ref, low_ref, modulation_ref, update_ref, rest_ref, staged_ref, semaphore
+):
+    split = low_ref.shape[1]
     near = kept_ref[...] + beside_ref[...].astype(jnp.float32)
-    total = near + across_ref[...].astype(jnp.float32)
-    out_ref[...] = (modulation_ref[2:3] * total).astype(jnp.bfloat16)
+    total = near[:, :split] + low_ref[...].astype(jnp.float32)
+    staged_ref[...] = (modulation_ref[2:3, :split] * total).astype(jnp.bfloat16)
+    copy = pltpu.make_async_copy(staged_ref, update_ref.at[:, :split], semaphore)
+    copy.start()
+    rest_ref[...] = near[:, split:]
+    copy.wait()
+
+
+def finish_high_kernel(
+    begun_ref, rest_ref, high_ref, modulation_ref, update_ref, staged_ref, semaphores
+):
+    width = high_ref.shape[1]
+    split = modulation_ref.shape[1] - width
+    pieces = semaphores.shape[0]
+    copies = []
+    for piece in range(pieces):
+        columns = slice(piece * width // pieces, (piece + 1) * width // pieces)
+        target = slice(split + columns.start, split + columns.stop)
+        total = rest_ref[:, columns] + high_ref[:, columns].astype(jnp.float32)
+        staged_ref[:, columns] = (modulation_ref[2:3, target] * total).astype(jnp.bfloat16)
+        copies.append(
+            pltpu.make_async_copy(
+                staged_ref.at[:, columns], update_ref.at[:, target], semaphores.at[piece]
+            )
+        )
+        copies[-1].start()
+    for copy in copies:
+        copy.wait()
 
 
 def key_mask(length_ref, slots, chunk):
@@ -319,6 +367,15 @@
         )
 
 
+def project_out(attended, weight_ref, first, kept_ref, sent_ref):
+    chunk, width = kept_ref.shape
+    columns = slice(first, first + width)
+    partial = jnp.dot(attended, weight_ref[:, columns], preferred_element_type=jnp.float32)
+    partial = partial.astype(jnp.bfloat16)
+    kept_ref[...] = partial[:chunk].astype(jnp.float32)
+    sent_ref[...] = partial[chunk:]
+
+
 def late_kernel(
     first, query_ref, max_ref, denominator_ref, weighted_ref, late_ref, three_other_ref, weight_ref,
     kept_ref, sent_ref, attended_ref
@@ -359,10 +416,12 @@
         attended_ref[:, head * head_dim : (head + 1) * head_dim] = (total / denominator).astype(
             jnp.bfloat16
         )
-    partial = jnp.dot(attended_ref[...], weight_ref[...], preferred_element_type=jnp.float32)
-    partial = partial.astype(jnp.bfloat16)
-    kept_ref[...] = partial[:chunk].astype(jnp.float32)
-    sent_ref[...] = partial[chunk:]
+    project_out(attended_ref[...], weight_ref, 0, kept_ref, sent_ref)
+
+
+def rest_kernel(attended_ref, weight_ref, kept_ref, sent_ref):
+    first = weight_ref.shape[1] - kept_ref.shape[1]
+    project_out(attended_ref[...], weight_ref, first, kept_ref, sent_ref)
 
 
 def attend_early(lengths, queries, sources):
@@ -385,18 +444,34 @@
     )
 
 
-def attend_half(half, queries, state, last_source, out_weight):
+def halves_shape(chunk, width):
+    return [
+        jax.ShapeDtypeStruct((chunk, width), jnp.float32),
+        jax.ShapeDtypeStruct((chunk, width), jnp.bfloat16),
+    ]
+
+
+def attend_half(half, queries, state, last_source, out_weight, width):
     _, _, chunk, _ = last_source.shape
-    depth, width = out_weight.shape
+    depth = out_weight.shape[0]
     rows = 2 * chunk
     return kernel_call(
         functools.partial(late_kernel, half * rows),
         (queries,) + state + (last_source, out_weight),
-        [
-            jax.ShapeDtypeStruct((chunk, width), jnp.float32),
-            jax.ShapeDtypeStruct((chunk, width), jnp.bfloat16),
-        ],
-        [pltpu.VMEM((rows, depth), jnp.bfloat16)],
+        halves_shape(chunk, width) + [jax.ShapeDtypeStruct((rows, depth), jnp.bfloat16)],
+        [],
+        12,
+        (2 * rows * depth * width, 2 * depth * width, 0),
+    )
+
+
+def project_rest(attended, out_weight, width):
+    rows, depth = attended.shape
+    return kernel_call(
+        rest_kernel,
+        (attended, out_weight),
+        halves_shape(rows // 2, width),
+        [],
         12,
         (2 * rows * depth * width, 2 * depth * width, 0),
     )
@@ -433,18 +508,29 @@
     half = jnp.bfloat16
 
     piece = (heads_dev, rows, both)
-    stale_own, stale_beside, stale_across, normed = kernel_call(
+    stale_own, stale_beside, stale_across, held_tokens, held_modulation = pl.pallas_call(
         enter_kernel,
-        (stale_cache, tokens, modulation),
-        [
+        in_specs=[pl.BlockSpec(memory_space=pltpu.HBM)] * 3,
+        out_specs=[VMEM] * 5,
+        out_shape=[
             pltpu.VMEM(piece, half),
             pltpu.VMEM(piece, half),
             pltpu.VMEM((2,) + piece, half),
-            pltpu.VMEM((rows, width), half),
-        ],
-        [pltpu.VMEM((both // 128, rows * heads, 128), jnp.float32)],
-        60,
-        (8 * rows * width, 4 * rows * (heads * both + width), 0),
+            pltpu.VMEM(tokens.shape, tokens.dtype),
+            pltpu.VMEM(modulation.shape, modulation.dtype),
+        ],
+        scratch_shapes=[
+            pltpu.VMEM(stale_cache.shape, half),
+            pltpu.VMEM((both // 128, rows * heads, 128), jnp.float32),
+            pltpu.SemaphoreType.DMA((3,)),
+        ],
+        compiler_params=pltpu.CompilerParams(vmem_limit_bytes=60 * MIB),
+        cost_estimate=pl.CostEstimate(
+            flops=0, bytes_accessed=4 * rows * (heads * both + width), transcendentals=0
+        ),
+    )(stale_cache, tokens, modulation)
+    normed = small_call(
+        normalize_kernel, (held_tokens, held_modulation), tokens.shape
     )
     came_beside = swap(stale_beside, "rep")
     came_across = swap(stale_across, "head")
@@ -452,7 +538,9 @@
     two_own = hop(chip_rows, 2)
     one_own = hop(chip_rows, 1)
     came_diagonal = swap(came_across, "rep")
-    other_rows = small_call(join_other_kernel, (came_across, came_diagonal), (2,) + piece)
+    other_rows = small_call(
+        join_other_kernel, (came_across, came_diagonal), (2,) + piece
+    )
     two_other = hop(other_rows, 2)
     forward = small_call(join_forward_kernel, (other_rows, two_own), (4,) + piece)
     one_other = hop(forward, 1)
@@ -472,7 +560,6 @@
         cost_estimate=pl.CostEstimate(
             flops=0, bytes_accessed=4 * heads_dev * width * triple, transcendentals=0
         ),
-        name="relayout",
     )(in_weight)
     across = swap(normed, "head")
     beside = swap(normed, "rep")
@@ -509,27 +596,50 @@
     )[0]
 
     flat_weight = out_weight.reshape(heads_dev * head_dim, width)
-    far_kept, far_sent = attend_half(1, queries, state, three_other, flat_weight)
-    far_received = swap(far_sent, "rep")
-    far_sum = kernel_call(
-        add_kernel,
-        (far_kept, far_received),
-        [jax.ShapeDtypeStruct((rows, width), half)],
-        [],
-        4,
-        (rows * width, 8 * rows * width, 0),
-    )[0]
-    received = swap(far_sum, "head")
-    near_kept, near_sent = attend_half(0, queries, state, three_other, flat_weight)
+    part_width = width // 2
+    low_kept, low_sent, attended = attend_half(
+        1, queries, state, three_other, flat_weight, part_width
+    )
+    low_received = swap(low_sent, "rep")
+    high_kept, high_sent = project_rest(attended, flat_weight, width - part_width)
+    high_received = swap(high_sent, "rep")
+    low_sum = small_call(add_kernel, (low_kept, low_received), low_kept.shape)
+    low_across = swap(low_sum, "head")
+    high_sum = small_call(add_kernel, (high_kept, high_received), high_kept.shape)
+    high_across = swap(high_sum, "head")
+    near_kept, near_sent, _ = attend_half(0, queries, state, three_other, flat_weight, width)
     near_received = swap(near_sent, "rep")
-    update = kernel_call(
-        finish_kernel,
-        (near_kept, near_received, received, modulation),
-        [jax.ShapeDtypeStruct((rows, width), half)],
-        [],
-        4,
-        (3 * rows * width, 10 * rows * width, 0),
-    )[0]
+    whole = pl.BlockSpec(memory_space=pltpu.HBM)
+    small = pltpu.CompilerParams(vmem_limit_bytes=4 * MIB)
+    begun, rest = pl.pallas_call(
+        finish_low_kernel,
+        in_specs=[VMEM] * 4,
+        out_specs=[whole, VMEM],
+        out_shape=[
+            jax.ShapeDtypeStruct((rows, width), half),
+            jax.ShapeDtypeStruct((rows, width - part_width), jnp.float32),
+        ],
+        scratch_shapes=[pltpu.VMEM((rows, part_width), half), pltpu.SemaphoreType.DMA],
+        compiler_params=small,
+        cost_estimate=pl.CostEstimate(
+            flops=3 * rows * width, bytes_accessed=8 * rows * width, transcendentals=0
+        ),
+    )(near_kept, near_received, low_across, held_modulation)
+    update = pl.pallas_call(
+        finish_high_kernel,
+        in_specs=[whole] + [VMEM] * 3,
+        out_specs=whole,
+        out_shape=jax.ShapeDtypeStruct((rows, width), half),
+        scratch_shapes=[
+            pltpu.VMEM((rows, width - part_width), half),
+            pltpu.SemaphoreType.DMA((2,)),
+        ],
+        input_output_aliases={0: 0},
+        compiler_params=small,
+        cost_estimate=pl.CostEstimate(
+            flops=rows * width, bytes_accessed=4 * rows * width, transcendentals=0
+        ),
+    )(begun, rest, high_across, held_modulation)
     return (update, new_cache)
 
 

time: 54.5 us -> 49.7 us (0.912)
  waiting for transfers between devices: 21.9 us -> 14.5 us
  starting transfers between devices: 17.8 us -> 19.7 us
  Pallas kernels: 13.7 us -> 14.5 us
    ppermute x5, waiting for transfers between devices: 12.5 us -> 7.51 us  [hop(): lax.ppermute(values, 'patch', [(place, place ^ distance) for place in ran...]
    pallas_call x0 -> x3, Pallas kernels: none -> 2.56 us  [the longest x1 1.2 us: paired_block(): pl.pallas_call(enter_kernel, in_specs=[pl.BlockSpec(memory_space=pltpu.HB...]
    ppermute x12 -> x14, waiting for transfers between devices: 9.42 us -> 7 us  [swap(): return lax.ppermute(values, axis, [(0, 1), (1, 0)])]
    ppermute x12 -> x14, starting transfers between devices: 6.58 us -> 8.49 us  [swap(): return lax.ppermute(values, axis, [(0, 1), (1, 0)])]
    pallas_call x11 -> x12, Pallas kernels: 8.73 us -> 6.94 us  [kernel_call(): pl.pallas_call(body, in_specs=[SMEM] * smem_inputs + [VMEM] * (count - sm...]
  transfers between devices with their start and end apart: 17 -> 19, of which waited for: 6 -> 6; matrix products, arithmetic and copies ran while one was open for 0% -> 0% of each run, Pallas kernels for 19% -> 25%
where the time goes in v5:
time: 49.7 us; the launch traced here: 49.5 us
  starting transfers between devices  19.7 us (40%)
  Pallas kernels  14.5 us (29%)
  waiting for transfers between devices  14.5 us (29%)
  between operations  0.81 us (2%)
    ppermute x5, starting transfers between devices, hop(): lax.ppermute(values, 'patch', [(place, place ^ distance) for place in ran...  11.2 us
    ppermute x14, starting transfers between devices, swap(): return lax.ppermute(values, axis, [(0, 1), (1, 0)])  8.49 us
    ppermute x5, waiting for transfers between devices, hop(): lax.ppermute(values, 'patch', [(place, place ^ distance) for place in ran...  7.51 us
    ppermute x14, waiting for transfers between devices, swap(): return lax.ppermute(values, axis, [(0, 1), (1, 0)])  7 us
    pallas_call x12, Pallas kernels, kernel_call(): pl.pallas_call(body, in_specs=[SMEM] * smem_inputs + [VMEM] * (count - sm...  6.94 us
    pallas_call x1, Pallas kernels, paired_block(): pl.pallas_call(relayout_kernel, in_specs=[pl.BlockSpec(memory_space=pltpu...  4.98 us
    pallas_call x1, Pallas kernels, paired_block(): pl.pallas_call(enter_kernel, in_specs=[pl.BlockSpec(memory_space=pltpu.HB...  1.2 us
  transfers between devices with their start and end apart: 19, of which 6 were waited for; matrix products, arithmetic and copies ran while one was open for 0% of the time, Pallas kernels for 25%

profile of v5, /device:TPU:0, one launch (start us, length us, event | category | flops | bytes accessed | tf_op | source)
XLA Modules:
  0.0 49.5 jit_solution(10727486798815595700)
XLA Ops:
  0.6 1.2 %shard_map.95 = (bf16[4,32,256]{2,1,0:T(8,128)(2,1)S(1)}, bf16[4,32,256]{2,1,0:T(8,128)(2,1)S(1)}, bf16[2,4,32,256]{3,2,1,0:T(8,128)(2,1)S(1)}, bf16[32,3072]{1,0:T(8,128)(2,1)S(1)}, f32[3,3072]{1,0:T(4,128)S(1)}) custom-call(bf16[32,16,256]{2,1,0:T(8,128)(2,1)} %stale_ref.1, bf16[32,3072]{1,0:T(8,128)(2,1)} %token_ref.1, f32[3,3072]{1,0:T(4,128)} %modulation_ref.1), custom_call_target="tpu_custom_call" | custom-call | bytes 917504 | tf_op jit(solution)/shard_map/pallas_call | solution.py:511
  1.8 3.0 %collective-permute-start.5 = (bf16[2,4,32,256]{3,2,1,0:T(8,128)(2,1)S(1)}, bf16[2,4,32,256]{3,2,1,0:T(8,128)(2,1)S(1)}, u32[]{:S(2)}, u32[]{:S(2)}) collective-permute-start(bf16[2,4,32,256]{3,2,1,0:T(8,128)(2,1)S(1)} %get-tuple-element.32), channel_id=1, source_target_pairs={{0,2},{2,0},{1,3},{3,1},{4,6},{6,4},{5,7},{7,5},{8,10},{10,8},{9,1... | collective-permute-start | bytes 393224 | tf_op jit(solution)/shard_map/ppermute | solution.py:133
  4.9 0.3 shard_map.96.own_ref
  5.2 0.1 collective-permute-start.1
  5.2 0.1 collective-permute-start.3
  5.3 3.9 %collective-permute-done.5.across_ref = bf16[2,4,32,256]{3,2,1,0:T(8,128)(2,1)S(1)} collective-permute-done((bf16[2,4,32,256]{3,2,1,0:T(8,128)(2,1)S(1)}, bf16[2,4,32,256]{3,2,1,0:T(8,128)(2,1)S(1)}, u32[]{:S(2)}, u32[]{:S(2)}) %collective-permute-start.5) | collective-permute-done | bytes 131104 | tf_op jit(solution)/shard_map/ppermute | solution.py:133
  9.2 0.0 collective-permute-start.6
  9.2 0.0 collective-permute-done.3.beside_ref
  9.2 3.2 %collective-permute-start.7 = (bf16[2,4,32,256]{3,2,1,0:T(8,128)(2,1)S(1)}, bf16[2,4,32,256]{3,2,1,0:T(8,128)(2,1)S(1)}, u32[]{:S(2)}, u32[]{:S(2)}) collective-permute-start(bf16[2,4,32,256]{3,2,1,0:T(8,128)(2,1)S(1)} %shard_map.99), channel_id=1, source_target_pairs={{0,8},{4,12},{8,0},{12,4},{1,9},{5,13},{9,1},{13,5},{2,10},{6,14},... | collective-permute-start | bytes 393224 | tf_op jit(solution)/shard_map/ppermute | solution.py:488
  12.4 0.2 collective-permute-start
  12.7 0.0 collective-permute-done.1.across_ref
  12.7 0.3 collective-permute-start.2
  12.9 0.0 collective-permute-done.6.diagonal_ref
  13.0 6.4 %collective-permute-done.7.came_ref.two_own_ref = bf16[2,4,32,256]{3,2,1,0:T(8,128)(2,1)S(1)} collective-permute-done((bf16[2,4,32,256]{3,2,1,0:T(8,128)(2,1)S(1)}, bf16[2,4,32,256]{3,2,1,0:T(8,128)(2,1)S(1)}, u32[]{:S(2)}, u32[]{:S(2)}) %collective-permute-start.7) | collective-permute-done | bytes 131104 | tf_op jit(solution)/shard_map/ppermute | solution.py:488
  19.4 0.0 copy-start.2
  19.4 0.0 copy-start.3
  19.4 0.8 %collective-permute-start.8 = (bf16[4,4,32,256]{3,2,1,0:T(8,128)(2,1)S(1)}, bf16[4,4,32,256]{3,2,1,0:T(8,128)(2,1)S(1)}, u32[]{:S(2)}, u32[]{:S(2)}) collective-permute-start(bf16[4,4,32,256]{3,2,1,0:T(8,128)(2,1)S(1)} %shard_map.101), channel_id=1, source_target_pairs={{0,4},{4,0},{8,12},{12,8},{1,5},{5,1},{9,13},{13,9},{2,6},{6,2},{1... | collective-permute-start | bytes 786440 | tf_op jit(solution)/shard_map/ppermute | solution.py:488
  20.3 3.4 %collective-permute-start.9 = (bf16[2,4,32,256]{3,2,1,0:T(8,128)(2,1)S(1)}, bf16[2,4,32,256]{3,2,1,0:T(8,128)(2,1)S(1)}, u32[]{:S(2)}, u32[]{:S(2)}) collective-permute-start(bf16[2,4,32,256]{3,2,1,0:T(8,128)(2,1)S(1)} %shard_map.100.other_ref), channel_id=1, source_target_pairs={{0,8},{4,12},{8,0},{12,4},{1,9},{5,13},{9,1},{13,5},{2,10},{6,14},... | collective-permute-start | bytes 393224 | tf_op jit(solution)/shard_map/ppermute | solution.py:488
  23.6 0.1 collective-permute-start.4
  23.7 5.0 %shard_map.97.weight_ref = bf16[4,3072,384]{2,1,0:T(8,128)(2,1)S(1)} custom-call(bf16[3072,4,384]{2,1,0:T(4,128)(2,1)} %weight_ref.1), custom_call_target="tpu_custom_call" | custom-call | bytes 18874368 | tf_op jit(solution)/shard_map/pallas_call | solution.py:549
  28.7 0.0 copy-start.1
  28.7 0.0 copy-start
  28.7 1.1 %collective-permute-done.9.two_other_ref = bf16[2,4,32,256]{3,2,1,0:T(8,128)(2,1)S(1)} collective-permute-done((bf16[2,4,32,256]{3,2,1,0:T(8,128)(2,1)S(1)}, bf16[2,4,32,256]{3,2,1,0:T(8,128)(2,1)S(1)}, u32[]{:S(2)}, u32[]{:S(2)}) %collective-permute-start.9) | collective-permute-done | bytes 131104 | tf_op jit(solution)/shard_map/ppermute | solution.py:488
  29.8 3.8 %collective-permute-start.10 = (bf16[2,4,32,256]{3,2,1,0:T(8,128)(2,1)S(1)}, bf16[2,4,32,256]{3,2,1,0:T(8,128)(2,1)S(1)}, u32[]{:S(2)}, u32[]{:S(2)}) collective-permute-start(bf16[2,4,32,256]{3,2,1,0:T(8,128)(2,1)S(1)} %collective-permute-done.9.two_other_ref), channel_id=1, source_target_pairs={{0,4},{4,0},{8,12},{12,8},{1,5},{5,1},{9,13},{13,9},{2,6},{6,2},{1... | collective-permute-start | bytes 393224 | tf_op jit(solution)/shard_map/ppermute | solution.py:488
  33.6 0.0 collective-permute-done.beside_ref
  33.6 0.0 collective-permute-done.2.diagonal_ref
  33.6 0.0 copy-done.2
  33.6 0.0 copy-done.3
  33.6 1.9 %shard_map.98 = (bf16[4,128,128]{2,1,0:T(8,128)(2,1)S(1)}, bf16[4,32,256]{2,1,0:T(8,128)(2,1)S(1)}, bf16[4,32,256]{2,1,0:T(8,128)(2,1)S(1)}, bf16[2,4,32,256]{3,2,1,0:T(8,128)(2,1)S(1)}) custom-call(bf16[32,3072]{1,0:T(8,128)(2,1)S(1)} %shard_map.96.own_ref, bf16[32,3072]{1,0:T(8,128)(2,1)S(1)} %collective-permute-done.beside_ref, ...), custom_call_target="tpu_custom_call" | custom-call | flops 1207959552 | bytes 9437184 | tf_op jit(solution)/shard_map/pallas_call | solution.py:143
  35.5 1.6 %collective-permute-start.17 = (bf16[2,4,32,256]{3,2,1,0:T(8,128)(2,1)S(1)}, bf16[2,4,32,256]{3,2,1,0:T(8,128)(2,1)S(1)}, u32[]{:S(2)}, u32[]{:S(2)}) collective-permute-start(bf16[2,4,32,256]{3,2,1,0:T(8,128)(2,1)S(1)} %get-tuple-element.29.across_ref), channel_id=1, source_target_pairs={{0,2},{2,0},{1,3},{3,1},{4,6},{6,4},{5,7},{7,5},{8,10},{10,8},{9,1... | collective-permute-start | bytes 393224 | tf_op jit(solution)/shard_map/ppermute | solution.py:133
  37.0 0.0 collective-permute-done.4.one_own_ref
  37.0 0.0 collective-permute-done.8.one_other_ref
  37.0 0.0 copy-done.1
  37.1 1.2 %shard_map.102 = (f32[4,128,1]{2,1,0:T(8,128)S(1)}, f32[4,128,1]{2,1,0:T(8,128)S(1)}, f32[4,128,128]{2,1,0:T(8,128)S(1)}, s32[1,64]{1,0:T(1,128)S(1)}) custom-call(s32[4]{0:T(128)S(1)} %copy-done.1, bf16[4,128,128]{2,1,0:T(8,128)(2,1)S(1)} %get-tuple-element.26.query_ref, bf16[4,32,256]{2,1,0:T(8,128)(2,1)S(1)} %get-tuple-element.27.own_ref, ...), custom_call_target="tpu_custom_call" | custom-call | flops 117440512 | bytes 917504 | tf_op jit(solution)/shard_map/pallas_call | solution.py:143
  38.3 0.0 collective-permute-done.10.three_other_ref
  38.3 0.0 copy-done
  38.3 0.9 %shard_map.104 = (f32[32,1536]{1,0:T(8,128)S(1)}, bf16[32,1536]{1,0:T(8,128)(2,1)S(1)}, bf16[64,512]{1,0:T(8,128)(2,1)S(1)}) custom-call(bf16[4,128,128]{2,1,0:T(8,128)(2,1)S(1)} %get-tuple-element.26.query_ref, f32[4,128,1]{2,1,0:T(8,128)S(1)} %get-tuple-element.33.max_ref, f32[4,128,1]{2,1,0:T(8,128)S(1)} %get-tuple-element.34.denominator_ref, ...), custom_call_target="tpu_custom_call" | custom-call | flops 100663296 | bytes 1572864 | tf_op jit(solution)/shard_map/pallas_call | solution.py:143
  39.2 0.4 shard_map.107
  39.6 0.1 collective-permute-start.14
  39.6 0.5 %collective-permute-start.12 = (bf16[32,1536]{1,0:T(8,128)(2,1)S(1)}, bf16[32,1536]{1,0:T(8,128)(2,1)S(1)}, u32[]{:S(2)}, u32[]{:S(2)}) collective-permute-start(bf16[32,1536]{1,0:T(8,128)(2,1)S(1)} %get-tuple-element.40), channel_id=1, source_target_pairs={{0,1},{1,0},{2,3},{3,2},{4,5},{5,4},{6,7},{7,6},{8,9},{9,8},{10,11... | collective-permute-start | bytes 294920 | tf_op jit(solution)/shard_map/ppermute | solution.py:133
  40.1 1.2 %shard_map.103 = (f32[32,3072]{1,0:T(8,128)S(1)}, bf16[32,3072]{1,0:T(8,128)(2,1)S(1)}, bf16[64,512]{1,0:T(8,128)(2,1)}) custom-call(bf16[4,128,128]{2,1,0:T(8,128)(2,1)S(1)} %get-tuple-element.26.query_ref, f32[4,128,1]{2,1,0:T(8,128)S(1)} %get-tuple-element.33.max_ref, f32[4,128,1]{2,1,0:T(8,128)S(1)} %get-tuple-element.34.denominator_ref, ...), custom_call_target="tpu_custom_call" | custom-call | flops 201326592 | bytes 3145728 | tf_op jit(solution)/shard_map/pallas_call | solution.py:143
  41.4 0.1 collective-permute-start.11
  41.5 0.0 collective-permute-done.17.across_ref
  41.5 0.4 collective-permute-start.18
  41.9 0.0 collective-permute-done.12.received_ref
  41.9 0.6 %collective-permute-start.13 = (bf16[32,1536]{1,0:T(8,128)(2,1)S(1)}, bf16[32,1536]{1,0:T(8,128)(2,1)S(1)}, u32[]{:S(2)}, u32[]{:S(2)}) collective-permute-start(bf16[32,1536]{1,0:T(8,128)(2,1)S(1)} %shard_map.105), channel_id=1, source_target_pairs={{0,2},{2,0},{1,3},{3,1},{4,6},{6,4},{5,7},{7,5},{8,10},{10,8},{9,1... | collective-permute-start | bytes 294920 | tf_op jit(solution)/shard_map/ppermute | solution.py:133
  42.5 0.0 collective-permute-done.14.received_ref
  42.6 1.6 %collective-permute-start.15 = (bf16[32,1536]{1,0:T(8,128)(2,1)S(1)}, bf16[32,1536]{1,0:T(8,128)(2,1)S(1)}, u32[]{:S(2)}, u32[]{:S(2)}) collective-permute-start(bf16[32,1536]{1,0:T(8,128)(2,1)S(1)} %shard_map.108), channel_id=1, source_target_pairs={{0,2},{2,0},{1,3},{3,1},{4,6},{6,4},{5,7},{7,5},{8,10},{10,8},{9,1... | collective-permute-start | bytes 294920 | tf_op jit(solution)/shard_map/ppermute | solution.py:133
  44.1 0.0 collective-permute-start.16
  44.1 1.3 %collective-permute-done.16.beside_ref = bf16[4,32,256]{2,1,0:T(8,128)(2,1)S(1)} collective-permute-done((bf16[4,32,256]{2,1,0:T(8,128)(2,1)S(1)}, bf16[4,32,256]{2,1,0:T(8,128)(2,1)S(1)}, u32[]{:S(2)}, u32[]{:S(2)}) %collective-permute-start.16) | collective-permute-done | bytes 65568 | tf_op jit(solution)/shard_map/ppermute | solution.py:133
  45.4 0.0 collective-permute-done.18.diagonal_ref
  45.4 1.0 %shard_map.110 = bf16[32,16,256]{2,1,0:T(8,128)(2,1)} custom-call(bf16[4,32,256]{2,1,0:T(8,128)(2,1)S(1)} %get-tuple-element.27.own_ref, bf16[4,32,256]{2,1,0:T(8,128)(2,1)S(1)} %collective-permute-done.16.beside_ref, bf16[2,4,32,256]{3,2,1,0:T(8,128)(2,1)S(1)} %collective-permute-done.17.across_ref, ...), custom_call_target="tpu_custom_call" | custom-call | bytes 524288 | tf_op jit(solution)/shard_map/pallas_call | solution.py:143
  46.4 1.3 %collective-permute-done.13.low_ref = bf16[32,1536]{1,0:T(8,128)(2,1)S(1)} collective-permute-done((bf16[32,1536]{1,0:T(8,128)(2,1)S(1)}, bf16[32,1536]{1,0:T(8,128)(2,1)S(1)}, u32[]{:S(2)}, u32[]{:S(2)}) %collective-permute-start.13) | collective-permute-done | bytes 98336 | tf_op jit(solution)/shard_map/ppermute | solution.py:133
  47.7 0.0 collective-permute-done.11.beside_ref
  47.7 0.7 %shard_map.106 = (bf16[32,3072]{1,0:T(8,128)(2,1)}, f32[32,1536]{1,0:T(8,128)S(1)}) custom-call(f32[32,3072]{1,0:T(8,128)S(1)} %get-tuple-element.37.kept_ref, bf16[32,3072]{1,0:T(8,128)(2,1)S(1)} %collective-permute-done.11.beside_ref, bf16[32,1536]{1,0:T(8,128)(2,1)S(1)} %collective-permute-done.13.low_ref, f32[3,3072]{1,0:T(4,128)S(1)} %get-tuple-element.25.modulation_ref), custom_call_target="tpu_custom_call" | custom-call | flops 294912 | bytes 786432 | tf_op jit(solution)/shard_map/pallas_call | solution.py:614
  48.4 0.5 %collective-permute-done.15.high_ref = bf16[32,1536]{1,0:T(8,128)(2,1)S(1)} collective-permute-done((bf16[32,1536]{1,0:T(8,128)(2,1)S(1)}, bf16[32,1536]{1,0:T(8,128)(2,1)S(1)}, u32[]{:S(2)}, u32[]{:S(2)}) %collective-permute-start.15) | collective-permute-done | bytes 98336 | tf_op jit(solution)/shard_map/ppermute | solution.py:133
  48.9 0.7 %shard_map.109 = bf16[32,3072]{1,0:T(8,128)(2,1)} custom-call(bf16[32,3072]{1,0:T(8,128)(2,1)} %get-tuple-element.41.begun_ref, f32[32,1536]{1,0:T(8,128)S(1)} %get-tuple-element.42.rest_ref, bf16[32,1536]{1,0:T(8,128)(2,1)S(1)} %collective-permute-done.15.high_ref, f32[3,3072]{1,0:T(4,128)S(1)} %get-tuple-element.25.modulation_ref), custom_call_target="tpu_custom_call", output_to_operand_aliasing={{}: (0, {})} | custom-call | flops 98304 | bytes 393216 | tf_op jit(solution)/shard_map/pallas_call | solution.py:628
  (5 shorter events, 0.1 us)
Async XLA Ops:
  1.8 7.4 %collective-permute-start.5 = (bf16[2,4,32,256]{3,2,1,0:T(8,128)(2,1)S(1)}, bf16[2,4,32,256]{3,2,1,0:T(8,128)(2,1)S(1)}, u32[]{:S(2)}, u32[]{:S(2)}) collective-permute-start(bf16[2,4,32,256]{3,2,1,0:T(8,128)(2,1)S(1)} %get-tuple-element.32), channel_id=1, source_target_pairs={{0,2},{2,0},{1,3},{3,1},{4,6},{6,4},{5,7},{7,5},{8,10},{10,8},{9,1... | collective-permute-start | bytes 393224 | tf_op jit(solution)/shard_map/ppermute | solution.py:133
  5.2 7.5 %collective-permute-start.1 = (bf16[32,3072]{1,0:T(8,128)(2,1)S(1)}, bf16[32,3072]{1,0:T(8,128)(2,1)S(1)}, u32[]{:S(2)}, u32[]{:S(2)}) collective-permute-start(bf16[32,3072]{1,0:T(8,128)(2,1)S(1)} %shard_map.96.own_ref), channel_id=1, source_target_pairs={{0,2},{2,0},{1,3},{3,1},{4,6},{6,4},{5,7},{7,5},{8,10},{10,8},{9,1... | collective-permute-start | bytes 589832 | tf_op jit(solution)/shard_map/ppermute | solution.py:133
  5.2 4.0 %collective-permute-start.3 = (bf16[4,32,256]{2,1,0:T(8,128)(2,1)S(1)}, bf16[4,32,256]{2,1,0:T(8,128)(2,1)S(1)}, u32[]{:S(2)}, u32[]{:S(2)}) collective-permute-start(bf16[4,32,256]{2,1,0:T(8,128)(2,1)S(1)} %get-tuple-element.31), channel_id=1, source_target_pairs={{0,1},{1,0},{2,3},{3,2},{4,5},{5,4},{6,7},{7,6},{8,9},{9,8},{10,11... | collective-permute-start | bytes 196616 | tf_op jit(solution)/shard_map/ppermute | solution.py:133
  9.2 3.7 %collective-permute-start.6 = (bf16[2,4,32,256]{3,2,1,0:T(8,128)(2,1)S(1)}, bf16[2,4,32,256]{3,2,1,0:T(8,128)(2,1)S(1)}, u32[]{:S(2)}, u32[]{:S(2)}) collective-permute-start(bf16[2,4,32,256]{3,2,1,0:T(8,128)(2,1)S(1)} %collective-permute-done.5.across_ref), channel_id=1, source_target_pairs={{0,1},{1,0},{2,3},{3,2},{4,5},{5,4},{6,7},{7,6},{8,9},{9,8},{10,11... | collective-permute-start | bytes 393224 | tf_op jit(solution)/shard_map/ppermute | solution.py:133
  9.2 10.2 %collective-permute-start.7 = (bf16[2,4,32,256]{3,2,1,0:T(8,128)(2,1)S(1)}, bf16[2,4,32,256]{3,2,1,0:T(8,128)(2,1)S(1)}, u32[]{:S(2)}, u32[]{:S(2)}) collective-permute-start(bf16[2,4,32,256]{3,2,1,0:T(8,128)(2,1)S(1)} %shard_map.99), channel_id=1, source_target_pairs={{0,8},{4,12},{8,0},{12,4},{1,9},{5,13},{9,1},{13,5},{2,10},{6,14},... | collective-permute-start | bytes 393224 | tf_op jit(solution)/shard_map/ppermute | solution.py:488
  12.4 21.2 %collective-permute-start = (bf16[32,3072]{1,0:T(8,128)(2,1)S(1)}, bf16[32,3072]{1,0:T(8,128)(2,1)S(1)}, u32[]{:S(2)}, u32[]{:S(2)}) collective-permute-start(bf16[32,3072]{1,0:T(8,128)(2,1)S(1)} %shard_map.96.own_ref), channel_id=1, source_target_pairs={{0,1},{1,0},{2,3},{3,2},{4,5},{5,4},{6,7},{7,6},{8,9},{9,8},{10,11... | collective-permute-start | bytes 589832 | tf_op jit(solution)/shard_map/ppermute | solution.py:133
  12.7 20.9 %collective-permute-start.2 = (bf16[32,3072]{1,0:T(8,128)(2,1)S(1)}, bf16[32,3072]{1,0:T(8,128)(2,1)S(1)}, u32[]{:S(2)}, u32[]{:S(2)}) collective-permute-start(bf16[32,3072]{1,0:T(8,128)(2,1)S(1)} %collective-permute-done.1.across_ref), channel_id=1, source_target_pairs={{0,1},{1,0},{2,3},{3,2},{4,5},{5,4},{6,7},{7,6},{8,9},{9,8},{10,11... | collective-permute-start | bytes 589832 | tf_op jit(solution)/shard_map/ppermute | solution.py:133
  19.4 14.2 %copy-start.2 = (f32[128]{0:T(128)S(1)}, f32[128]{0:T(128)}, u32[]{:S(2)}) copy-start(f32[128]{0:T(128)} %param.11) | copy-start | bytes 1540
  19.4 14.2 %copy-start.3 = (f32[128]{0:T(128)S(1)}, f32[128]{0:T(128)}, u32[]{:S(2)}) copy-start(f32[128]{0:T(128)} %param.12) | copy-start | bytes 1540
  19.4 17.6 %collective-permute-start.8 = (bf16[4,4,32,256]{3,2,1,0:T(8,128)(2,1)S(1)}, bf16[4,4,32,256]{3,2,1,0:T(8,128)(2,1)S(1)}, u32[]{:S(2)}, u32[]{:S(2)}) collective-permute-start(bf16[4,4,32,256]{3,2,1,0:T(8,128)(2,1)S(1)} %shard_map.101), channel_id=1, source_target_pairs={{0,4},{4,0},{8,12},{12,8},{1,5},{5,1},{9,13},{13,9},{2,6},{6,2},{1... | collective-permute-start | bytes 786440 | tf_op jit(solution)/shard_map/ppermute | solution.py:488
  20.3 9.5 %collective-permute-start.9 = (bf16[2,4,32,256]{3,2,1,0:T(8,128)(2,1)S(1)}, bf16[2,4,32,256]{3,2,1,0:T(8,128)(2,1)S(1)}, u32[]{:S(2)}, u32[]{:S(2)}) collective-permute-start(bf16[2,4,32,256]{3,2,1,0:T(8,128)(2,1)S(1)} %shard_map.100.other_ref), channel_id=1, source_target_pairs={{0,8},{4,12},{8,0},{12,4},{1,9},{5,13},{9,1},{13,5},{2,10},{6,14},... | collective-permute-start | bytes 393224 | tf_op jit(solution)/shard_map/ppermute | solution.py:488
  23.6 13.4 %collective-permute-start.4 = (bf16[2,4,32,256]{3,2,1,0:T(8,128)(2,1)S(1)}, bf16[2,4,32,256]{3,2,1,0:T(8,128)(2,1)S(1)}, u32[]{:S(2)}, u32[]{:S(2)}) collective-permute-start(bf16[2,4,32,256]{3,2,1,0:T(8,128)(2,1)S(1)} %shard_map.99), channel_id=1, source_target_pairs={{0,4},{4,0},{8,12},{12,8},{1,5},{5,1},{9,13},{13,9},{2,6},{6,2},{1... | collective-permute-start | bytes 393224 | tf_op jit(solution)/shard_map/ppermute | solution.py:488
  28.7 8.4 %copy-start.1 = (s32[4]{0:T(128)S(1)}, s32[4]{0:T(128)}, u32[]{:S(2)}) copy-start(s32[4]{0:T(128)} %length_ref.1) | copy-start | bytes 52
  28.7 9.6 %copy-start = (bf16[4,128,3072]{2,1,0:T(8,128)(2,1)S(1)}, bf16[4,128,3072]{2,1,0:T(8,128)(2,1)}, u32[]{:S(2)}) copy-start(bf16[4,128,3072]{2,1,0:T(8,128)(2,1)} %param.13) | copy-start | bytes 9437188
  29.8 8.5 %collective-permute-start.10 = (bf16[2,4,32,256]{3,2,1,0:T(8,128)(2,1)S(1)}, bf16[2,4,32,256]{3,2,1,0:T(8,128)(2,1)S(1)}, u32[]{:S(2)}, u32[]{:S(2)}) collective-permute-start(bf16[2,4,32,256]{3,2,1,0:T(8,128)(2,1)S(1)} %collective-permute-done.9.two_other_ref), channel_id=1, source_target_pairs={{0,4},{4,0},{8,12},{12,8},{1,5},{5,1},{9,13},{13,9},{2,6},{6,2},{1... | collective-permute-start | bytes 393224 | tf_op jit(solution)/shard_map/ppermute | solution.py:488
  35.5 6.0 %collective-permute-start.17 = (bf16[2,4,32,256]{3,2,1,0:T(8,128)(2,1)S(1)}, bf16[2,4,32,256]{3,2,1,0:T(8,128)(2,1)S(1)}, u32[]{:S(2)}, u32[]{:S(2)}) collective-permute-start(bf16[2,4,32,256]{3,2,1,0:T(8,128)(2,1)S(1)} %get-tuple-element.29.across_ref), channel_id=1, source_target_pairs={{0,2},{2,0},{1,3},{3,1},{4,6},{6,4},{5,7},{7,5},{8,10},{10,8},{9,1... | collective-permute-start | bytes 393224 | tf_op jit(solution)/shard_map/ppermute | solution.py:133
  39.6 3.0 %collective-permute-start.14 = (bf16[32,1536]{1,0:T(8,128)(2,1)S(1)}, bf16[32,1536]{1,0:T(8,128)(2,1)S(1)}, u32[]{:S(2)}, u32[]{:S(2)}) collective-permute-start(bf16[32,1536]{1,0:T(8,128)(2,1)S(1)} %get-tuple-element.45), channel_id=1, source_target_pairs={{0,1},{1,0},{2,3},{3,2},{4,5},{5,4},{6,7},{7,6},{8,9},{9,8},{10,11... | collective-permute-start | bytes 294920 | tf_op jit(solution)/shard_map/ppermute | solution.py:133
  39.6 2.3 %collective-permute-start.12 = (bf16[32,1536]{1,0:T(8,128)(2,1)S(1)}, bf16[32,1536]{1,0:T(8,128)(2,1)S(1)}, u32[]{:S(2)}, u32[]{:S(2)}) collective-permute-start(bf16[32,1536]{1,0:T(8,128)(2,1)S(1)} %get-tuple-element.40), channel_id=1, source_target_pairs={{0,1},{1,0},{2,3},{3,2},{4,5},{5,4},{6,7},{7,6},{8,9},{9,8},{10,11... | collective-permute-start | bytes 294920 | tf_op jit(solution)/shard_map/ppermute | solution.py:133
  41.4 6.3 %collective-permute-start.11 = (bf16[32,3072]{1,0:T(8,128)(2,1)S(1)}, bf16[32,3072]{1,0:T(8,128)(2,1)S(1)}, u32[]{:S(2)}, u32[]{:S(2)}) collective-permute-start(bf16[32,3072]{1,0:T(8,128)(2,1)S(1)} %get-tuple-element.38), channel_id=1, source_target_pairs={{0,1},{1,0},{2,3},{3,2},{4,5},{5,4},{6,7},{7,6},{8,9},{9,8},{10,11... | collective-permute-start | bytes 589832 | tf_op jit(solution)/shard_map/ppermute | solution.py:133
  41.5 3.9 %collective-permute-start.18 = (bf16[2,4,32,256]{3,2,1,0:T(8,128)(2,1)S(1)}, bf16[2,4,32,256]{3,2,1,0:T(8,128)(2,1)S(1)}, u32[]{:S(2)}, u32[]{:S(2)}) collective-permute-start(bf16[2,4,32,256]{3,2,1,0:T(8,128)(2,1)S(1)} %collective-permute-done.17.across_ref), channel_id=1, source_target_pairs={{0,1},{1,0},{2,3},{3,2},{4,5},{5,4},{6,7},{7,6},{8,9},{9,8},{10,11... | collective-permute-start | bytes 393224 | tf_op jit(solution)/shard_map/ppermute | solution.py:133
  41.9 5.7 %collective-permute-start.13 = (bf16[32,1536]{1,0:T(8,128)(2,1)S(1)}, bf16[32,1536]{1,0:T(8,128)(2,1)S(1)}, u32[]{:S(2)}, u32[]{:S(2)}) collective-permute-start(bf16[32,1536]{1,0:T(8,128)(2,1)S(1)} %shard_map.105), channel_id=1, source_target_pairs={{0,2},{2,0},{1,3},{3,1},{4,6},{6,4},{5,7},{7,5},{8,10},{10,8},{9,1... | collective-permute-start | bytes 294920 | tf_op jit(solution)/shard_map/ppermute | solution.py:133
  42.6 6.3 %collective-permute-start.15 = (bf16[32,1536]{1,0:T(8,128)(2,1)S(1)}, bf16[32,1536]{1,0:T(8,128)(2,1)S(1)}, u32[]{:S(2)}, u32[]{:S(2)}) collective-permute-start(bf16[32,1536]{1,0:T(8,128)(2,1)S(1)} %shard_map.108), channel_id=1, source_target_pairs={{0,2},{2,0},{1,3},{3,1},{4,6},{6,4},{5,7},{7,5},{8,10},{10,8},{9,1... | collective-permute-start | bytes 294920 | tf_op jit(solution)/shard_map/ppermute | solution.py:133
  44.1 1.3 %collective-permute-start.16 = (bf16[4,32,256]{2,1,0:T(8,128)(2,1)S(1)}, bf16[4,32,256]{2,1,0:T(8,128)(2,1)S(1)}, u32[]{:S(2)}, u32[]{:S(2)}) collective-permute-start(bf16[4,32,256]{2,1,0:T(8,128)(2,1)S(1)} %get-tuple-element.28.beside_ref), channel_id=1, source_target_pairs={{0,1},{1,0},{2,3},{3,2},{4,5},{5,4},{6,7},{7,6},{8,9},{9,8},{10,11... | collective-permute-start | bytes 196616 | tf_op jit(solution)/shard_map/ppermute | solution.py:133
